TPU v7x, 512 devices: a whole 4x8x8 slice. The times are simulated.
512 devices in a mesh: section: 16 (over z, x_hi), expert: 32 (over y, x_lo, core).
Axes of the slice: x: 4 (x_hi: 2, x_lo: 2; x = x_hi * 2 + x_lo), y: 8, z: 8, core: 2. Of those that a mesh axis runs over, the one named last changes fastest.
Arguments:
- fwd_sent: bfloat16 [16, 2048, 4096], P('section', 'expert'), may hold values from -6 to 6
- bwd_sent: bfloat16 [16, 2048, 4096], P('section', 'expert'), may hold values from -6 to 6
- bwd_saved: bfloat16 [16, 2048, 4096], P('section', 'expert'), may hold values from -6 to 6
- fwd_routes: int32 [16, 2048, 8], P('section', 'expert'), may hold values from 0 to 127, all different within a row; in each aligned block of 64 rows (0 to 63, 64 to 127, ..., all dimensions but the last counted through in order) at most 8 rows name the same one
- bwd_routes: int32 [16, 2048, 8], P('section', 'expert'), may hold values from 0 to 127, all different within a row; in each aligned block of 64 rows (0 to 63, 64 to 127, ..., all dimensions but the last counted through in order) at most 8 rows name the same one
- fwd_logits: float32 [16, 2048, 128], P('section', 'expert'), may hold values from -3 to 330
- bwd_logits: float32 [16, 2048, 128], P('section', 'expert'), may hold values from -3 to 330
- norm_gain: bfloat16 [16, 4096], P('section'), may hold values from 0.5 to 1.5
- w_gate: bfloat16 [16, 4096, 3072], P('section', None, 'expert'), may hold values from -0.09375 to 0.09375
- w_up: bfloat16 [16, 4096, 3072], P('section', None, 'expert'), may hold values from -0.09375 to 0.09375
- w_down: bfloat16 [16, 3072, 4096], P('section', 'expert'), may hold values from -0.4375 to 0.4375
Outputs:
- fwd_out: bfloat16 [16, 2048, 4096], P('section', 'expert')
- bwd_out: bfloat16 [16, 2048, 4096], P('section', 'expert')
- balance: float32 [16, 128], P('section')
Inputs may be any that keep to these rules, and one draw needn't show every extreme that they name: `fwd_routes`: each token names 8 different experts; among the 64 tokens of one index of expert no expert is named more than 8 times, a bound that some block reaches. `bwd_routes`: as for fwd_routes.
All inputs are finite; a program needn't handle non-finite values.
Results may differ from a plain program's by a relative error of at most 0.0045.
Values may be sent and summed in bfloat16 or wider, within the bound.
No kernel may reach another device: no remote copies, remote signals or barrier semaphores. Data moves between devices by JAX's collectives and lax.ppermute only.
A program may use at most 64 MiB of HBM per device.

v0:
```python
import jax
import jax.numpy as jnp
from jax import lax
from jax.sharding import PartitionSpec as P

EXPERTS = 128
TOPK = 8
EXP_WIN = 2
CAP = 8


epsilon = 1e-06
exact = lax.Precision.HIGHEST


def from_behind(block, axis, distance):
    devices = range(lax.axis_size(axis))
    route = [((i - distance) % len(devices), i) for i in devices]
    return lax.ppermute(block, axis, route)


def norm_rows(values, gain_row):
    widened = values.astype(jnp.float32)
    inverse = lax.rsqrt(jnp.mean(widened * widened, axis=-1, keepdims=True) + epsilon)
    normed = (widened * inverse * gain_row.astype(jnp.float32)).astype(jnp.bfloat16)
    return (normed, widened, inverse)


def slot_tables(routes, logits):
    tokens_here = routes.shape[0]
    expert_ids = jnp.arange(logits.shape[1], dtype=jnp.int32)
    chosen = jnp.sum(
        jnp.where(routes[:, :, None] == expert_ids[None, None, :], logits[:, None, :], 0.0), axis=2
    )
    gates = jax.nn.softmax(chosen, axis=1)
    match = (routes[:, :, None] == jnp.arange(EXP_WIN, dtype=jnp.int32)[None, None, :]).astype(
        jnp.int32
    )
    flat = match.reshape(tokens_here * TOPK, EXP_WIN)
    earlier = (jnp.cumsum(flat, axis=0) - flat).reshape(tokens_here, TOPK, EXP_WIN)
    placed = match[..., None] * (earlier[..., None] == jnp.arange(CAP, dtype=jnp.int32)).astype(
        jnp.int32
    )
    select = jnp.sum(placed, axis=1).astype(jnp.float32)
    gate_slot = jnp.sum(placed.astype(jnp.float32) * gates[:, :, None, None], axis=(0, 1))
    return (select, gate_slot)


def usage_terms(routes, logits):
    expert_ids = jnp.arange(logits.shape[1], dtype=jnp.int32)
    counts = jnp.sum(
        (routes[:, :, None] == expert_ids[None, None, :]).astype(jnp.float32), axis=(0, 1)
    )
    prob_sums = jnp.sum(jax.nn.softmax(logits, axis=1), axis=0)
    return (counts, prob_sums)


def spread_rows(slot_rows, devices):
    held, slots, width = slot_rows.shape
    return jnp.broadcast_to(slot_rows[:, None], (held, devices // held, slots, width)).reshape(
        devices, slots, width
    )


def combine_parts(returned):
    devices, slots, width = returned.shape
    return jnp.sum(
        returned.astype(jnp.float32).reshape(EXP_WIN, devices // EXP_WIN, slots, width), axis=1
    )


def expert_forward(arrived, gate_slab, up_slab, down_slab):
    layout = arrived.shape
    flat = arrived.reshape(-1, layout[-1])
    gate_pre = jnp.dot(flat, gate_slab, preferred_element_type=jnp.float32)
    up_pre = jnp.dot(flat, up_slab, preferred_element_type=jnp.float32)
    hidden = (jax.nn.silu(gate_pre) * up_pre).astype(jnp.bfloat16)
    result = jnp.dot(hidden, down_slab, preferred_element_type=jnp.float32).astype(jnp.bfloat16)
    return result.reshape(layout)


def expert_backward(arrived, arrived_grads, gate_slab, up_slab, down_slab):
    layout = arrived.shape
    flat = arrived.reshape(-1, layout[-1])
    grad_flat = arrived_grads.reshape(-1, layout[-1])
    gate_pre = jnp.dot(flat, gate_slab, preferred_element_type=jnp.float32)
    up_pre = jnp.dot(flat, up_slab, preferred_element_type=jnp.float32)
    sigma = jax.nn.sigmoid(gate_pre)
    contract = (((1,), (1,)), ((), ()))
    d_hidden = lax.dot_general(grad_flat, down_slab, contract, preferred_element_type=jnp.float32)
    d_gate = (d_hidden * up_pre * sigma * (1.0 + gate_pre * (1.0 - sigma))).astype(jnp.bfloat16)
    d_up = (d_hidden * gate_pre * sigma).astype(jnp.bfloat16)
    result = lax.dot_general(d_gate, gate_slab, contract, preferred_element_type=jnp.float32)
    result = result + lax.dot_general(d_up, up_slab, contract, preferred_element_type=jnp.float32)
    return result.astype(jnp.bfloat16).reshape(layout)


def body(
    fwd_sent,
    bwd_sent,
    bwd_saved,
    fwd_routes,
    bwd_routes,
    fwd_logits,
    bwd_logits,
    norm_gain,
    w_gate,
    w_up,
    w_down,
):
    devices = lax.axis_size("expert")
    gain_row = norm_gain[0]
    gate_slab = w_gate[0]
    up_slab = w_up[0]
    down_slab = w_down[0]
    x_in = from_behind(fwd_sent[0], "section", 1)
    upstream = from_behind(bwd_sent[0], "section", -1)
    normed = norm_rows(x_in, gain_row)[0]
    fwd_select, fwd_gates = slot_tables(fwd_routes[0], fwd_logits[0])
    fwd_rows = jnp.einsum(
        "tec,td->ecd", fwd_select.astype(jnp.bfloat16), normed, preferred_element_type=jnp.float32
    ).astype(jnp.bfloat16)
    fwd_send = spread_rows(fwd_rows, devices)
    saved_normed, saved_wide, saved_inverse = norm_rows(bwd_saved[0], gain_row)
    bwd_select, bwd_gates = slot_tables(bwd_routes[0], bwd_logits[0])
    bwd_onehot = bwd_select.astype(jnp.bfloat16)
    saved_rows = jnp.einsum(
        "tec,td->ecd", bwd_onehot, saved_normed, preferred_element_type=jnp.float32
    ).astype(jnp.bfloat16)
    grad_rows = jnp.einsum("tec,td->ecd", bwd_onehot, upstream, preferred_element_type=jnp.float32)
    grad_rows = (grad_rows * bwd_gates[:, :, None]).astype(jnp.bfloat16)
    saved_send = spread_rows(saved_rows, devices)
    grad_send = spread_rows(grad_rows, devices)
    counts, prob_sums = usage_terms(fwd_routes[0], fwd_logits[0])
    counts, prob_sums = lax.psum((counts, prob_sums), "expert")
    fwd_parts = lax.all_to_all(
        expert_forward(
            lax.all_to_all(fwd_send, "expert", split_axis=0, concat_axis=0, tiled=True),
            gate_slab,
            up_slab,
            down_slab,
        ),
        "expert",
        split_axis=0,
        concat_axis=0,
        tiled=True,
    )
    bwd_parts = lax.all_to_all(
        expert_backward(
            lax.all_to_all(saved_send, "expert", split_axis=0, concat_axis=0, tiled=True),
            lax.all_to_all(grad_send, "expert", split_axis=0, concat_axis=0, tiled=True),
            gate_slab,
            up_slab,
            down_slab,
        ),
        "expert",
        split_axis=0,
        concat_axis=0,
        tiled=True,
    )
    fwd_expert = combine_parts(fwd_parts)
    mixed = jnp.einsum("tec,ecd->td", fwd_select * fwd_gates[None], fwd_expert, precision=exact)
    fwd_out = (x_in.astype(jnp.float32) + mixed).astype(jnp.bfloat16)
    back_expert = combine_parts(bwd_parts)
    d_normed = jnp.einsum("tec,ecd->td", bwd_select, back_expert, precision=exact)
    weighted = gain_row.astype(jnp.float32) * d_normed
    d_saved = saved_inverse * weighted - saved_wide * saved_inverse**3 * jnp.mean(
        saved_wide * weighted, axis=-1, keepdims=True
    )
    bwd_out = (upstream.astype(jnp.float32) + d_saved).astype(jnp.bfloat16)
    tokens_all = fwd_routes.shape[1] * devices
    balance = EXPERTS * (counts / (tokens_all * TOPK)) * (prob_sums / tokens_all)
    return (fwd_out[None], bwd_out[None], balance[None])


def solution(mesh):
    return jax.shard_map(
        body,
        mesh=mesh,
        in_specs=(
            P("section", "expert", None),
            P("section", "expert", None),
            P("section", "expert", None),
            P("section", "expert", None),
            P("section", "expert", None),
            P("section", "expert", None),
            P("section", "expert", None),
            P("section", None),
            P("section", None, "expert"),
            P("section", None, "expert"),
            P("section", "expert", None),
        ),
        out_specs=(P("section", "expert", None), P("section", "expert", None), P("section", None)),
        check_vma=False,
    )
```

profile of v0, /device:TPU:1, one launch (start us, length us, event | category | flops | bytes accessed | tf_op | source)
XLA Modules:
  0.0 351.0 jit_solution(1473543649482552613)
XLA Ops:
  0.6 0.8 copy.50
  1.7 0.6 reduce-window.16
  2.3 0.2 slice_reduce_fusion
  2.5 0.2 reduce-window.19
  3.0 0.7 compare_convert_fusion
  3.7 0.7 mul.195
  4.4 1.2 fusion.42
  5.7 0.6 multiply_multiply_fusion
  6.3 1.3 convolution_convert_fusion.1
  7.6 1.6 broadcast_in_dim.42
  9.2 10.7 %all-to-all-start.3 = ((bf16[32,8,4096]{2,1,0:T(8,128)(2,1)}), bf16[32,8,4096]{2,1,0:T(8,128)(2,1)S(1)}, u32[]{:S(2)}, u32[]{:S(2)}) async-start(bf16[32,8,4096]{2,1,0:T(8,128)(2,1)} %bitcast.137), calls=%async_computation.3 | async-start | bytes 4194304 | tf_op jit(solution)/shard_map/all_to_all | solution.py:150
  19.9 12.0 %collective-permute-start.1 = (bf16[64,4096]{1,0:T(8,128)(2,1)}, bf16[64,4096]{1,0:T(8,128)(2,1)S(1)}, u32[]{:S(2)}, u32[]{:S(2)}) collective-permute-start(bf16[64,4096]{1,0:T(8,128)(2,1)} %bitcast.150), channel_id=1, source_target_pairs={{32,0},{64,32},{96,64},{128,96},{160,128},{192,160},{224,192},{256... | collective-permute-start | bytes 1572872 | tf_op jit(solution)/shard_map/ppermute | solution.py:19
  32.0 0.2 select_reduce_fusion
  32.6 18.2 %collective-permute-done.1 = bf16[64,4096]{1,0:T(8,128)(2,1)S(1)} collective-permute-done((bf16[64,4096]{1,0:T(8,128)(2,1)}, bf16[64,4096]{1,0:T(8,128)(2,1)S(1)}, u32[]{:S(2)}, u32[]{:S(2)}) %collective-permute-start.1) | collective-permute-done | bytes 524320 | tf_op jit(solution)/shard_map/ppermute | solution.py:19
  50.7 0.2 fusion.7
  50.9 20.8 %all-to-all-done.3 = bf16[32,8,4096]{2,1,0:T(8,128)(2,1)S(1)} async-done(((bf16[32,8,4096]{2,1,0:T(8,128)(2,1)}), bf16[32,8,4096]{2,1,0:T(8,128)(2,1)S(1)}, u32[]{:S(2)}, u32[]{:S(2)}) %all-to-all-start.3) | async-done | bytes 2097184 | tf_op jit(solution)/shard_map/all_to_all | solution.py:150
  71.7 1.5 broadcast_in_dim.41
  73.2 4.9 %all-to-all-start.2 = ((bf16[32,8,4096]{2,1,0:T(8,128)(2,1)}), bf16[32,8,4096]{2,1,0:T(8,128)(2,1)}, u32[]{:S(2)}, u32[]{:S(2)}) async-start(bf16[32,8,4096]{2,1,0:T(8,128)(2,1)} %bitcast.136), calls=%async_computation.2 | async-start | bytes 4194304 | tf_op jit(solution)/shard_map/all_to_all | solution.py:151
  78.2 1.9 collective-permute-start
  80.4 0.6 reduce-window.14
  81.0 0.2 slice_reduce_fusion.1
  81.7 24.4 %collective-permute-done = bf16[64,4096]{1,0:T(8,128)(2,1)S(1)} collective-permute-done((bf16[64,4096]{1,0:T(8,128)(2,1)}, bf16[64,4096]{1,0:T(8,128)(2,1)S(1)}, u32[]{:S(2)}, u32[]{:S(2)}) %collective-permute-start) | collective-permute-done | bytes 524320 | tf_op jit(solution)/shard_map/ppermute | solution.py:19
  106.1 0.2 fusion.39
  106.3 1.0 convolution_convert_fusion.2
  107.3 20.9 %all-to-all-done.2 = bf16[32,8,4096]{2,1,0:T(8,128)(2,1)} async-done(((bf16[32,8,4096]{2,1,0:T(8,128)(2,1)}), bf16[32,8,4096]{2,1,0:T(8,128)(2,1)}, u32[]{:S(2)}, u32[]{:S(2)}) %all-to-all-start.2) | async-done | bytes 2097184 | tf_op jit(solution)/shard_map/all_to_all | solution.py:151
  128.3 1.6 broadcast_in_dim.37
  129.9 6.3 %all-to-all-start = ((bf16[32,8,4096]{2,1,0:T(8,128)(2,1)}), bf16[32,8,4096]{2,1,0:T(8,128)(2,1)}, u32[]{:S(2)}, u32[]{:S(2)}) async-start(bf16[32,8,4096]{2,1,0:T(8,128)(2,1)} %bitcast.138), calls=%async_computation | async-start | bytes 4194304 | tf_op jit(solution)/shard_map/all_to_all | solution.py:138
  136.2 2.0 fusion.8
  138.2 2.4 fusion.12
  140.6 5.6 %fusion.37 = f32[256,4096]{1,0:T(8,128)} fusion(f32[256,96]{0,1:T(8,128)S(1)} %fusion.12, bf16[32,8,4096]{2,1,0:T(8,128)(2,1)S(1)} %all-to-all-done.3, bf16[1,4096,96]{1,2,0:T(8,128)(2,1)S(1)} %copy-done, bf16[1,4096,96]{1,2,0:T(8,128)(2,1)} %param.19, f32[256,96]{0,1:T(8,128)S(1)} %fusion.8), kind=kOutput, calls=%fused_computation.39 | convolution fusion | flops 402898944 | bytes 8060928 | tf_op jit(solution)/shard_map/dot_general | solution.py:93
  146.2 4.3 %fusion.2 = bf16[32,8,4096]{2,1,0:T(8,128)(2,1)} fusion(f32[256,4096]{1,0:T(8,128)} %fusion.37, bf16[1,4096,96]{1,2,0:T(8,128)(2,1)S(1)} %copy-done, f32[256,96]{0,1:T(8,128)S(1)} %fusion.12, f32[256,96]{0,1:T(8,128)S(1)} %fusion.8), kind=kOutput, calls=%fused_computation.4 | convolution fusion | flops 203571200 | bytes 7274496 | tf_op jit(solution)/shard_map/dot_general | solution.py:94
  150.5 35.8 %all-to-all-done = bf16[32,8,4096]{2,1,0:T(8,128)(2,1)} async-done(((bf16[32,8,4096]{2,1,0:T(8,128)(2,1)}), bf16[32,8,4096]{2,1,0:T(8,128)(2,1)}, u32[]{:S(2)}, u32[]{:S(2)}) %all-to-all-start) | async-done | bytes 2097184 | tf_op jit(solution)/shard_map/all_to_all | solution.py:138
  186.3 5.7 %all-to-all-start.4 = ((bf16[32,8,4096]{2,1,0:T(8,128)(2,1)}), bf16[32,8,4096]{2,1,0:T(8,128)(2,1)S(1)}, u32[]{:S(2)}, u32[]{:S(2)}) async-start(bf16[32,8,4096]{2,1,0:T(8,128)(2,1)} %fusion.2), calls=%async_computation.4 | async-start | bytes 4194304 | tf_op jit(solution)/shard_map/all_to_all | solution.py:148
  192.0 2.5 fusion.16
  194.5 5.6 %fusion.1 = bf16[32,8,4096]{2,1,0:T(8,128)(2,1)} fusion(bf16[32,8,4096]{2,1,0:T(8,128)(2,1)} %all-to-all-done, bf16[1,96,4096]{2,1,0:T(8,128)(2,1)} %param.21, bf16[1,4096,96]{1,2,0:T(8,128)(2,1)S(1)} %copy-done, f32[256,96]{0,1:T(8,128)S(1)} %fusion.16), kind=kOutput, calls=%fused_computation.3 | convolution fusion | flops 403849216 | bytes 5865472 | tf_op jit(solution)/shard_map/dot_general | solution.py:78
  200.2 41.9 %all-to-all-done.4 = bf16[32,8,4096]{2,1,0:T(8,128)(2,1)S(1)} async-done(((bf16[32,8,4096]{2,1,0:T(8,128)(2,1)}), bf16[32,8,4096]{2,1,0:T(8,128)(2,1)S(1)}, u32[]{:S(2)}, u32[]{:S(2)}) %all-to-all-start.4) | async-done | bytes 2097184 | tf_op jit(solution)/shard_map/all_to_all | solution.py:148
  242.1 1.3 copy-done.1
  243.4 5.6 %all-to-all-start.1 = ((bf16[32,8,4096]{2,1,0:T(8,128)(2,1)}), bf16[32,8,4096]{2,1,0:T(8,128)(2,1)S(1)}, u32[]{:S(2)}, u32[]{:S(2)}) async-start(bf16[32,8,4096]{2,1,0:T(8,128)(2,1)} %fusion.1), calls=%async_computation.1 | async-start | bytes 4194304 | tf_op jit(solution)/shard_map/all_to_all | solution.py:136
  249.1 0.7 convert_reduce_fusion.2
  250.1 0.2 fusion.88
  250.4 91.7 %all-reduce = (f32[128]{0:T(128)S(1)}, f32[128]{0:T(128)S(1)}) all-reduce(f32[128]{0:T(128)S(1)} %divide_reduce_fusion, f32[128]{0:T(128)} %get-tuple-element.3), channel_id=1, replica_groups=mesh['section'=16,'expert'=32] {'expert'}, use_global_device_ids=true, to_apply=%region_24.25 | all-reduce | flops 256 | bytes 2048 | tf_op jit(solution)/shard_map/psum | solution.py:135
  342.2 0.5 multiply_bitcast_fusion
  342.7 1.9 convert_reduce_fusion
  344.7 2.2 fusion.49
  346.9 0.3 convert_reduce_fusion.1
  347.2 0.7 copy-done.6
  347.9 1.9 fusion.6
  349.9 1.1 fusion.62
  (80 shorter events, 2.3 us)
Async XLA Ops:
  0.6 140.0 %copy-start = (bf16[1,4096,96]{1,2,0:T(8,128)(2,1)S(1)}, bf16[1,4096,96]{1,2,0:T(8,128)(2,1)}, u32[]{:S(2)}) copy-start(bf16[1,4096,96]{1,2,0:T(8,128)(2,1)} %param.20) | copy-start | bytes 2359300
  4.4 4.8 %copy-start.12 = (f32[1,4096]{1,0:T(1,128)}, f32[1,4096]{1,0:T(1,128)S(1)}, u32[]{:S(2)}) copy-start(f32[1,4096]{1,0:T(1,128)S(1)} %mul.195) | copy-start | bytes 49156
  6.3 3.0 copy-start.21
  9.2 22.7 %copy-start.14 = (s32[1,64,8]{1,2,0:T(8,128)S(1)}, s32[1,64,8]{1,2,0:T(8,128)}, u32[]{:S(2)}) copy-start(s32[1,64,8]{1,2,0:T(8,128)} %param.15) | copy-start | bytes 6148
  9.2 22.8 %copy-start.19 = (f32[1,64,128]{2,1,0:T(8,128)S(1)}, f32[1,64,128]{2,1,0:T(8,128)}, u32[]{:S(2)}) copy-start(f32[1,64,128]{2,1,0:T(8,128)} %param.17) | copy-start | bytes 98308
  9.2 62.5 %all-to-all-start.3 = ((bf16[32,8,4096]{2,1,0:T(8,128)(2,1)}), bf16[32,8,4096]{2,1,0:T(8,128)(2,1)S(1)}, u32[]{:S(2)}, u32[]{:S(2)}) async-start(bf16[32,8,4096]{2,1,0:T(8,128)(2,1)} %bitcast.137), calls=%async_computation.3 | async-start | bytes 4194304 | tf_op jit(solution)/shard_map/all_to_all | solution.py:150
  19.9 30.8 %collective-permute-start.1 = (bf16[64,4096]{1,0:T(8,128)(2,1)}, bf16[64,4096]{1,0:T(8,128)(2,1)S(1)}, u32[]{:S(2)}, u32[]{:S(2)}) collective-permute-start(bf16[64,4096]{1,0:T(8,128)(2,1)} %bitcast.150), channel_id=1, source_target_pairs={{32,0},{64,32},{96,64},{128,96},{160,128},{192,160},{224,192},{256... | collective-permute-start | bytes 1572872 | tf_op jit(solution)/shard_map/ppermute | solution.py:19
  50.7 22.5 %copy-start.7 = (bf16[64,4096]{1,0:T(8,128)(2,1)}, bf16[64,4096]{1,0:T(8,128)(2,1)S(1)}, u32[]{:S(2)}) copy-start(bf16[64,4096]{1,0:T(8,128)(2,1)S(1)} %collective-permute-done.1) | copy-start | bytes 1572868
  73.2 6.9 %copy-start.15 = (s32[1,64,8]{1,2,0:T(8,128)S(1)}, s32[1,64,8]{1,2,0:T(8,128)}, u32[]{:S(2)}) copy-start(s32[1,64,8]{1,2,0:T(8,128)} %param.14) | copy-start | bytes 6148
  73.2 55.0 %all-to-all-start.2 = ((bf16[32,8,4096]{2,1,0:T(8,128)(2,1)}), bf16[32,8,4096]{2,1,0:T(8,128)(2,1)}, u32[]{:S(2)}, u32[]{:S(2)}) async-start(bf16[32,8,4096]{2,1,0:T(8,128)(2,1)} %bitcast.136), calls=%async_computation.2 | async-start | bytes 4194304 | tf_op jit(solution)/shard_map/all_to_all | solution.py:151
  78.2 27.9 %collective-permute-start = (bf16[64,4096]{1,0:T(8,128)(2,1)}, bf16[64,4096]{1,0:T(8,128)(2,1)S(1)}, u32[]{:S(2)}, u32[]{:S(2)}) collective-permute-start(bf16[64,4096]{1,0:T(8,128)(2,1)} %bitcast.151), channel_id=1, source_target_pairs={{480,0},{0,32},{32,64},{64,96},{96,128},{128,160},{160,192},{192,2... | collective-permute-start | bytes 1572872 | tf_op jit(solution)/shard_map/ppermute | solution.py:19
  81.7 24.6 %copy-start.10 = (s32[64,8,2]{0,2,1:T(2,128)}, s32[64,8,2]{0,2,1:T(2,128)S(1)}, u32[]{:S(2)}) copy-start(s32[64,8,2]{0,2,1:T(2,128)S(1)} %compare_convert_fusion.1) | copy-start | bytes 12292
  81.7 24.6 %copy-start.17 = (s32[64,2,8]{0,2,1:T(8,128)}, s32[64,2,8]{0,2,1:T(8,128)S(1)}, u32[]{:S(2)}) copy-start(s32[64,2,8]{0,2,1:T(8,128)S(1)} %select_reduce_fusion.3) | copy-start | bytes 12292
  106.1 23.8 %copy-start.5 = (bf16[64,4096]{1,0:T(8,128)(2,1)}, bf16[64,4096]{1,0:T(8,128)(2,1)S(1)}, u32[]{:S(2)}) copy-start(bf16[64,4096]{1,0:T(8,128)(2,1)S(1)} %collective-permute-done) | copy-start | bytes 1572868
  129.9 56.5 %all-to-all-start = ((bf16[32,8,4096]{2,1,0:T(8,128)(2,1)}), bf16[32,8,4096]{2,1,0:T(8,128)(2,1)}, u32[]{:S(2)}, u32[]{:S(2)}) async-start(bf16[32,8,4096]{2,1,0:T(8,128)(2,1)} %bitcast.138), calls=%async_computation | async-start | bytes 4194304 | tf_op jit(solution)/shard_map/all_to_all | solution.py:138
  136.2 2.0 copy-start.4
  186.3 55.7 %all-to-all-start.4 = ((bf16[32,8,4096]{2,1,0:T(8,128)(2,1)}), bf16[32,8,4096]{2,1,0:T(8,128)(2,1)S(1)}, u32[]{:S(2)}, u32[]{:S(2)}) async-start(bf16[32,8,4096]{2,1,0:T(8,128)(2,1)} %fusion.2), calls=%async_computation.4 | async-start | bytes 4194304 | tf_op jit(solution)/shard_map/all_to_all | solution.py:148
  200.2 48.8 %copy-start.16 = (s32[1,64,8]{1,2,0:T(8,128)S(1)}, s32[1,64,8]{1,2,0:T(8,128)}, u32[]{:S(2)}) copy-start(s32[1,64,8]{1,2,0:T(8,128)} %param.14) | copy-start | bytes 6148
  200.2 48.9 %copy-start.9 = (f32[1,64,128]{2,1,0:T(8,128)S(1)}, f32[1,64,128]{2,1,0:T(8,128)}, u32[]{:S(2)}) copy-start(f32[1,64,128]{2,1,0:T(8,128)} %param.16) | copy-start | bytes 98308
  200.2 141.9 %copy-start.11 = (s32[64,8,2]{0,2,1:T(2,128)S(1)}, s32[64,8,2]{0,2,1:T(2,128)}, u32[]{:S(2)}) copy-start(s32[64,8,2]{0,2,1:T(2,128)} %copy-done.10) | copy-start | bytes 12292
  242.1 1.3 copy-start.1
  243.4 103.5 %all-to-all-start.1 = ((bf16[32,8,4096]{2,1,0:T(8,128)(2,1)}), bf16[32,8,4096]{2,1,0:T(8,128)(2,1)S(1)}, u32[]{:S(2)}, u32[]{:S(2)}) async-start(bf16[32,8,4096]{2,1,0:T(8,128)(2,1)} %fusion.1), calls=%async_computation.1 | async-start | bytes 4194304 | tf_op jit(solution)/shard_map/all_to_all | solution.py:136
  249.0 95.6 %copy-start.2 = (bf16[1,64,4096]{2,1,0:T(8,128)(2,1)S(1)}, bf16[1,64,4096]{2,1,0:T(8,128)(2,1)}, u32[]{:S(2)}) copy-start(bf16[1,64,4096]{2,1,0:T(8,128)(2,1)} %param.13) | copy-start | bytes 1572868
  249.0 95.6 %copy-start.13 = (f32[1,4096]{1,0:T(1,128)S(1)}, f32[1,4096]{1,0:T(1,128)}, u32[]{:S(2)}) copy-start(f32[1,4096]{1,0:T(1,128)} %copy-done.12) | copy-start | bytes 49156
  344.6 2.6 copy-start.18
  346.8 3.0 copy-start.20
  346.9 3.0 copy-start.22
  346.9 1.0 copy-start.6
  346.9 3.0 copy-start.3
  346.9 3.0 copy-start.8
where the time goes:
time: 354 us; the launch traced here: 351 us
  waiting for transfers between devices  162 us (46%)
  blocking collectives  91.7 us (26%)
  starting transfers between devices  47.2 us (13%)
  matrix products  29.1 us (8%)
  other arithmetic  10.9 us (3%)
  local copies, waits for them, and re-layouts  9.16 us (3%)
    psum x1, blocking collectives, body(): counts, prob_sums = lax.psum((counts, prob_sums), 'expert')  91.7 us
    ppermute x2, waiting for transfers between devices, from_behind(): return lax.ppermute(block, axis, route)  42.5 us
    all_to_all x1, waiting for transfers between devices, body(): lax.all_to_all(expert_backward(lax.all_to_all(saved_send, 'expert', split...  41.9 us
    all_to_all x1, waiting for transfers between devices, body(): lax.all_to_all(fwd_send, 'expert', split_axis=0, concat_axis=0, tiled=True)  35.8 us
    all_to_all x1, waiting for transfers between devices, body(): lax.all_to_all(grad_send, 'expert', split_axis=0, concat_axis=0, tiled=True)  20.9 us
    all_to_all x1, waiting for transfers between devices, body(): lax.all_to_all(saved_send, 'expert', split_axis=0, concat_axis=0, tiled=T...  20.8 us
    ppermute x2, starting transfers between devices, from_behind(): return lax.ppermute(block, axis, route)  13.9 us
    all_to_all x1, starting transfers between devices, body(): lax.all_to_all(saved_send, 'expert', split_axis=0, concat_axis=0, tiled=T...  10.7 us
  transfers between devices with their start and end apart: 7, of which 6 were waited for; matrix products, arithmetic and copies ran while one was open for 9% of the time, Pallas kernels for 0%

commit v1 on v0

v1 whole, which is shorter than its diff:
```python
import jax
import jax.numpy as jnp
from jax import lax
from jax.experimental import pallas as pl
from jax.experimental.pallas import tpu as pltpu
from jax.sharding import Mesh, PartitionSpec as P

EXPERTS = 128
TOPK = 8
EXP_WIN = 2
CAP = 8
SLOTS = EXP_WIN * CAP
EPS = 1e-06
exact = lax.Precision.HIGHEST
f32 = jnp.float32
bf16 = jnp.bfloat16
NT = (((1,), (1,)), ((), ()))
PARAMS = pltpu.CompilerParams(vmem_limit_bytes=48 << 20)
EXPERT_AXES = ("y", "xl", "core")


def kernel_call(body, outs, *args):
    return pl.pallas_call(body, out_shape=outs, compiler_params=PARAMS)(*args)


def shape(dims, dtype):
    return jax.ShapeDtypeStruct(dims, dtype)


def iota(dims, axis):
    return lax.broadcasted_iota(jnp.int32, dims, axis)


def slot_tables(routes_t, logits):
    tokens, experts = logits.shape
    ids = iota((experts, tokens), 0)
    hot_t = jnp.zeros((experts, tokens), f32)
    for k in range(TOPK):
        hot_t = hot_t + jnp.where(ids == routes_t[k : k + 1, :], 1.0, 0.0)
    rows, cols = iota((tokens, tokens), 0), iota((tokens, tokens), 1)
    eye = jnp.where(rows == cols, 1.0, 0.0).astype(bf16)
    hot = lax.dot_general(eye, hot_t.astype(bf16), NT, preferred_element_type=f32)
    chosen = jnp.where(hot > 0.5, logits, -jnp.inf)
    powers = jnp.exp(chosen - jnp.max(chosen, axis=1, keepdims=True))
    gates = powers / jnp.sum(powers, axis=1, keepdims=True)
    before = jnp.where(rows < cols, 1.0, 0.0).astype(bf16)
    first = hot_t[0:8, :]
    earlier = jnp.dot(first.astype(bf16), before, preferred_element_type=f32)
    slot = iota((CAP, tokens), 0).astype(f32)
    select = jnp.concatenate(
        [
            jnp.where((earlier[e : e + 1, :] == slot) & (first[e : e + 1, :] > 0.5), 1.0, 0.0)
            for e in range(EXP_WIN)
        ],
        axis=0,
    )
    select_t = lax.dot_general(eye, select.astype(bf16), NT, preferred_element_type=f32)
    picked = jnp.dot(select, gates, precision=exact, preferred_element_type=f32)
    own = iota((SLOTS, experts), 1) == iota((SLOTS, experts), 0) // CAP
    gate_slot = jnp.sum(jnp.where(own, picked, 0.0), axis=1, keepdims=True)
    return hot, select.astype(bf16), select_t.astype(bf16), gate_slot


def spread(send_ref, rows):
    stops = send_ref.shape[0]
    for i in range(stops):
        e = i * EXP_WIN // stops
        send_ref[i, :, :] = rows[e * CAP : (e + 1) * CAP, :]


def normed_rows(rows, gain):
    inverse = lax.rsqrt(jnp.mean(rows * rows, axis=1, keepdims=True) + EPS)
    return (rows * inverse * gain).astype(bf16), inverse


def prepare_body(
    saved, gain, broutes, blogits, froutes, flogits,
    send, picked, inverse_out, bsel, bsel_t, bgate, fsel, fsel_t, fgate, usage,
):
    wide = (SLOTS, EXPERTS)
    _, select, select_t, gate = slot_tables(broutes[...], blogits[...])
    bsel[...], bsel_t[...], bgate[...] = select, select_t, jnp.broadcast_to(gate, wide)
    rows = jnp.dot(select, saved[...], preferred_element_type=f32)
    normed, inverse = normed_rows(rows, gain[...].astype(f32))
    picked[...] = rows.astype(bf16)
    inverse_out[...] = jnp.broadcast_to(inverse, wide)
    spread(send, normed)
    logits = flogits[...]
    hot, select, select_t, gate = slot_tables(froutes[...], logits)
    fsel[...], fsel_t[...], fgate[...] = select, select_t, jnp.broadcast_to(gate, wide)
    powers = jnp.exp(logits - jnp.max(logits, axis=1, keepdims=True))
    probs = powers / jnp.sum(powers, axis=1, keepdims=True)
    usage[...] = jnp.concatenate(
        [jnp.sum(hot, axis=0, keepdims=True), jnp.sum(probs, axis=0, keepdims=True)], axis=0
    )


def grad_rows_body(upstream, select, gate, send):
    rows = jnp.dot(select[...], upstream[...], preferred_element_type=f32)
    spread(send, (rows * gate[:, 0:1]).astype(bf16))


def fwd_rows_body(x_in, select, gain, send):
    rows = jnp.dot(select[...], x_in[...], preferred_element_type=f32)
    spread(send, normed_rows(rows, gain[...].astype(f32))[0])


def nt(a, b):
    return lax.dot_general(a, b, NT, preferred_element_type=f32)


COLS = 512


def fwd_expert_body(mine, other, slab, slab2, out_mine, out_other):
    hid = slab.shape[0] // 3
    for rows, out in ((mine[...], out_mine), (other[...], out_other)):
        hidden = []
        for w in (slab, slab2):
            pre = nt(rows, w[0 : 2 * hid, :])
            hidden.append((jax.nn.silu(pre[:, :hid]) * pre[:, hid:]).astype(bf16))
        for c in range(0, out.shape[1], COLS):
            part = sum(
                jnp.dot(h, w[2 * hid :, c : c + COLS], preferred_element_type=f32)
                for h, w in zip(hidden, (slab, slab2))
            )
            out[:, c : c + COLS] = part.astype(bf16)


def bwd_expert_body(mine, other, gmine, gother, slab, slab2, out_mine, out_other):
    hid = slab.shape[0] // 3
    for rows, grads, out in (
        (mine[...], gmine[...], out_mine),
        (other[...], gother[...], out_other),
    ):
        back = []
        for w in (slab, slab2):
            pre = nt(rows, w[0 : 2 * hid, :])
            d_hidden = nt(grads, w[2 * hid :, :])
            a, b = pre[:, :hid], pre[:, hid:]
            sigma = jax.nn.sigmoid(a)
            d_gate = (d_hidden * b * sigma * (1.0 + a * (1.0 - sigma))).astype(bf16)
            d_up = (d_hidden * a * sigma).astype(bf16)
            back.append((d_gate, d_up))
        for c in range(0, out.shape[1], COLS):
            part = jnp.zeros((out.shape[0], COLS), f32)
            for (d_gate, d_up), w in zip(back, (slab, slab2)):
                part = part + jnp.dot(d_gate, w[0:hid, c : c + COLS], preferred_element_type=f32)
                part = part + jnp.dot(
                    d_up, w[hid : 2 * hid, c : c + COLS], preferred_element_type=f32
                )
            out[:, c : c + COLS] = part.astype(bf16)


def gathered(parts):
    stops = parts.shape[0]
    half = stops // EXP_WIN
    return jnp.concatenate(
        [
            sum(parts[e * half + i, :, :].astype(f32) for i in range(half))
            for e in range(EXP_WIN)
        ],
        axis=0,
    )


def placed(select_t, rows):
    high = rows.astype(bf16)
    rest = rows - high.astype(f32)
    mid = rest.astype(bf16)
    low = (rest - mid.astype(f32)).astype(bf16)
    return sum(jnp.dot(select_t, p, preferred_element_type=f32) for p in (low, mid, high))


def fwd_out_body(parts, select_t, gate, x_in, out):
    rows = gathered(parts) * gate[:, 0:1]
    out[...] = (x_in[...].astype(f32) + placed(select_t[...], rows)).astype(bf16)


def bwd_out_body(parts, select_t, picked, inverse, gain, upstream, out):
    weighted = gain[...].astype(f32) * gathered(parts)
    inv = inverse[:, 0:1]
    x = picked[...].astype(f32)
    rows = inv * weighted - x * (inv * inv * inv) * jnp.mean(x * weighted, axis=1, keepdims=True)
    out[...] = (upstream[...].astype(f32) + placed(select_t[...], rows)).astype(bf16)


def shifted(block, axis, distance):
    n = lax.axis_size(axis)
    return lax.ppermute(block, axis, [((i - distance) % n, i) for i in range(n)])


def over_y(block):
    return lax.all_to_all(block, "y", split_axis=0, concat_axis=0, tiled=True)


def body(
    fwd_sent, bwd_sent, bwd_saved, fwd_routes, bwd_routes, fwd_logits, bwd_logits,
    norm_gain, w_gate, w_up, w_down,
):
    stops = lax.axis_size("y")
    tokens, width = fwd_sent.shape[1:]
    upstream = shifted(bwd_sent[0], "section", -1)
    x_in = shifted(fwd_sent[0], "section", 1)
    slab = jnp.concatenate([w_gate[0].T, w_up[0].T, w_down[0]], axis=0)
    slab2 = shifted(slab, "core", 1)
    saved = bwd_saved[0]
    sent = shape((stops, CAP, width), bf16)
    sel, sel_t = shape((SLOTS, tokens), bf16), shape((tokens, SLOTS), bf16)
    wide = shape((SLOTS, EXPERTS), f32)
    saved_send, picked, inverse, bsel, bsel_t, bgate, fsel, fsel_t, fgate, usage = kernel_call(
        prepare_body,
        (sent, shape((SLOTS, width), bf16), wide, sel, sel_t, wide, sel, sel_t, wide,
         shape((2, EXPERTS), f32)),
        saved, norm_gain, bwd_routes[0].T, bwd_logits[0], fwd_routes[0].T, fwd_logits[0],
    )
    saved_mine = over_y(saved_send).reshape(-1, width)
    saved_other = shifted(saved_mine, "xl", 1)
    grad_send = kernel_call(grad_rows_body, sent, upstream, bsel, bgate)
    grad_mine = over_y(grad_send).reshape(-1, width)
    grad_other = shifted(grad_mine, "xl", 1)
    fwd_send = kernel_call(fwd_rows_body, sent, x_in, fsel, norm_gain)
    fwd_mine = over_y(fwd_send).reshape(-1, width)
    fwd_other = shifted(fwd_mine, "xl", 1)
    result = shape(saved_mine.shape, bf16)
    back_mine, back_other = kernel_call(
        bwd_expert_body, (result, result), saved_mine, saved_other, grad_mine, grad_other, slab, slab2
    )
    back = (back_mine.astype(f32) + shifted(back_other, "xl", 1).astype(f32)).astype(bf16)
    back_parts = over_y(back.reshape(stops, CAP, width))
    out_mine, out_other = kernel_call(
        fwd_expert_body, (result, result), fwd_mine, fwd_other, slab, slab2
    )
    outs = (out_mine.astype(f32) + shifted(out_other, "xl", 1).astype(f32)).astype(bf16)
    out_parts = over_y(outs.reshape(stops, CAP, width))
    full = shape((tokens, width), bf16)
    bwd_out = kernel_call(
        bwd_out_body, full, back_parts, bsel_t, picked, inverse, norm_gain, upstream
    )
    fwd_out = kernel_call(fwd_out_body, full, out_parts, fsel_t, fgate, x_in)
    devices = lax.axis_size(EXPERT_AXES)
    shared = lax.all_to_all(
        jnp.broadcast_to(usage[None], (devices, 2, EXPERTS)),
        EXPERT_AXES, split_axis=0, concat_axis=0, tiled=True,
    )
    counts, prob_sums = jnp.sum(shared, axis=0)
    tokens_all = tokens * devices
    balance = EXPERTS * (counts / (tokens_all * TOPK)) * (prob_sums / tokens_all)
    return (fwd_out[None], bwd_out[None], balance[None])


def solution(mesh):
    sections = mesh.shape["section"]
    grid = mesh.devices.reshape(sections, -1, 2, 2)
    inner = Mesh(grid, ("section",) + EXPERT_AXES)
    rows = P("section", EXPERT_AXES, None)
    return jax.shard_map(
        body,
        mesh=inner,
        in_specs=(
            rows, rows, rows, rows, rows, rows, rows,
            P("section", None),
            P("section", None, EXPERT_AXES),
            P("section", None, EXPERT_AXES),
            rows,
        ),
        out_specs=(rows, rows, P("section", None)),
        check_vma=False,
    )
```

time: 354 us -> 170 us (0.48)
  the two profiles are of different devices: /device:TPU:1 before, /device:TPU:2 now
where the time goes in v1:
time: 170 us; the launch traced here: 169 us
  starting transfers between devices  66.6 us (39%)
  waiting for transfers between devices  62.1 us (37%)
  Pallas kernels  19.3 us (11%)
  local copies, waits for them, and re-layouts  13.8 us (8%)
  other arithmetic  5.98 us (4%)
    all_to_all x5, starting transfers between devices, over_y(): return lax.all_to_all(block, 'y', split_axis=0, concat_axis=0, tiled=True)  32 us
    all_to_all x5, waiting for transfers between devices, over_y(): return lax.all_to_all(block, 'y', split_axis=0, concat_axis=0, tiled=True)  31.6 us
    ppermute x8, waiting for transfers between devices, shifted(): lax.ppermute(block, axis, [((i - distance) % n, i) for i in range(n)])  30.5 us
    ppermute x8, starting transfers between devices, shifted(): lax.ppermute(block, axis, [((i - distance) % n, i) for i in range(n)])  26.3 us
    pallas_call x7, Pallas kernels, kernel_call(): return pl.pallas_call(body, out_shape=outs, compiler_params=PARAMS)(*args)  19.3 us
    unnamed x56, local copies, waits for them, and re-layouts  13.2 us
    all_to_all x1, starting transfers between devices, body(): lax.all_to_all(jnp.broadcast_to(usage[None], (devices, 2, EXPERTS)), EXPE...  8.35 us
  transfers between devices with their start and end apart: 14, of which 7 were waited for; matrix products, arithmetic and copies ran while one was open for 4% of the time, Pallas kernels for 9%

profile of v1, /device:TPU:2, one launch (start us, length us, event | category | flops | bytes accessed | tf_op | source)
XLA Modules:
  0.0 168.6 jit_solution(15150535361138511742)
XLA Ops:
  0.6 1.0 copy-done.5
  1.7 0.7 copy-done.6
  2.4 0.8 copy-done.8
  3.2 0.8 copy-done.9
  3.9 0.7 copy-done.20
  4.6 0.7 copy-done.21
  5.3 1.7 %shard_map.130 = (bf16[8,8,4096]{2,1,0:T(8,128)(2,1)}, bf16[16,4096]{1,0:T(8,128)(2,1)S(1)}, f32[16,128]{1,0:T(8,128)S(1)}, bf16[16,64]{1,0:T(8,128)(2,1)S(1)}, ...) custom-call(bf16[64,4096]{1,0:T(8,128)(2,1)S(1)} %bitcast.27, ...), custom_call_target="tpu_custom_call" | custom-call | tf_op jit(solution)/shard_map/pallas_call | solution.py:23
  7.0 0.6 copy-done.10
  7.6 0.6 copy-done.12
  8.2 0.6 copy-done.14
  9.4 0.6 copy-done.18
  10.0 0.6 copy-done.22
  10.6 0.6 copy-done.24
  11.8 7.1 %all-to-all-start.2 = ((bf16[8,8,4096]{2,1,0:T(8,128)(2,1)}), bf16[8,8,4096]{2,1,0:T(8,128)(2,1)}, u32[]{:S(2)}, u32[]{:S(2)}) async-start(bf16[8,8,4096]{2,1,0:T(8,128)(2,1)} %get-tuple-element.22), calls=%async_computation.2 | async-start | bytes 1048576 | tf_op jit(solution)/shard_map/all_to_all | solution.py:194
  18.9 4.0 %collective-permute-start = (bf16[64,4096]{1,0:T(8,128)(2,1)}, bf16[64,4096]{1,0:T(8,128)(2,1)S(1)}, u32[]{:S(2)}, u32[]{:S(2)}) collective-permute-start(bf16[64,4096]{1,0:T(8,128)(2,1)} %bitcast.37), channel_id=1, source_target_pairs={{480,0},{0,32},{32,64},{64,96},{96,128},{128,160},{160,192},{192,2... | collective-permute-start | bytes 1572872 | tf_op jit(solution)/shard_map/ppermute | solution.py:190
  22.9 1.8 %pad_maximum_fusion.slab = bf16[288,4096]{1,0:T(8,128)(2,1)S(1)} fusion(bf16[96,4096]{1,0:T(8,128)(2,1)} %bitcast.32, bf16[96,4096]{1,0:T(8,128)(2,1)} %bitcast.33, bf16[96,4096]{1,0:T(8,128)(2,1)} %bitcast.34), kind=kLoop, calls=%fused_computation | loop fusion | flops 7077888 | bytes 4718592 | tf_op jit(solution)/shard_map/concatenate | solution.py:205
  24.7 1.9 %collective-permute-start.2 = (bf16[288,4096]{1,0:T(8,128)(2,1)S(1)}, bf16[288,4096]{1,0:T(8,128)(2,1)}, u32[]{:S(2)}, u32[]{:S(2)}) collective-permute-start(bf16[288,4096]{1,0:T(8,128)(2,1)S(1)} %pad_maximum_fusion.slab), channel_id=1, source_target_pairs={{1,0},{0,1},{3,2},{2,3},{5,4},{4,5},{7,6},{6,7},{9,8},{8,9},{11,10... | collective-permute-start | bytes 7077896 | tf_op jit(solution)/shard_map/ppermute | solution.py:190
  26.6 16.6 %collective-permute-done.x_in = bf16[64,4096]{1,0:T(8,128)(2,1)S(1)} collective-permute-done((bf16[64,4096]{1,0:T(8,128)(2,1)}, bf16[64,4096]{1,0:T(8,128)(2,1)S(1)}, u32[]{:S(2)}, u32[]{:S(2)}) %collective-permute-start) | collective-permute-done | bytes 524320 | tf_op jit(solution)/shard_map/ppermute | solution.py:190
  43.2 1.1 shard_map.131
  44.3 6.9 %all-to-all-start = ((bf16[8,8,4096]{2,1,0:T(8,128)(2,1)}), bf16[8,8,4096]{2,1,0:T(8,128)(2,1)}, u32[]{:S(2)}, u32[]{:S(2)}) async-start(bf16[8,8,4096]{2,1,0:T(8,128)(2,1)} %shard_map.131), calls=%async_computation | async-start | bytes 1048576 | tf_op jit(solution)/shard_map/all_to_all | solution.py:194
  51.3 5.1 %collective-permute-start.5 = (bf16[64,4096]{1,0:T(8,128)(2,1)}, bf16[64,4096]{1,0:T(8,128)(2,1)S(1)}, u32[]{:S(2)}, u32[]{:S(2)}) collective-permute-start(bf16[64,4096]{1,0:T(8,128)(2,1)} %bitcast.38), channel_id=1, source_target_pairs={{32,0},{64,32},{96,64},{128,96},{160,128},{192,160},{224,192},{256... | collective-permute-start | bytes 1572872 | tf_op jit(solution)/shard_map/ppermute | solution.py:190
  56.4 10.6 %collective-permute-done.5.upstream = bf16[64,4096]{1,0:T(8,128)(2,1)S(1)} collective-permute-done((bf16[64,4096]{1,0:T(8,128)(2,1)}, bf16[64,4096]{1,0:T(8,128)(2,1)S(1)}, u32[]{:S(2)}, u32[]{:S(2)}) %collective-permute-start.5) | collective-permute-done | bytes 524320 | tf_op jit(solution)/shard_map/ppermute | solution.py:190
  67.1 0.7 copy-done.19
  67.8 0.7 copy-done.23
  68.7 0.8 copy-done
  69.4 6.9 %all-to-all-start.3 = ((bf16[8,8,4096]{2,1,0:T(8,128)(2,1)}), bf16[8,8,4096]{2,1,0:T(8,128)(2,1)}, u32[]{:S(2)}, u32[]{:S(2)}) async-start(bf16[8,8,4096]{2,1,0:T(8,128)(2,1)} %copy-done), calls=%async_computation.3 | async-start | bytes 1048576 | tf_op jit(solution)/shard_map/all_to_all | solution.py:194
  76.4 3.3 %collective-permute-start.1 = (bf16[64,4096]{1,0:T(8,128)(2,1)}, bf16[64,4096]{1,0:T(8,128)(2,1)}, u32[]{:S(2)}, u32[]{:S(2)}) collective-permute-start(bf16[64,4096]{1,0:T(8,128)(2,1)} %bitcast.8.mine), channel_id=1, source_target_pairs={{2,0},{0,2},{3,1},{1,3},{6,4},{4,6},{7,5},{5,7},{10,8},{8,10},{11,... | collective-permute-start | bytes 1572872 | tf_op jit(solution)/shard_map/ppermute | solution.py:190
  79.7 2.5 %collective-permute-start.4 = (bf16[64,4096]{1,0:T(8,128)(2,1)}, bf16[64,4096]{1,0:T(8,128)(2,1)}, u32[]{:S(2)}, u32[]{:S(2)}) collective-permute-start(bf16[64,4096]{1,0:T(8,128)(2,1)} %bitcast.16.mine), channel_id=1, source_target_pairs={{2,0},{0,2},{3,1},{1,3},{6,4},{4,6},{7,5},{5,7},{10,8},{8,10},{11,... | collective-permute-start | bytes 1572872 | tf_op jit(solution)/shard_map/ppermute | solution.py:190
  82.2 9.1 %all-to-all-done.3 = bf16[8,8,4096]{2,1,0:T(8,128)(2,1)} async-done(((bf16[8,8,4096]{2,1,0:T(8,128)(2,1)}), bf16[8,8,4096]{2,1,0:T(8,128)(2,1)}, u32[]{:S(2)}, u32[]{:S(2)}) %all-to-all-start.3) | async-done | bytes 524320 | tf_op jit(solution)/shard_map/all_to_all | solution.py:194
  91.3 3.5 %collective-permute-start.6 = (bf16[64,4096]{1,0:T(8,128)(2,1)}, bf16[64,4096]{1,0:T(8,128)(2,1)}, u32[]{:S(2)}, u32[]{:S(2)}) collective-permute-start(bf16[64,4096]{1,0:T(8,128)(2,1)} %bitcast.18.gmine), channel_id=1, source_target_pairs={{2,0},{0,2},{3,1},{1,3},{6,4},{4,6},{7,5},{5,7},{10,8},{8,10},{11,... | collective-permute-start | bytes 1572872 | tf_op jit(solution)/shard_map/ppermute | solution.py:190
  94.8 5.9 %shard_map.132 = (bf16[64,4096]{1,0:T(8,128)(2,1)S(1)}, bf16[64,4096]{1,0:T(8,128)(2,1)}) custom-call(bf16[64,4096]{1,0:T(8,128)(2,1)} %bitcast.8.mine, bf16[64,4096]{1,0:T(8,128)(2,1)} %collective-permute-done.1.other, bf16[288,4096]{1,0:T(8,128)(2,1)S(1)} %pad_maximum_fusion.slab, bf16[288,4096]{1,0:T(8,128)(2,1)} %collective-permute-done.2.slab2), custom_call_target="tpu_custom_call" | custom-call | tf_op jit(solution)/shard_map/pallas_call | solution.py:23
  100.7 0.8 copy-done.1
  101.5 2.5 %collective-permute-start.3 = (bf16[64,4096]{1,0:T(8,128)(2,1)}, bf16[64,4096]{1,0:T(8,128)(2,1)}, u32[]{:S(2)}, u32[]{:S(2)}) collective-permute-start(bf16[64,4096]{1,0:T(8,128)(2,1)} %get-tuple-element.19), channel_id=1, source_target_pairs={{2,0},{0,2},{3,1},{1,3},{6,4},{4,6},{7,5},{5,7},{10,8},{8,10},{11,... | collective-permute-start | bytes 1572872 | tf_op jit(solution)/shard_map/ppermute | solution.py:190
  104.0 0.6 broadcast_in_dim.15
  104.6 8.4 %all-to-all-start.5 = ((f32[32,2,128]{2,1,0:T(2,128)}), f32[32,2,128]{2,1,0:T(2,128)}, u32[]{:S(2)}, u32[]{:S(2)}) async-start(f32[32,2,128]{2,1,0:T(2,128)} %broadcast_in_dim.15), calls=%async_computation.5 | async-start | bytes 65536 | tf_op jit(solution)/shard_map/all_to_all | solution.py:242
  113.0 2.9 %collective-permute-done.6.gother = bf16[64,4096]{1,0:T(8,128)(2,1)} collective-permute-done((bf16[64,4096]{1,0:T(8,128)(2,1)}, bf16[64,4096]{1,0:T(8,128)(2,1)}, u32[]{:S(2)}, u32[]{:S(2)}) %collective-permute-start.6) | collective-permute-done | bytes 524320 | tf_op jit(solution)/shard_map/ppermute | solution.py:190
  115.9 7.4 %shard_map.135 = (bf16[64,4096]{1,0:T(8,128)(2,1)S(1)}, bf16[64,4096]{1,0:T(8,128)(2,1)}) custom-call(bf16[64,4096]{1,0:T(8,128)(2,1)} %bitcast.16.mine, bf16[64,4096]{1,0:T(8,128)(2,1)} %collective-permute-done.4.other, bf16[64,4096]{1,0:T(8,128)(2,1)} %bitcast.18.gmine, bf16[64,4096]{1,0:T(8,128)(2,1)} %collective-permute-done.6.gother, ...), custom_call_target="tpu_custom_call" | custom-call | tf_op jit(solution)/shard_map/pallas_call | solution.py:23
  123.3 0.8 copy-done.3
  124.1 3.5 %collective-permute-start.7 = (bf16[64,4096]{1,0:T(8,128)(2,1)}, bf16[64,4096]{1,0:T(8,128)(2,1)S(1)}, u32[]{:S(2)}, u32[]{:S(2)}) collective-permute-start(bf16[64,4096]{1,0:T(8,128)(2,1)} %get-tuple-element.26), channel_id=1, source_target_pairs={{2,0},{0,2},{3,1},{1,3},{6,4},{4,6},{7,5},{5,7},{10,8},{8,10},{11,... | collective-permute-start | bytes 1572872 | tf_op jit(solution)/shard_map/ppermute | solution.py:190
  127.6 2.0 %fusion = bf16[8,8,4096]{2,1,0:T(8,128)(2,1)} fusion(bf16[64,4096]{1,0:T(8,128)(2,1)} %collective-permute-done.3, bf16[64,4096]{1,0:T(8,128)(2,1)S(1)} %copy-done.2), kind=kLoop, calls=%fused_computation.3 | loop fusion | flops 1048576 | bytes 1572864 | tf_op jit(solution)/shard_map/reshape | solution.py:235
  129.6 7.5 %all-to-all-start.1 = ((bf16[8,8,4096]{2,1,0:T(8,128)(2,1)}), bf16[8,8,4096]{2,1,0:T(8,128)(2,1)S(1)}, u32[]{:S(2)}, u32[]{:S(2)}) async-start(bf16[8,8,4096]{2,1,0:T(8,128)(2,1)} %fusion), calls=%async_computation.1 | async-start | bytes 1048576 | tf_op jit(solution)/shard_map/all_to_all | solution.py:194
  137.4 0.9 fusion.1
  138.3 12.0 %all-to-all-done.1.parts = bf16[8,8,4096]{2,1,0:T(8,128)(2,1)S(1)} async-done(((bf16[8,8,4096]{2,1,0:T(8,128)(2,1)}), bf16[8,8,4096]{2,1,0:T(8,128)(2,1)S(1)}, u32[]{:S(2)}, u32[]{:S(2)}) %all-to-all-start.1) | async-done | bytes 524320 | tf_op jit(solution)/shard_map/all_to_all | solution.py:194
  150.4 3.5 %all-to-all-start.4 = ((bf16[8,8,4096]{2,1,0:T(8,128)(2,1)}), bf16[8,8,4096]{2,1,0:T(8,128)(2,1)S(1)}, u32[]{:S(2)}, u32[]{:S(2)}) async-start(bf16[8,8,4096]{2,1,0:T(8,128)(2,1)} %fusion.1), calls=%async_computation.4 | async-start | bytes 1048576 | tf_op jit(solution)/shard_map/all_to_all | solution.py:194
  153.9 0.8 reduce_sum.9
  155.2 1.4 shard_map.133
  156.6 10.5 %all-to-all-done.4.parts = bf16[8,8,4096]{2,1,0:T(8,128)(2,1)S(1)} async-done(((bf16[8,8,4096]{2,1,0:T(8,128)(2,1)}), bf16[8,8,4096]{2,1,0:T(8,128)(2,1)S(1)}, u32[]{:S(2)}, u32[]{:S(2)}) %all-to-all-start.4) | async-done | bytes 524320 | tf_op jit(solution)/shard_map/all_to_all | solution.py:194
  167.1 1.5 shard_map.136
  (49 shorter events, 2.3 us)
Async XLA Ops:
  0.6 1.0 copy-start.5
  1.7 0.7 copy-start.6
  2.4 0.8 copy-start.8
  3.2 0.8 copy-start.9
  3.9 0.7 copy-start.20
  4.6 0.7 copy-start.21
  7.0 0.6 copy-start.10
  7.6 0.6 copy-start.12
  8.2 0.6 copy-start.14
  8.8 0.6 copy-start.16
  9.4 0.6 copy-start.18
  10.0 0.6 copy-start.22
  10.6 0.6 copy-start.24
  11.2 0.6 copy-start.26
  11.8 32.6 %all-to-all-start.2 = ((bf16[8,8,4096]{2,1,0:T(8,128)(2,1)}), bf16[8,8,4096]{2,1,0:T(8,128)(2,1)}, u32[]{:S(2)}, u32[]{:S(2)}) async-start(bf16[8,8,4096]{2,1,0:T(8,128)(2,1)} %get-tuple-element.22), calls=%async_computation.2 | async-start | bytes 1048576 | tf_op jit(solution)/shard_map/all_to_all | solution.py:194
  18.9 24.3 %collective-permute-start = (bf16[64,4096]{1,0:T(8,128)(2,1)}, bf16[64,4096]{1,0:T(8,128)(2,1)S(1)}, u32[]{:S(2)}, u32[]{:S(2)}) collective-permute-start(bf16[64,4096]{1,0:T(8,128)(2,1)} %bitcast.37), channel_id=1, source_target_pairs={{480,0},{0,32},{32,64},{64,96},{96,128},{128,160},{160,192},{192,2... | collective-permute-start | bytes 1572872 | tf_op jit(solution)/shard_map/ppermute | solution.py:190
  22.9 20.3 %copy-start.7 = (bf16[1,4096]{1,0:T(2,128)(2,1)S(1)}, bf16[1,4096]{1,0:T(2,128)(2,1)}, u32[]{:S(2)}) copy-start(bf16[1,4096]{1,0:T(2,128)(2,1)} %gain.5) | copy-start | bytes 24580
  22.9 20.3 %copy-start.25 = (bf16[16,64]{1,0:T(8,128)(2,1)S(1)}, bf16[16,64]{1,0:T(8,128)(2,1)}, u32[]{:S(2)}) copy-start(bf16[16,64]{1,0:T(8,128)(2,1)} %copy-done.24) | copy-start | bytes 6148
  24.7 70.1 %collective-permute-start.2 = (bf16[288,4096]{1,0:T(8,128)(2,1)S(1)}, bf16[288,4096]{1,0:T(8,128)(2,1)}, u32[]{:S(2)}, u32[]{:S(2)}) collective-permute-start(bf16[288,4096]{1,0:T(8,128)(2,1)S(1)} %pad_maximum_fusion.slab), channel_id=1, source_target_pairs={{1,0},{0,1},{3,2},{2,3},{5,4},{4,5},{7,6},{6,7},{9,8},{8,9},{11,10... | collective-permute-start | bytes 7077896 | tf_op jit(solution)/shard_map/ppermute | solution.py:190
  44.3 25.1 %all-to-all-start = ((bf16[8,8,4096]{2,1,0:T(8,128)(2,1)}), bf16[8,8,4096]{2,1,0:T(8,128)(2,1)}, u32[]{:S(2)}, u32[]{:S(2)}) async-start(bf16[8,8,4096]{2,1,0:T(8,128)(2,1)} %shard_map.131), calls=%async_computation | async-start | bytes 1048576 | tf_op jit(solution)/shard_map/all_to_all | solution.py:194
  51.3 15.8 %collective-permute-start.5 = (bf16[64,4096]{1,0:T(8,128)(2,1)}, bf16[64,4096]{1,0:T(8,128)(2,1)S(1)}, u32[]{:S(2)}, u32[]{:S(2)}) collective-permute-start(bf16[64,4096]{1,0:T(8,128)(2,1)} %bitcast.38), channel_id=1, source_target_pairs={{32,0},{64,32},{96,64},{128,96},{160,128},{192,160},{224,192},{256... | collective-permute-start | bytes 1572872 | tf_op jit(solution)/shard_map/ppermute | solution.py:190
  67.1 0.7 copy-start.19
  67.8 0.7 copy-start.23
  68.6 0.8 copy-start
  69.4 21.9 %all-to-all-start.3 = ((bf16[8,8,4096]{2,1,0:T(8,128)(2,1)}), bf16[8,8,4096]{2,1,0:T(8,128)(2,1)}, u32[]{:S(2)}, u32[]{:S(2)}) async-start(bf16[8,8,4096]{2,1,0:T(8,128)(2,1)} %copy-done), calls=%async_computation.3 | async-start | bytes 1048576 | tf_op jit(solution)/shard_map/all_to_all | solution.py:194
  76.4 18.4 %collective-permute-start.1 = (bf16[64,4096]{1,0:T(8,128)(2,1)}, bf16[64,4096]{1,0:T(8,128)(2,1)}, u32[]{:S(2)}, u32[]{:S(2)}) collective-permute-start(bf16[64,4096]{1,0:T(8,128)(2,1)} %bitcast.8.mine), channel_id=1, source_target_pairs={{2,0},{0,2},{3,1},{1,3},{6,4},{4,6},{7,5},{5,7},{10,8},{8,10},{11,... | collective-permute-start | bytes 1572872 | tf_op jit(solution)/shard_map/ppermute | solution.py:190
  79.7 33.3 %collective-permute-start.4 = (bf16[64,4096]{1,0:T(8,128)(2,1)}, bf16[64,4096]{1,0:T(8,128)(2,1)}, u32[]{:S(2)}, u32[]{:S(2)}) collective-permute-start(bf16[64,4096]{1,0:T(8,128)(2,1)} %bitcast.16.mine), channel_id=1, source_target_pairs={{2,0},{0,2},{3,1},{1,3},{6,4},{4,6},{7,5},{5,7},{10,8},{8,10},{11,... | collective-permute-start | bytes 1572872 | tf_op jit(solution)/shard_map/ppermute | solution.py:190
  91.3 12.7 %copy-start.27 = (f32[2,128]{1,0:T(2,128)S(1)}, f32[2,128]{1,0:T(2,128)}, u32[]{:S(2)}) copy-start(f32[2,128]{1,0:T(2,128)} %copy-done.26) | copy-start | bytes 3076
  91.3 24.6 %collective-permute-start.6 = (bf16[64,4096]{1,0:T(8,128)(2,1)}, bf16[64,4096]{1,0:T(8,128)(2,1)}, u32[]{:S(2)}, u32[]{:S(2)}) collective-permute-start(bf16[64,4096]{1,0:T(8,128)(2,1)} %bitcast.18.gmine), channel_id=1, source_target_pairs={{2,0},{0,2},{3,1},{1,3},{6,4},{4,6},{7,5},{5,7},{10,8},{8,10},{11,... | collective-permute-start | bytes 1572872 | tf_op jit(solution)/shard_map/ppermute | solution.py:190
  100.7 0.8 copy-start.1
  101.5 26.1 %collective-permute-start.3 = (bf16[64,4096]{1,0:T(8,128)(2,1)}, bf16[64,4096]{1,0:T(8,128)(2,1)}, u32[]{:S(2)}, u32[]{:S(2)}) collective-permute-start(bf16[64,4096]{1,0:T(8,128)(2,1)} %get-tuple-element.19), channel_id=1, source_target_pairs={{2,0},{0,2},{3,1},{1,3},{6,4},{4,6},{7,5},{5,7},{10,8},{8,10},{11,... | collective-permute-start | bytes 1572872 | tf_op jit(solution)/shard_map/ppermute | solution.py:190
  104.6 25.0 %all-to-all-start.5 = ((f32[32,2,128]{2,1,0:T(2,128)}), f32[32,2,128]{2,1,0:T(2,128)}, u32[]{:S(2)}, u32[]{:S(2)}) async-start(f32[32,2,128]{2,1,0:T(2,128)} %broadcast_in_dim.15), calls=%async_computation.5 | async-start | bytes 65536 | tf_op jit(solution)/shard_map/all_to_all | solution.py:242
  113.0 14.6 %copy-start.2 = (bf16[64,4096]{1,0:T(8,128)(2,1)S(1)}, bf16[64,4096]{1,0:T(8,128)(2,1)}, u32[]{:S(2)}) copy-start(bf16[64,4096]{1,0:T(8,128)(2,1)} %copy-done.1) | copy-start | bytes 1572868
  123.3 0.8 copy-start.3
  124.1 13.3 %copy-start.4 = (bf16[64,4096]{1,0:T(8,128)(2,1)S(1)}, bf16[64,4096]{1,0:T(8,128)(2,1)}, u32[]{:S(2)}) copy-start(bf16[64,4096]{1,0:T(8,128)(2,1)} %copy-done.3) | copy-start | bytes 1572868
  124.1 13.3 %collective-permute-start.7 = (bf16[64,4096]{1,0:T(8,128)(2,1)}, bf16[64,4096]{1,0:T(8,128)(2,1)S(1)}, u32[]{:S(2)}, u32[]{:S(2)}) collective-permute-start(bf16[64,4096]{1,0:T(8,128)(2,1)} %get-tuple-element.26), channel_id=1, source_target_pairs={{2,0},{0,2},{3,1},{1,3},{6,4},{4,6},{7,5},{5,7},{10,8},{8,10},{11,... | collective-permute-start | bytes 1572872 | tf_op jit(solution)/shard_map/ppermute | solution.py:190
  127.6 27.6 %copy-start.13 = (bf16[64,16]{1,0:T(8,128)(2,1)S(1)}, bf16[64,16]{1,0:T(8,128)(2,1)}, u32[]{:S(2)}) copy-start(bf16[64,16]{1,0:T(8,128)(2,1)} %copy-done.12) | copy-start | bytes 6148
  127.6 27.6 %copy-start.17 = (f32[16,128]{1,0:T(8,128)S(1)}, f32[16,128]{1,0:T(8,128)}, u32[]{:S(2)}) copy-start(f32[16,128]{1,0:T(8,128)} %copy-done.16) | copy-start | bytes 24580
  129.6 20.8 %all-to-all-start.1 = ((bf16[8,8,4096]{2,1,0:T(8,128)(2,1)}), bf16[8,8,4096]{2,1,0:T(8,128)(2,1)S(1)}, u32[]{:S(2)}, u32[]{:S(2)}) async-start(bf16[8,8,4096]{2,1,0:T(8,128)(2,1)} %fusion), calls=%async_computation.1 | async-start | bytes 1048576 | tf_op jit(solution)/shard_map/all_to_all | solution.py:194
  137.1 30.0 %copy-start.11 = (bf16[64,16]{1,0:T(8,128)(2,1)S(1)}, bf16[64,16]{1,0:T(8,128)(2,1)}, u32[]{:S(2)}) copy-start(bf16[64,16]{1,0:T(8,128)(2,1)} %copy-done.10) | copy-start | bytes 6148
  137.1 30.0 %copy-start.15 = (f32[16,128]{1,0:T(8,128)S(1)}, f32[16,128]{1,0:T(8,128)}, u32[]{:S(2)}) copy-start(f32[16,128]{1,0:T(8,128)} %copy-done.14) | copy-start | bytes 24580
  150.4 16.7 %all-to-all-start.4 = ((bf16[8,8,4096]{2,1,0:T(8,128)(2,1)}), bf16[8,8,4096]{2,1,0:T(8,128)(2,1)S(1)}, u32[]{:S(2)}, u32[]{:S(2)}) async-start(bf16[8,8,4096]{2,1,0:T(8,128)(2,1)} %fusion.1), calls=%async_computation.4 | async-start | bytes 1048576 | tf_op jit(solution)/shard_map/all_to_all | solution.py:194

commit v2 on v1

v2 whole, which is shorter than its diff:
```python
import jax
import jax.numpy as jnp
from jax import lax
from jax.experimental import pallas as pl
from jax.experimental.pallas import tpu as pltpu
from jax.sharding import Mesh, PartitionSpec as P

EXPERTS = 128
TOPK = 8
EXP_WIN = 2
CAP = 8
SLOTS = EXP_WIN * CAP
EPS = 1e-06
exact = lax.Precision.HIGHEST
f32 = jnp.float32
bf16 = jnp.bfloat16
NT = (((1,), (1,)), ((), ()))
PARAMS = pltpu.CompilerParams(vmem_limit_bytes=48 << 20)
EXPERT_AXES = ("y", "xl", "core")


def shape(dims, dtype):
    return jax.ShapeDtypeStruct(dims, dtype)


def iota(dims, axis):
    return lax.broadcasted_iota(jnp.int32, dims, axis)


def slot_tables(routes_t, logits):
    tokens, experts = logits.shape
    ids = iota((experts, tokens), 0)
    hot_t = jnp.zeros((experts, tokens), f32)
    for k in range(TOPK):
        hot_t = hot_t + jnp.where(ids == routes_t[k : k + 1, :], 1.0, 0.0)
    rows, cols = iota((tokens, tokens), 0), iota((tokens, tokens), 1)
    eye = jnp.where(rows == cols, 1.0, 0.0).astype(bf16)
    hot = lax.dot_general(eye, hot_t.astype(bf16), NT, preferred_element_type=f32)
    chosen = jnp.where(hot > 0.5, logits, -jnp.inf)
    powers = jnp.exp(chosen - jnp.max(chosen, axis=1, keepdims=True))
    gates = powers / jnp.sum(powers, axis=1, keepdims=True)
    before = jnp.where(rows < cols, 1.0, 0.0).astype(bf16)
    first = hot_t[0:8, :]
    earlier = jnp.dot(first.astype(bf16), before, preferred_element_type=f32)
    slot = iota((CAP, tokens), 0).astype(f32)
    select = jnp.concatenate(
        [
            jnp.where((earlier[e : e + 1, :] == slot) & (first[e : e + 1, :] > 0.5), 1.0, 0.0)
            for e in range(EXP_WIN)
        ],
        axis=0,
    )
    select_t = lax.dot_general(eye, select.astype(bf16), NT, preferred_element_type=f32)
    picked = jnp.dot(select, gates, precision=exact, preferred_element_type=f32)
    own = iota((SLOTS, experts), 1) == iota((SLOTS, experts), 0) // CAP
    gate_slot = jnp.sum(jnp.where(own, picked, 0.0), axis=1, keepdims=True)
    return hot, select.astype(bf16), select_t.astype(bf16), gate_slot


HBM = pl.BlockSpec(memory_space=pltpu.HBM)
VMEM = pl.BlockSpec(memory_space=pltpu.VMEM)


def in_hbm(dims, dtype):
    return pltpu.HBM(dims, dtype)


def kernel_call(body, outs, in_specs, out_specs, scratch, *args):
    args = [
        pltpu.with_memory_space_constraint(v, pltpu.HBM) if spec is HBM else v
        for v, spec in zip(args, in_specs)
    ]
    return pl.pallas_call(
        body, out_shape=outs, in_specs=in_specs, out_specs=out_specs, scratch_shapes=scratch,
        compiler_params=PARAMS,
    )(*args)


def started(sems, *pairs):
    copies = [pltpu.make_async_copy(src, dst, sems.at[i]) for i, (src, dst) in enumerate(pairs)]
    for copy in copies:
        copy.start()
    return copies


def wait_all(copies):
    for copy in copies:
        copy.wait()


def normed_rows(rows, gain):
    inverse = lax.rsqrt(jnp.mean(rows * rows, axis=1, keepdims=True) + EPS)
    return (rows * inverse * gain).astype(bf16), inverse


def by_expert(stops):
    return [(i, i * EXP_WIN // stops * CAP) for i in range(stops)]


def prepare_body(
    saved_h, gain_h, broutes_h, blogits_h, froutes_h, flogits_h,
    send, picked, columns, rows16, usage,
    saved, gain, broutes, blogits, froutes, flogits, sems,
):
    copies = started(
        sems, (broutes_h, broutes), (blogits_h, blogits), (froutes_h, froutes),
        (flogits_h, flogits), (gain_h, gain), (saved_h, saved),
    )
    wait_all(copies[:4])
    _, select, bselect_t, bgate = slot_tables(broutes[...], blogits[...])
    logits = flogits[...]
    hot, _, fselect_t, fgate = slot_tables(froutes[...], logits)
    powers = jnp.exp(logits - jnp.max(logits, axis=1, keepdims=True))
    probs = powers / jnp.sum(powers, axis=1, keepdims=True)
    usage[...] = jnp.concatenate(
        [jnp.sum(hot, axis=0, keepdims=True), jnp.sum(probs, axis=0, keepdims=True)], axis=0
    )
    wait_all(copies[4:])
    rows = jnp.dot(select, saved[...], preferred_element_type=f32)
    normed, inverse = normed_rows(rows, gain[...].astype(f32))
    picked[...] = rows.astype(bf16)
    columns[0, :, :] = bselect_t
    columns[1, :, :] = fselect_t
    wide = (SLOTS, EXPERTS)
    rows16[0, :, :] = jnp.broadcast_to(bgate, wide)
    rows16[1, :, :] = jnp.broadcast_to(fgate, wide)
    rows16[2, :, :] = jnp.broadcast_to(inverse, wide)
    for i, r in by_expert(send.shape[0]):
        send[i, :, :] = normed[r : r + CAP, :]


def rows_body(x_in, upstream, columns_h, rows16_h, gain_h, send, columns, gates, gain, sems):
    copies = started(sems, (columns_h, columns), (rows16_h.at[0], gates), (gain_h, gain))
    copies[0].wait()

    def chosen(i, block):
        return lax.dot_general(
            columns[i, :, :], block[...], (((0,), (0,)), ((), ())), preferred_element_type=f32
        )

    rows = chosen(1, x_in)
    grads = chosen(0, upstream)
    wait_all(copies[1:])
    normed = normed_rows(rows, gain[...].astype(f32))[0]
    grads = (grads * gates[:, 0:1]).astype(bf16)
    for i, r in by_expert(send.shape[0]):
        send[i, 0:CAP, :] = normed[r : r + CAP, :]
        send[i, CAP : 2 * CAP, :] = grads[r : r + CAP, :]


COLS = 512


def nt(a, b):
    return lax.dot_general(a, b, NT, preferred_element_type=f32)


def hidden_terms(saved, mixed, slab):
    hid = slab.shape[0] // 3
    kept = nt(saved, slab[0 : 2 * hid, :])
    pre = nt(mixed, slab[...]).reshape(-1, 2 * CAP, 3 * hid)
    forward, grads = pre[:, 0:CAP, :], pre[:, CAP:, :]
    h = jax.nn.silu(forward[:, :, :hid]) * forward[:, :, hid : 2 * hid]
    kept = kept.reshape(-1, CAP, 2 * hid)
    a, b, d_hidden = kept[:, :, :hid], kept[:, :, hid:], grads[:, :, 2 * hid :]
    sigma = jax.nn.sigmoid(a)
    d_gate = d_hidden * b * sigma * (1.0 + a * (1.0 - sigma))
    d_up = d_hidden * a * sigma
    none = jnp.zeros_like(h)
    top = jnp.concatenate([none, none, h], axis=2)
    low = jnp.concatenate([d_gate, d_up, none], axis=2)
    return jnp.concatenate([top, low], axis=1).reshape(-1, 3 * hid).astype(bf16)


def expert_first_body(saved_h, mixed_h, slab_h, slab2_h, out, saved, mixed, slab, slab2, sems):
    copies = started(
        sems, (saved_h, saved), (mixed_h, mixed), (slab_h, slab), (slab2_h, slab2)
    )
    wait_all(copies[:3])
    left = hidden_terms(saved[...], mixed[...], slab)
    copies[3].wait()
    left2 = hidden_terms(saved[...], mixed[...], slab2)
    for c in range(0, out.shape[1], COLS):
        cut = slice(c, c + COLS)
        part = jnp.dot(left, slab[:, cut], preferred_element_type=f32)
        out[:, cut] = part + jnp.dot(left2, slab2[:, cut], preferred_element_type=f32)


def expert_second_body(
    saved_h, mixed_h, slab_h, slab2_h, part_h, out, saved, mixed, slab, slab2, first, sems
):
    copies = started(
        sems, (saved_h, saved), (mixed_h, mixed), (slab_h, slab), (slab2_h, slab2), (part_h, first)
    )
    wait_all(copies[:3])
    left = hidden_terms(saved[...], mixed[...], slab)
    wait_all(copies[3:])
    left2 = hidden_terms(saved[...], mixed[...], slab2)
    for c in range(0, out.shape[1], COLS):
        cut = slice(c, c + COLS)
        part = first[:, cut] + jnp.dot(left, slab[:, cut], preferred_element_type=f32)
        part = part + jnp.dot(left2, slab2[:, cut], preferred_element_type=f32)
        out[:, cut] = part.astype(bf16)


def placed(select_t, rows):
    high = rows.astype(bf16)
    rest = rows - high.astype(f32)
    mid = rest.astype(bf16)
    low = (rest - mid.astype(f32)).astype(bf16)
    return sum(jnp.dot(select_t, p, preferred_element_type=f32) for p in (low, mid, high))


def combine_body(
    parts, columns_h, rows16_h, picked_h, gain_h, x_in, upstream, fwd_out, bwd_out,
    columns, rows16, picked, gain, sems,
):
    wait_all(
        started(
            sems, (columns_h, columns), (rows16_h, rows16), (picked_h, picked), (gain_h, gain)
        )
    )
    half = parts.shape[0] // EXP_WIN

    def summed(start):
        return jnp.concatenate(
            [
                sum(
                    parts[e * half + i, start : start + CAP, :].astype(f32) for i in range(half)
                )
                for e in range(EXP_WIN)
            ],
            axis=0,
        )

    rows = summed(0) * rows16[1, :, 0:1]
    fwd_out[...] = (x_in[...].astype(f32) + placed(columns[1, :, :], rows)).astype(bf16)
    weighted = gain[...].astype(f32) * summed(CAP)
    inv = rows16[2, :, 0:1]
    x = picked[...].astype(f32)
    rows = inv * weighted - x * (inv * inv * inv) * jnp.mean(x * weighted, axis=1, keepdims=True)
    bwd_out[...] = (upstream[...].astype(f32) + placed(columns[0, :, :], rows)).astype(bf16)


def shifted(block, axis, distance):
    n = lax.axis_size(axis)
    return lax.ppermute(block, axis, [((i - distance) % n, i) for i in range(n)])


def over_y(block):
    return lax.all_to_all(block, "y", split_axis=0, concat_axis=0, tiled=True)


def body(
    fwd_sent, bwd_sent, bwd_saved, fwd_routes, bwd_routes, fwd_logits, bwd_logits,
    norm_gain, w_gate, w_up, w_down,
):
    stops = lax.axis_size("y")
    tokens, width = fwd_sent.shape[1:]
    dma = pltpu.SemaphoreType.DMA
    upstream = shifted(bwd_sent[0], "section", -1)
    x_in = shifted(fwd_sent[0], "section", 1)
    slab = jnp.concatenate([w_gate[0].T, w_up[0].T, w_down[0]], axis=0)
    slab_core = shifted(slab, "core", 1)
    slab_x = shifted(slab, "xl", 1)
    saved_send, picked, columns, rows16, usage = kernel_call(
        prepare_body,
        (in_hbm((stops, CAP, width), bf16), in_hbm((SLOTS, width), bf16),
         in_hbm((EXP_WIN, tokens, SLOTS), bf16), in_hbm((3, SLOTS, EXPERTS), f32),
         in_hbm((2, EXPERTS), f32)),
        [HBM] * 6, [VMEM] * 5,
        [pltpu.VMEM((tokens, width), bf16), pltpu.VMEM((1, width), bf16),
         pltpu.VMEM((TOPK, tokens), jnp.int32), pltpu.VMEM((tokens, EXPERTS), f32),
         pltpu.VMEM((TOPK, tokens), jnp.int32), pltpu.VMEM((tokens, EXPERTS), f32), dma((6,))],
        bwd_saved[0], norm_gain, bwd_routes[0].T, bwd_logits[0], fwd_routes[0].T, fwd_logits[0],
    )
    devices = lax.axis_size(EXPERT_AXES)
    shared = lax.all_to_all(
        jnp.broadcast_to(usage[None], (devices, 2, EXPERTS)),
        EXPERT_AXES, split_axis=0, concat_axis=0, tiled=True,
    )
    saved_send, shared = lax.optimization_barrier((saved_send, shared))
    saved_all = over_y(saved_send).reshape(-1, width)
    mixed_send = kernel_call(
        rows_body, in_hbm((stops, 2 * CAP, width), bf16), [VMEM, VMEM, HBM, HBM, HBM], VMEM,
        [pltpu.VMEM((EXP_WIN, tokens, SLOTS), bf16), pltpu.VMEM((SLOTS, EXPERTS), f32),
         pltpu.VMEM((1, width), bf16), dma((3,))],
        x_in, upstream, columns, rows16, norm_gain,
    )
    mixed_all = over_y(mixed_send).reshape(-1, width)
    loads = [pltpu.VMEM(v.shape, bf16) for v in (saved_all, mixed_all, slab, slab)]
    first = kernel_call(
        expert_first_body, in_hbm(mixed_all.shape, f32), [HBM] * 4, VMEM, loads + [dma((4,))],
        saved_all, mixed_all, slab, slab_core,
    )
    slab_x, first = lax.optimization_barrier((slab_x, first))
    slab_x_core = shifted(slab_x, "core", 1)
    result = kernel_call(
        expert_second_body, in_hbm(mixed_all.shape, bf16), [HBM] * 5, VMEM,
        loads + [pltpu.VMEM(first.shape, f32), dma((5,))],
        saved_all, mixed_all, slab_x, slab_x_core, first,
    )
    parts = over_y(result.reshape(stops, 2 * CAP, width))
    full = in_hbm((tokens, width), bf16)
    fwd_out, bwd_out = kernel_call(
        combine_body, (full, full), [VMEM] + [HBM] * 4 + [VMEM] * 2, [VMEM] * 2,
        [pltpu.VMEM(columns.shape, bf16),
         pltpu.VMEM(rows16.shape, f32), pltpu.VMEM(picked.shape, bf16),
         pltpu.VMEM((1, width), bf16), dma((4,))],
        parts, columns, rows16, picked, norm_gain, x_in, upstream,
    )
    counts, prob_sums = jnp.sum(shared, axis=0)
    tokens_all = tokens * devices
    balance = EXPERTS * (counts / (tokens_all * TOPK)) * (prob_sums / tokens_all)
    return (fwd_out[None], bwd_out[None], balance[None])


def solution(mesh):
    sections = mesh.shape["section"]
    grid = mesh.devices.reshape(sections, -1, 2, 2)
    inner = Mesh(grid, ("section",) + EXPERT_AXES)
    rows = P("section", EXPERT_AXES, None)
    return jax.shard_map(
        body,
        mesh=inner,
        in_specs=(
            rows, rows, rows, rows, rows, rows, rows,
            P("section", None),
            P("section", None, EXPERT_AXES),
            P("section", None, EXPERT_AXES),
            rows,
        ),
        out_specs=(rows, rows, P("section", None)),
        check_vma=False,
    )
```

time: 170 us -> 153 us (0.900)
  the two profiles are of different devices: /device:TPU:2 before, /device:TPU:1 now
where the time goes in v2:
time: 153 us; the launch traced here: 152 us
  starting transfers between devices  46 us (30%)
  waiting for transfers between devices  42.1 us (28%)
  blocking collectives  33.2 us (22%)
  Pallas kernels  23.6 us (15%)
  other arithmetic  3.82 us (2%)
  local copies, waits for them, and re-layouts  2.64 us (2%)
    all_to_all x2, waiting for transfers between devices, over_y(): return lax.all_to_all(block, 'y', split_axis=0, concat_axis=0, tiled=True)  33.6 us
    all_to_all x1, blocking collectives, over_y(): return lax.all_to_all(block, 'y', split_axis=0, concat_axis=0, tiled=True)  33.2 us
    pallas_call x5, Pallas kernels, kernel_call(): pl.pallas_call(body, out_shape=outs, in_specs=in_specs, out_specs=out_spe...  23.6 us
    ppermute x5, starting transfers between devices, shifted(): lax.ppermute(block, axis, [((i - distance) % n, i) for i in range(n)])  22.1 us
    all_to_all x2, starting transfers between devices, over_y(): return lax.all_to_all(block, 'y', split_axis=0, concat_axis=0, tiled=True)  13.5 us
    all_to_all x1, starting transfers between devices, body(): lax.all_to_all(jnp.broadcast_to(usage[None], (devices, 2, EXPERTS)), EXPE...  10.4 us
    ppermute x5, waiting for transfers between devices, shifted(): lax.ppermute(block, axis, [((i - distance) % n, i) for i in range(n)])  8.52 us
    concatenate x1, other arithmetic, body(): slab = jnp.concatenate([w_gate[0].T, w_up[0].T, w_down[0]], axis=0)  3.26 us
  transfers between devices with their start and end apart: 8, of which 5 were waited for; matrix products, arithmetic and copies ran while one was open for 3% of the time, Pallas kernels for 7%

profile of v2, /device:TPU:1, one launch (start us, length us, event | category | flops | bytes accessed | tf_op | source)
XLA Modules:
  0.0 152.0 jit_solution(11127418440088681833)
XLA Ops:
  0.6 2.8 %shard_map.130 = (bf16[8,8,4096]{2,1,0:T(8,128)(2,1)}, bf16[16,4096]{1,0:T(8,128)(2,1)}, bf16[2,64,16]{2,1,0:T(8,128)(2,1)}, f32[3,16,128]{2,1,0:T(8,128)}, f32[2,128]{1,0:T(2,128)}) custom-call(bf16[64,4096]{1,0:T(8,128)(2,1)} %bitcast.31, bf16[1,4096]{1,0:T(2,128)(2,1)} %gain_h.5, s32[8,64]{1,0:T(8,128)} %bitcast.34, f32[64,128]{1,0:T(8,128)} %bitcast.32, ...), custom_call_target="tpu_custom_call" | custom-call | tf_op jit(solution)/shard_map/pallas_call | solution.py:73
  3.4 1.2 broadcast_in_dim.6
  4.7 10.4 %all-to-all-start = ((f32[32,2,128]{2,1,0:T(2,128)}), f32[32,2,128]{2,1,0:T(2,128)S(1)}, u32[]{:S(2)}, u32[]{:S(2)}) async-start(f32[32,2,128]{2,1,0:T(2,128)} %broadcast_in_dim.6), calls=%async_computation | async-start | bytes 65536 | tf_op jit(solution)/shard_map/all_to_all | solution.py:278
  15.0 3.7 %collective-permute-start = (bf16[64,4096]{1,0:T(8,128)(2,1)}, bf16[64,4096]{1,0:T(8,128)(2,1)S(1)}, u32[]{:S(2)}, u32[]{:S(2)}) collective-permute-start(bf16[64,4096]{1,0:T(8,128)(2,1)} %bitcast.36), channel_id=1, source_target_pairs={{480,0},{0,32},{32,64},{64,96},{96,128},{128,160},{160,192},{192,2... | collective-permute-start | bytes 1572872 | tf_op jit(solution)/shard_map/ppermute | solution.py:247
  18.7 10.4 %collective-permute-start.1 = (bf16[64,4096]{1,0:T(8,128)(2,1)}, bf16[64,4096]{1,0:T(8,128)(2,1)S(1)}, u32[]{:S(2)}, u32[]{:S(2)}) collective-permute-start(bf16[64,4096]{1,0:T(8,128)(2,1)} %bitcast.37), channel_id=1, source_target_pairs={{32,0},{64,32},{96,64},{128,96},{160,128},{192,160},{224,192},{256... | collective-permute-start | bytes 1572872 | tf_op jit(solution)/shard_map/ppermute | solution.py:247
  29.1 0.0 all-to-all-done
  29.1 6.6 %all-to-all-start.1 = ((bf16[8,8,4096]{2,1,0:T(8,128)(2,1)}), bf16[8,8,4096]{2,1,0:T(8,128)(2,1)S(1)}, u32[]{:S(2)}, u32[]{:S(2)}) async-start(bf16[8,8,4096]{2,1,0:T(8,128)(2,1)} %get-tuple-element.16), calls=%async_computation.1 | async-start | bytes 1048576 | tf_op jit(solution)/shard_map/all_to_all | solution.py:251
  35.7 3.3 %pad_maximum_fusion.slab_h = bf16[288,4096]{1,0:T(8,128)(2,1)} fusion(bf16[96,4096]{1,0:T(8,128)(2,1)} %bitcast.28, bf16[96,4096]{1,0:T(8,128)(2,1)} %bitcast.29, bf16[96,4096]{1,0:T(8,128)(2,1)} %bitcast.30), kind=kLoop, calls=%fused_computation | loop fusion | flops 7077888 | bytes 4718592 | tf_op jit(solution)/shard_map/concatenate | solution.py:263
  39.0 2.8 %collective-permute-start.3 = (bf16[288,4096]{1,0:T(8,128)(2,1)}, bf16[288,4096]{1,0:T(8,128)(2,1)}, u32[]{:S(2)}, u32[]{:S(2)}) collective-permute-start(bf16[288,4096]{1,0:T(8,128)(2,1)} %pad_maximum_fusion.slab_h), channel_id=1, source_target_pairs={{1,0},{0,1},{3,2},{2,3},{5,4},{4,5},{7,6},{6,7},{9,8},{8,9},{11,10... | collective-permute-start | bytes 7077896 | tf_op jit(solution)/shard_map/ppermute | solution.py:247
  41.8 2.5 %collective-permute-start.2 = (bf16[288,4096]{1,0:T(8,128)(2,1)}, bf16[288,4096]{1,0:T(8,128)(2,1)}, u32[]{:S(2)}, u32[]{:S(2)}) collective-permute-start(bf16[288,4096]{1,0:T(8,128)(2,1)} %pad_maximum_fusion.slab_h), channel_id=1, source_target_pairs={{2,0},{0,2},{3,1},{1,3},{6,4},{4,6},{7,5},{5,7},{10,8},{8,10},{11,... | collective-permute-start | bytes 7077896 | tf_op jit(solution)/shard_map/ppermute | solution.py:247
  44.3 0.0 collective-permute-done.x_in
  44.3 2.2 %collective-permute-done.1.upstream = bf16[64,4096]{1,0:T(8,128)(2,1)S(1)} collective-permute-done((bf16[64,4096]{1,0:T(8,128)(2,1)}, bf16[64,4096]{1,0:T(8,128)(2,1)S(1)}, u32[]{:S(2)}, u32[]{:S(2)}) %collective-permute-start.1) | collective-permute-done | bytes 524320 | tf_op jit(solution)/shard_map/ppermute | solution.py:247
  46.5 2.2 %shard_map.131 = bf16[8,16,4096]{2,1,0:T(8,128)(2,1)} custom-call(bf16[64,4096]{1,0:T(8,128)(2,1)S(1)} %collective-permute-done.x_in, bf16[64,4096]{1,0:T(8,128)(2,1)S(1)} %collective-permute-done.1.upstream, bf16[2,64,16]{2,1,0:T(8,128)(2,1)} %get-tuple-element.17.columns_h, f32[3,16,128]{2,1,0:T(8,128)} %get-tuple-element.18.rows16_h, bf16[1,4096]{1,0:T(2,128)(2,1)} %gain_h.5), custom_call_target="tpu_custom_call" | custom-call | tf_op jit(solution)/shard_map/pallas_call | solution.py:73
  48.8 4.9 %all-to-all-done.1 = bf16[8,8,4096]{2,1,0:T(8,128)(2,1)S(1)} async-done(((bf16[8,8,4096]{2,1,0:T(8,128)(2,1)}), bf16[8,8,4096]{2,1,0:T(8,128)(2,1)S(1)}, u32[]{:S(2)}, u32[]{:S(2)}) %all-to-all-start.1) | async-done | bytes 524320 | tf_op jit(solution)/shard_map/all_to_all | solution.py:251
  53.7 0.0 copy-start
  53.7 33.2 %all_to_all.20 = bf16[8,16,4096]{2,1,0:T(8,128)(2,1)} all-to-all(bf16[8,16,4096]{2,1,0:T(8,128)(2,1)} %shard_map.131), channel_id=1, replica_groups=mesh['section'=16,'y'=8,'xl'=2,'core'=2] {'y'}, dimensions={0} | all-to-all | bytes 2097152 | tf_op jit(solution)/shard_map/all_to_all | solution.py:251
  86.9 0.0 collective-permute-done.3.slab2_h
  86.9 0.0 copy-done
  86.9 8.1 %shard_map.132.part_h = f32[128,4096]{1,0:T(8,128)} custom-call(bf16[64,4096]{1,0:T(8,128)(2,1)} %bitcast.25, bf16[128,4096]{1,0:T(8,128)(2,1)} %bitcast.23, bf16[288,4096]{1,0:T(8,128)(2,1)} %pad_maximum_fusion.slab_h, bf16[288,4096]{1,0:T(8,128)(2,1)} %collective-permute-done.3.slab2_h), custom_call_target="tpu_custom_call" | custom-call | tf_op jit(solution)/shard_map/pallas_call | solution.py:73
  94.9 1.9 %collective-permute-done.2.slab_h = bf16[288,4096]{1,0:T(8,128)(2,1)} collective-permute-done((bf16[288,4096]{1,0:T(8,128)(2,1)}, bf16[288,4096]{1,0:T(8,128)(2,1)}, u32[]{:S(2)}, u32[]{:S(2)}) %collective-permute-start.2) | collective-permute-done | bytes 2359328 | tf_op jit(solution)/shard_map/ppermute | solution.py:247
  96.9 2.7 %collective-permute-start.4 = (bf16[288,4096]{1,0:T(8,128)(2,1)}, bf16[288,4096]{1,0:T(8,128)(2,1)S(1)}, u32[]{:S(2)}, u32[]{:S(2)}) collective-permute-start(bf16[288,4096]{1,0:T(8,128)(2,1)} %collective-permute-done.2.slab_h), channel_id=1, source_target_pairs={{1,0},{0,1},{3,2},{2,3},{5,4},{4,5},{7,6},{6,7},{9,8},{8,9},{11,10... | collective-permute-start | bytes 7077896 | tf_op jit(solution)/shard_map/ppermute | solution.py:247
  99.6 4.3 %collective-permute-done.4.slab2_h = bf16[288,4096]{1,0:T(8,128)(2,1)S(1)} collective-permute-done((bf16[288,4096]{1,0:T(8,128)(2,1)}, bf16[288,4096]{1,0:T(8,128)(2,1)S(1)}, u32[]{:S(2)}, u32[]{:S(2)}) %collective-permute-start.4) | collective-permute-done | bytes 2359328 | tf_op jit(solution)/shard_map/ppermute | solution.py:247
  103.9 0.0 copy-start.1
  103.9 1.4 copy-done.1
  105.3 7.6 %shard_map.133 = bf16[128,4096]{1,0:T(8,128)(2,1)} custom-call(bf16[64,4096]{1,0:T(8,128)(2,1)} %bitcast.26, bf16[128,4096]{1,0:T(8,128)(2,1)} %bitcast.24, bf16[288,4096]{1,0:T(8,128)(2,1)} %collective-permute-done.2.slab_h, bf16[288,4096]{1,0:T(8,128)(2,1)} %copy-done.1, f32[128,4096]{1,0:T(8,128)} %shard_map.132.part_h), custom_call_target="tpu_custom_call" | custom-call | tf_op jit(solution)/shard_map/pallas_call | solution.py:73
  113.0 6.9 %all-to-all-start.3 = ((bf16[8,16,4096]{2,1,0:T(8,128)(2,1)}), bf16[8,16,4096]{2,1,0:T(8,128)(2,1)S(1)}, u32[]{:S(2)}, u32[]{:S(2)}) async-start(bf16[8,16,4096]{2,1,0:T(8,128)(2,1)} %bitcast.27), calls=%async_computation.3 | async-start | bytes 2097152 | tf_op jit(solution)/shard_map/all_to_all | solution.py:251
  120.0 0.5 multiply_multiply_fusion
  120.5 28.7 %all-to-all-done.3.parts = bf16[8,16,4096]{2,1,0:T(8,128)(2,1)S(1)} async-done(((bf16[8,16,4096]{2,1,0:T(8,128)(2,1)}), bf16[8,16,4096]{2,1,0:T(8,128)(2,1)S(1)}, u32[]{:S(2)}, u32[]{:S(2)}) %all-to-all-start.3) | async-done | bytes 1048608 | tf_op jit(solution)/shard_map/all_to_all | solution.py:251
  149.2 2.9 %shard_map.134 = (bf16[64,4096]{1,0:T(8,128)(2,1)}, bf16[64,4096]{1,0:T(8,128)(2,1)}) custom-call(bf16[8,16,4096]{2,1,0:T(8,128)(2,1)S(1)} %all-to-all-done.3.parts, bf16[2,64,16]{2,1,0:T(8,128)(2,1)} %get-tuple-element.17.columns_h, f32[3,16,128]{2,1,0:T(8,128)} %get-tuple-element.18.rows16_h, bf16[16,4096]{1,0:T(8,128)(2,1)} %get-tuple-element.21.picked_h, ...), custom_call_target="tpu_custom_call" | custom-call | tf_op jit(solution)/shard_map/pallas_call | solution.py:73
  (1 shorter events, 0.0 us)
Async XLA Ops:
  4.7 24.5 %all-to-all-start = ((f32[32,2,128]{2,1,0:T(2,128)}), f32[32,2,128]{2,1,0:T(2,128)S(1)}, u32[]{:S(2)}, u32[]{:S(2)}) async-start(f32[32,2,128]{2,1,0:T(2,128)} %broadcast_in_dim.6), calls=%async_computation | async-start | bytes 65536 | tf_op jit(solution)/shard_map/all_to_all | solution.py:278
  15.0 29.3 %collective-permute-start = (bf16[64,4096]{1,0:T(8,128)(2,1)}, bf16[64,4096]{1,0:T(8,128)(2,1)S(1)}, u32[]{:S(2)}, u32[]{:S(2)}) collective-permute-start(bf16[64,4096]{1,0:T(8,128)(2,1)} %bitcast.36), channel_id=1, source_target_pairs={{480,0},{0,32},{32,64},{64,96},{96,128},{128,160},{160,192},{192,2... | collective-permute-start | bytes 1572872 | tf_op jit(solution)/shard_map/ppermute | solution.py:247
  18.7 27.8 %collective-permute-start.1 = (bf16[64,4096]{1,0:T(8,128)(2,1)}, bf16[64,4096]{1,0:T(8,128)(2,1)S(1)}, u32[]{:S(2)}, u32[]{:S(2)}) collective-permute-start(bf16[64,4096]{1,0:T(8,128)(2,1)} %bitcast.37), channel_id=1, source_target_pairs={{32,0},{64,32},{96,64},{128,96},{160,128},{192,160},{224,192},{256... | collective-permute-start | bytes 1572872 | tf_op jit(solution)/shard_map/ppermute | solution.py:247
  29.1 24.5 %all-to-all-start.1 = ((bf16[8,8,4096]{2,1,0:T(8,128)(2,1)}), bf16[8,8,4096]{2,1,0:T(8,128)(2,1)S(1)}, u32[]{:S(2)}, u32[]{:S(2)}) async-start(bf16[8,8,4096]{2,1,0:T(8,128)(2,1)} %get-tuple-element.16), calls=%async_computation.1 | async-start | bytes 1048576 | tf_op jit(solution)/shard_map/all_to_all | solution.py:251
  39.0 47.9 %collective-permute-start.3 = (bf16[288,4096]{1,0:T(8,128)(2,1)}, bf16[288,4096]{1,0:T(8,128)(2,1)}, u32[]{:S(2)}, u32[]{:S(2)}) collective-permute-start(bf16[288,4096]{1,0:T(8,128)(2,1)} %pad_maximum_fusion.slab_h), channel_id=1, source_target_pairs={{1,0},{0,1},{3,2},{2,3},{5,4},{4,5},{7,6},{6,7},{9,8},{8,9},{11,10... | collective-permute-start | bytes 7077896 | tf_op jit(solution)/shard_map/ppermute | solution.py:247
  41.8 55.1 %collective-permute-start.2 = (bf16[288,4096]{1,0:T(8,128)(2,1)}, bf16[288,4096]{1,0:T(8,128)(2,1)}, u32[]{:S(2)}, u32[]{:S(2)}) collective-permute-start(bf16[288,4096]{1,0:T(8,128)(2,1)} %pad_maximum_fusion.slab_h), channel_id=1, source_target_pairs={{2,0},{0,2},{3,1},{1,3},{6,4},{4,6},{7,5},{5,7},{10,8},{8,10},{11,... | collective-permute-start | bytes 7077896 | tf_op jit(solution)/shard_map/ppermute | solution.py:247
  53.7 33.2 %copy-start = (bf16[8,8,4096]{2,1,0:T(8,128)(2,1)}, bf16[8,8,4096]{2,1,0:T(8,128)(2,1)S(1)}, u32[]{:S(2)}) copy-start(bf16[8,8,4096]{2,1,0:T(8,128)(2,1)S(1)} %all-to-all-done.1) | copy-start | bytes 1572868
  96.9 7.0 %collective-permute-start.4 = (bf16[288,4096]{1,0:T(8,128)(2,1)}, bf16[288,4096]{1,0:T(8,128)(2,1)S(1)}, u32[]{:S(2)}, u32[]{:S(2)}) collective-permute-start(bf16[288,4096]{1,0:T(8,128)(2,1)} %collective-permute-done.2.slab_h), channel_id=1, source_target_pairs={{1,0},{0,1},{3,2},{2,3},{5,4},{4,5},{7,6},{6,7},{9,8},{8,9},{11,10... | collective-permute-start | bytes 7077896 | tf_op jit(solution)/shard_map/ppermute | solution.py:247
  103.9 1.4 copy-start.1
  113.0 36.2 %all-to-all-start.3 = ((bf16[8,16,4096]{2,1,0:T(8,128)(2,1)}), bf16[8,16,4096]{2,1,0:T(8,128)(2,1)S(1)}, u32[]{:S(2)}, u32[]{:S(2)}) async-start(bf16[8,16,4096]{2,1,0:T(8,128)(2,1)} %bitcast.27), calls=%async_computation.3 | async-start | bytes 2097152 | tf_op jit(solution)/shard_map/all_to_all | solution.py:251

commit v3 on v2

--- a/solution.py
+++ b/solution.py
@@ -27,34 +27,43 @@
     return lax.broadcasted_iota(jnp.int32, dims, axis)
 
 
-def slot_tables(routes_t, logits):
-    tokens, experts = logits.shape
-    ids = iota((experts, tokens), 0)
-    hot_t = jnp.zeros((experts, tokens), f32)
+def hot_columns(routes_t, experts):
+    ids = iota((experts, routes_t.shape[1]), 0)
+    hot_t = jnp.zeros(ids.shape, f32)
     for k in range(TOPK):
         hot_t = hot_t + jnp.where(ids == routes_t[k : k + 1, :], 1.0, 0.0)
-    rows, cols = iota((tokens, tokens), 0), iota((tokens, tokens), 1)
-    eye = jnp.where(rows == cols, 1.0, 0.0).astype(bf16)
-    hot = lax.dot_general(eye, hot_t.astype(bf16), NT, preferred_element_type=f32)
-    chosen = jnp.where(hot > 0.5, logits, -jnp.inf)
-    powers = jnp.exp(chosen - jnp.max(chosen, axis=1, keepdims=True))
-    gates = powers / jnp.sum(powers, axis=1, keepdims=True)
-    before = jnp.where(rows < cols, 1.0, 0.0).astype(bf16)
+    return hot_t
+
+
+def selection(hot_t):
+    tokens = hot_t.shape[1]
     first = hot_t[0:8, :]
-    earlier = jnp.dot(first.astype(bf16), before, preferred_element_type=f32)
+    before = jnp.where(iota((tokens, tokens), 0) < iota((tokens, tokens), 1), 1.0, 0.0)
+    earlier = jnp.dot(first.astype(bf16), before.astype(bf16), preferred_element_type=f32)
     slot = iota((CAP, tokens), 0).astype(f32)
-    select = jnp.concatenate(
+    return jnp.concatenate(
         [
             jnp.where((earlier[e : e + 1, :] == slot) & (first[e : e + 1, :] > 0.5), 1.0, 0.0)
             for e in range(EXP_WIN)
         ],
         axis=0,
-    )
-    select_t = lax.dot_general(eye, select.astype(bf16), NT, preferred_element_type=f32)
-    picked = jnp.dot(select, gates, precision=exact, preferred_element_type=f32)
+    ).astype(bf16)
+
+
+def slot_tables(routes_t, logits):
+    tokens, experts = logits.shape
+    hot_t = hot_columns(routes_t, experts)
+    eye = jnp.where(iota((tokens, tokens), 0) == iota((tokens, tokens), 1), 1.0, 0.0).astype(bf16)
+    hot = lax.dot_general(eye, hot_t.astype(bf16), NT, preferred_element_type=f32)
+    chosen = jnp.where(hot > 0.5, logits, -jnp.inf)
+    powers = jnp.exp(chosen - jnp.max(chosen, axis=1, keepdims=True))
+    gates = powers / jnp.sum(powers, axis=1, keepdims=True)
+    select = selection(hot_t)
+    select_t = lax.dot_general(eye, select, NT, preferred_element_type=f32)
+    picked = jnp.dot(select.astype(f32), gates, precision=exact, preferred_element_type=f32)
     own = iota((SLOTS, experts), 1) == iota((SLOTS, experts), 0) // CAP
     gate_slot = jnp.sum(jnp.where(own, picked, 0.0), axis=1, keepdims=True)
-    return hot, select.astype(bf16), select_t.astype(bf16), gate_slot
+    return hot, select, select_t.astype(bf16), gate_slot
 
 
 HBM = pl.BlockSpec(memory_space=pltpu.HBM)
@@ -129,20 +138,23 @@
         send[i, :, :] = normed[r : r + CAP, :]
 
 
-def rows_body(x_in, upstream, columns_h, rows16_h, gain_h, send, columns, gates, gain, sems):
-    copies = started(sems, (columns_h, columns), (rows16_h.at[0], gates), (gain_h, gain))
-    copies[0].wait()
-
-    def chosen(i, block):
-        return lax.dot_general(
-            columns[i, :, :], block[...], (((0,), (0,)), ((), ())), preferred_element_type=f32
-        )
-
-    rows = chosen(1, x_in)
-    grads = chosen(0, upstream)
-    wait_all(copies[1:])
-    normed = normed_rows(rows, gain[...].astype(f32))[0]
-    grads = (grads * gates[:, 0:1]).astype(bf16)
+def pick_body(froutes_h, broutes_h, ahead_h, behind_h, fpicked, bpicked, froutes, broutes, ahead, behind, sems):
+    copies = started(
+        sems, (froutes_h, froutes), (broutes_h, broutes), (ahead_h, ahead), (behind_h, behind)
+    )
+    wait_all(copies[:2])
+    fselect = selection(hot_columns(froutes[...], EXPERTS))
+    bselect = selection(hot_columns(broutes[...], EXPERTS))
+    wait_all(copies[2:])
+    fpicked[...] = jnp.dot(fselect, ahead[...], preferred_element_type=f32).astype(bf16)
+    bpicked[...] = jnp.dot(bselect, behind[...], preferred_element_type=f32).astype(bf16)
+
+
+def rows_body(fpicked, bpicked, rows16_h, gain_h, send, gates, gain, sems):
+    copies = started(sems, (rows16_h.at[0], gates), (gain_h, gain))
+    wait_all(copies)
+    normed = normed_rows(fpicked[...].astype(f32), gain[...].astype(f32))[0]
+    grads = (bpicked[...].astype(f32) * gates[:, 0:1]).astype(bf16)
     for i, r in by_expert(send.shape[0]):
         send[i, 0:CAP, :] = normed[r : r + CAP, :]
         send[i, CAP : 2 * CAP, :] = grads[r : r + CAP, :]
@@ -187,15 +199,15 @@
 
 
 def expert_second_body(
-    saved_h, mixed_h, slab_h, slab2_h, part_h, out, saved, mixed, slab, slab2, first, sems
+    saved_h, mixed_h, slab_h, slab2, part_h, out, saved, mixed, slab, first, sems
 ):
     copies = started(
-        sems, (saved_h, saved), (mixed_h, mixed), (slab_h, slab), (slab2_h, slab2), (part_h, first)
+        sems, (saved_h, saved), (mixed_h, mixed), (slab_h, slab), (part_h, first)
     )
     wait_all(copies[:3])
     left = hidden_terms(saved[...], mixed[...], slab)
-    wait_all(copies[3:])
     left2 = hidden_terms(saved[...], mixed[...], slab2)
+    copies[3].wait()
     for c in range(0, out.shape[1], COLS):
         cut = slice(c, c + COLS)
         part = first[:, cut] + jnp.dot(left, slab[:, cut], preferred_element_type=f32)
@@ -247,6 +259,15 @@
     return lax.ppermute(block, axis, [((i - distance) % n, i) for i in range(n)])
 
 
+def summed_over(value, axes):
+    for axis in axes:
+        n, step = lax.axis_size(axis), 1
+        while step < n:
+            value = value + lax.ppermute(value, axis, [(i, i ^ step) for i in range(n)])
+            step *= 2
+    return value
+
+
 def over_y(block):
     return lax.all_to_all(block, "y", split_axis=0, concat_axis=0, tiled=True)
 
@@ -258,8 +279,9 @@
     stops = lax.axis_size("y")
     tokens, width = fwd_sent.shape[1:]
     dma = pltpu.SemaphoreType.DMA
-    upstream = shifted(bwd_sent[0], "section", -1)
-    x_in = shifted(fwd_sent[0], "section", 1)
+    fwd_routes_t, bwd_routes_t = fwd_routes[0].T, bwd_routes[0].T
+    froutes_next = shifted(fwd_routes_t, "section", -1)
+    broutes_last = shifted(bwd_routes_t, "section", 1)
     slab = jnp.concatenate([w_gate[0].T, w_up[0].T, w_down[0]], axis=0)
     slab_core = shifted(slab, "core", 1)
     slab_x = shifted(slab, "xl", 1)
@@ -272,20 +294,23 @@
         [pltpu.VMEM((tokens, width), bf16), pltpu.VMEM((1, width), bf16),
          pltpu.VMEM((TOPK, tokens), jnp.int32), pltpu.VMEM((tokens, EXPERTS), f32),
          pltpu.VMEM((TOPK, tokens), jnp.int32), pltpu.VMEM((tokens, EXPERTS), f32), dma((6,))],
-        bwd_saved[0], norm_gain, bwd_routes[0].T, bwd_logits[0], fwd_routes[0].T, fwd_logits[0],
-    )
-    devices = lax.axis_size(EXPERT_AXES)
-    shared = lax.all_to_all(
-        jnp.broadcast_to(usage[None], (devices, 2, EXPERTS)),
-        EXPERT_AXES, split_axis=0, concat_axis=0, tiled=True,
-    )
-    saved_send, shared = lax.optimization_barrier((saved_send, shared))
+        bwd_saved[0], norm_gain, bwd_routes_t, bwd_logits[0], fwd_routes_t, fwd_logits[0],
+    )
     saved_all = over_y(saved_send).reshape(-1, width)
+    routes_shape = pltpu.VMEM((TOPK, tokens), jnp.int32)
+    block = pltpu.VMEM((tokens, width), bf16)
+    slot_rows = in_hbm((SLOTS, width), bf16)
+    fpicked, bpicked = kernel_call(
+        pick_body, (slot_rows, slot_rows), [HBM] * 4, [VMEM] * 2,
+        [routes_shape, routes_shape, block, block, dma((4,))],
+        froutes_next, broutes_last, fwd_sent[0], bwd_sent[0],
+    )
+    fpicked = shifted(fpicked, "section", 1)
+    bpicked = shifted(bpicked, "section", -1)
     mixed_send = kernel_call(
-        rows_body, in_hbm((stops, 2 * CAP, width), bf16), [VMEM, VMEM, HBM, HBM, HBM], VMEM,
-        [pltpu.VMEM((EXP_WIN, tokens, SLOTS), bf16), pltpu.VMEM((SLOTS, EXPERTS), f32),
-         pltpu.VMEM((1, width), bf16), dma((3,))],
-        x_in, upstream, columns, rows16, norm_gain,
+        rows_body, in_hbm((stops, 2 * CAP, width), bf16), [VMEM, VMEM, HBM, HBM], VMEM,
+        [pltpu.VMEM((SLOTS, EXPERTS), f32), pltpu.VMEM((1, width), bf16), dma((2,))],
+        fpicked, bpicked, rows16, norm_gain,
     )
     mixed_all = over_y(mixed_send).reshape(-1, width)
     loads = [pltpu.VMEM(v.shape, bf16) for v in (saved_all, mixed_all, slab, slab)]
@@ -293,13 +318,18 @@
         expert_first_body, in_hbm(mixed_all.shape, f32), [HBM] * 4, VMEM, loads + [dma((4,))],
         saved_all, mixed_all, slab, slab_core,
     )
-    slab_x, first = lax.optimization_barrier((slab_x, first))
+    slab_x, first, fwd_block, bwd_block = lax.optimization_barrier(
+        (slab_x, first, fwd_sent[0], bwd_sent[0])
+    )
     slab_x_core = shifted(slab_x, "core", 1)
+    upstream = shifted(bwd_block, "section", -1)
+    x_in = shifted(fwd_block, "section", 1)
     result = kernel_call(
-        expert_second_body, in_hbm(mixed_all.shape, bf16), [HBM] * 5, VMEM,
-        loads + [pltpu.VMEM(first.shape, f32), dma((5,))],
+        expert_second_body, in_hbm(mixed_all.shape, bf16), [HBM, HBM, HBM, VMEM, HBM], VMEM,
+        loads[:3] + [pltpu.VMEM(first.shape, f32), dma((4,))],
         saved_all, mixed_all, slab_x, slab_x_core, first,
     )
+    result, usage = lax.optimization_barrier((result, usage))
     parts = over_y(result.reshape(stops, 2 * CAP, width))
     full = in_hbm((tokens, width), bf16)
     fwd_out, bwd_out = kernel_call(
@@ -309,8 +339,8 @@
          pltpu.VMEM((1, width), bf16), dma((4,))],
         parts, columns, rows16, picked, norm_gain, x_in, upstream,
     )
-    counts, prob_sums = jnp.sum(shared, axis=0)
-    tokens_all = tokens * devices
+    counts, prob_sums = summed_over(usage, EXPERT_AXES)
+    tokens_all = tokens * lax.axis_size(EXPERT_AXES)
     balance = EXPERTS * (counts / (tokens_all * TOPK)) * (prob_sums / tokens_all)
     return (fwd_out[None], bwd_out[None], balance[None])
 

time: 153 us -> 208 us (1.36)
  starting transfers between devices: 46 us -> 80.5 us
  waiting for transfers between devices: 42.1 us -> 65.3 us
    ppermute x5 -> x9, waiting for transfers between devices: 8.52 us -> 45.5 us  [shifted(): lax.ppermute(block, axis, [((i - distance) % n, i) for i in range(n)])]
    all_to_all x2, waiting for transfers between devices: 33.6 us -> 0.01 us  [over_y(): return lax.all_to_all(block, 'y', split_axis=0, concat_axis=0, tiled=True)]
    ppermute x5 -> x9, starting transfers between devices: 22.1 us -> 48.8 us  [shifted(): lax.ppermute(block, axis, [((i - distance) % n, i) for i in range(n)])]
    ppermute x0 -> x5, starting transfers between devices: none -> 20.5 us  [summed_over(): value = value + lax.ppermute(value, axis, [(i, i ^ step) for i in range(n)])]
    ppermute x0 -> x5, waiting for transfers between devices: none -> 19.8 us  [summed_over(): value = value + lax.ppermute(value, axis, [(i, i ^ step) for i in range(n)])]
    all_to_all x1 -> x0, starting transfers between devices: 10.4 us -> none  [body(): lax.all_to_all(jnp.broadcast_to(usage[None], (devices, 2, EXPERTS)), EXPE...]
    all_to_all x2, starting transfers between devices: 13.5 us -> 11.2 us  [over_y(): return lax.all_to_all(block, 'y', split_axis=0, concat_axis=0, tiled=True)]
    pallas_call x5 -> x6, Pallas kernels: 23.6 us -> 25.2 us  [kernel_call(): pl.pallas_call(body, out_shape=outs, in_specs=in_specs, out_specs=out_spe...]
  transfers between devices with their start and end apart: 8 -> 16, of which waited for: 5 -> 9; matrix products, arithmetic and copies ran while one was open for 3% -> 1% of each run, Pallas kernels for 7% -> 6%
where the time goes in v3:
time: 208 us
  starting transfers between devices  80.5 us (39%)
  waiting for transfers between devices  65.3 us (31%)
  blocking collectives  32.7 us (16%)
  Pallas kernels  25.2 us (12%)
  other arithmetic  2.31 us (1%)
    ppermute x9, starting transfers between devices, shifted(): lax.ppermute(block, axis, [((i - distance) % n, i) for i in range(n)])  48.8 us
    ppermute x9, waiting for transfers between devices, shifted(): lax.ppermute(block, axis, [((i - distance) % n, i) for i in range(n)])  45.5 us
    all_to_all x1, blocking collectives, over_y(): return lax.all_to_all(block, 'y', split_axis=0, concat_axis=0, tiled=True)  32.7 us
    pallas_call x6, Pallas kernels, kernel_call(): pl.pallas_call(body, out_shape=outs, in_specs=in_specs, out_specs=out_spe...  25.2 us
    ppermute x5, starting transfers between devices, summed_over(): value = value + lax.ppermute(value, axis, [(i, i ^ step) for i in range(n)])  20.5 us
    ppermute x5, waiting for transfers between devices, summed_over(): value = value + lax.ppermute(value, axis, [(i, i ^ step) for i in range(n)])  19.8 us
    all_to_all x2, starting transfers between devices, over_y(): return lax.all_to_all(block, 'y', split_axis=0, concat_axis=0, tiled=True)  11.2 us
  transfers between devices with their start and end apart: 16, of which 9 were waited for; matrix products, arithmetic and copies ran while one was open for 1% of the time, Pallas kernels for 6%

profile of v3, /device:TPU:1, one launch (start us, length us, event | category | flops | bytes accessed | tf_op | source)
XLA Modules:
  0.0 207.6 jit_solution(7130356669724064358)
XLA Ops:
  0.6 2.8 %shard_map.130 = (bf16[8,8,4096]{2,1,0:T(8,128)(2,1)}, bf16[16,4096]{1,0:T(8,128)(2,1)}, bf16[2,64,16]{2,1,0:T(8,128)(2,1)}, f32[3,16,128]{2,1,0:T(8,128)}, f32[2,128]{1,0:T(2,128)}) custom-call(bf16[64,4096]{1,0:T(8,128)(2,1)} %bitcast.31, bf16[1,4096]{1,0:T(2,128)(2,1)} %gain_h.5, s32[8,64]{1,0:T(8,128)} %bitcast.40, f32[64,128]{1,0:T(8,128)} %bitcast.36, ...), custom_call_target="tpu_custom_call" | custom-call | tf_op jit(solution)/shard_map/pallas_call | solution.py:82
  3.4 7.7 %all-to-all-start = ((bf16[8,8,4096]{2,1,0:T(8,128)(2,1)}), bf16[8,8,4096]{2,1,0:T(8,128)(2,1)S(1)}, u32[]{:S(2)}, u32[]{:S(2)}) async-start(bf16[8,8,4096]{2,1,0:T(8,128)(2,1)} %get-tuple-element.18), calls=%async_computation | async-start | bytes 1048576 | tf_op jit(solution)/shard_map/all_to_all | solution.py:272
  11.1 0.0 copy-start.5
  11.1 1.8 pad_maximum_fusion.slab_h
  12.9 0.0 copy-start
  12.9 4.6 %collective-permute-start.5 = (bf16[288,4096]{1,0:T(8,128)(2,1)S(1)}, bf16[288,4096]{1,0:T(8,128)(2,1)}, u32[]{:S(2)}, u32[]{:S(2)}) collective-permute-start(bf16[288,4096]{1,0:T(8,128)(2,1)S(1)} %pad_maximum_fusion.slab_h), channel_id=1, source_target_pairs={{1,0},{0,1},{3,2},{2,3},{5,4},{4,5},{7,6},{6,7},{9,8},{8,9},{11,10... | collective-permute-start | bytes 7077896 | tf_op jit(solution)/shard_map/ppermute | solution.py:259
  17.5 1.9 collective-permute-start.4
  19.5 12.3 %collective-permute-start = (s32[8,64]{1,0:T(8,128)S(1)}, s32[8,64]{1,0:T(8,128)S(1)}, u32[]{:S(2)}, u32[]{:S(2)}) collective-permute-start(s32[8,64]{1,0:T(8,128)S(1)} %bitcast.39), channel_id=1, source_target_pairs={{32,0},{64,32},{96,64},{128,96},{160,128},{192,160},{224,192},{256... | collective-permute-start | bytes 6152 | tf_op jit(solution)/shard_map/ppermute | solution.py:259
  31.7 1.9 collective-permute-start.1
  33.7 38.9 %collective-permute-done.froutes_h = s32[8,64]{1,0:T(8,128)S(1)} collective-permute-done((s32[8,64]{1,0:T(8,128)S(1)}, s32[8,64]{1,0:T(8,128)S(1)}, u32[]{:S(2)}, u32[]{:S(2)}) %collective-permute-start) | collective-permute-done | bytes 2080 | tf_op jit(solution)/shard_map/ppermute | solution.py:259
  72.6 0.0 collective-permute-done.1.broutes_h
  72.6 0.6 copy-done.6
  73.2 0.0 copy-done.7
  73.2 2.2 %shard_map.131 = (bf16[16,4096]{1,0:T(8,128)(2,1)}, bf16[16,4096]{1,0:T(8,128)(2,1)}) custom-call(s32[8,64]{1,0:T(8,128)} %copy-done.6, s32[8,64]{1,0:T(8,128)} %copy-done.7, bf16[64,4096]{1,0:T(8,128)(2,1)} %bitcast.32, bf16[64,4096]{1,0:T(8,128)(2,1)} %bitcast.34), custom_call_target="tpu_custom_call" | custom-call | tf_op jit(solution)/shard_map/pallas_call | solution.py:82
  75.4 3.2 %collective-permute-start.2 = (bf16[16,4096]{1,0:T(8,128)(2,1)}, bf16[16,4096]{1,0:T(8,128)(2,1)S(1)}, u32[]{:S(2)}, u32[]{:S(2)}) collective-permute-start(bf16[16,4096]{1,0:T(8,128)(2,1)} %get-tuple-element.19), channel_id=1, source_target_pairs={{480,0},{0,32},{32,64},{64,96},{96,128},{128,160},{160,192},{192,2... | collective-permute-start | bytes 393224 | tf_op jit(solution)/shard_map/ppermute | solution.py:259
  78.6 9.6 %collective-permute-start.3 = (bf16[16,4096]{1,0:T(8,128)(2,1)}, bf16[16,4096]{1,0:T(8,128)(2,1)S(1)}, u32[]{:S(2)}, u32[]{:S(2)}) collective-permute-start(bf16[16,4096]{1,0:T(8,128)(2,1)} %get-tuple-element.20), channel_id=1, source_target_pairs={{32,0},{64,32},{96,64},{128,96},{160,128},{192,160},{224,192},{256... | collective-permute-start | bytes 393224 | tf_op jit(solution)/shard_map/ppermute | solution.py:259
  88.2 1.0 collective-permute-done.2.fpicked
  89.2 1.2 collective-permute-done.3.bpicked
  90.4 1.9 shard_map.132
  92.4 0.0 all-to-all-done
  92.4 0.0 copy-start.1
  92.4 32.7 %all_to_all.15 = bf16[8,16,4096]{2,1,0:T(8,128)(2,1)} all-to-all(bf16[8,16,4096]{2,1,0:T(8,128)(2,1)} %shard_map.132), channel_id=1, replica_groups=mesh['section'=16,'y'=8,'xl'=2,'core'=2] {'y'}, dimensions={0} | all-to-all | bytes 2097152 | tf_op jit(solution)/shard_map/all_to_all | solution.py:272
  125.1 0.0 collective-permute-done.5.slab2_h
  125.1 8.1 %shard_map.133.part_h = f32[128,4096]{1,0:T(8,128)} custom-call(bf16[64,4096]{1,0:T(8,128)(2,1)} %bitcast.25, bf16[128,4096]{1,0:T(8,128)(2,1)} %bitcast.23, bf16[288,4096]{1,0:T(8,128)(2,1)} %copy-done, bf16[288,4096]{1,0:T(8,128)(2,1)} %collective-permute-done.5.slab2_h), custom_call_target="tpu_custom_call" | custom-call | tf_op jit(solution)/shard_map/pallas_call | solution.py:82
  133.3 0.0 copy-start.2
  133.3 0.0 collective-permute-done.4.slab_h
  133.3 0.0 copy-start.3
  133.3 6.0 %collective-permute-start.6 = (bf16[288,4096]{1,0:T(8,128)(2,1)}, bf16[288,4096]{1,0:T(8,128)(2,1)S(1)}, u32[]{:S(2)}, u32[]{:S(2)}) collective-permute-start(bf16[288,4096]{1,0:T(8,128)(2,1)} %collective-permute-done.4.slab_h), channel_id=1, source_target_pairs={{1,0},{0,1},{3,2},{2,3},{5,4},{4,5},{7,6},{6,7},{9,8},{8,9},{11,10... | collective-permute-start | bytes 7077896 | tf_op jit(solution)/shard_map/ppermute | solution.py:259
  139.3 4.3 %collective-permute-done.6.slab2 = bf16[288,4096]{1,0:T(8,128)(2,1)S(1)} collective-permute-done((bf16[288,4096]{1,0:T(8,128)(2,1)}, bf16[288,4096]{1,0:T(8,128)(2,1)S(1)}, u32[]{:S(2)}, u32[]{:S(2)}) %collective-permute-start.6) | collective-permute-done | bytes 2359328 | tf_op jit(solution)/shard_map/ppermute | solution.py:259
  143.7 7.3 %shard_map.134 = bf16[128,4096]{1,0:T(8,128)(2,1)} custom-call(bf16[64,4096]{1,0:T(8,128)(2,1)} %bitcast.26, bf16[128,4096]{1,0:T(8,128)(2,1)} %bitcast.24, bf16[288,4096]{1,0:T(8,128)(2,1)} %collective-permute-done.4.slab_h, bf16[288,4096]{1,0:T(8,128)(2,1)S(1)} %collective-permute-done.6.slab2, f32[128,4096]{1,0:T(8,128)} %shard_map.133.part_h), custom_call_target="tpu_custom_call" | custom-call | tf_op jit(solution)/shard_map/pallas_call | solution.py:82
  151.0 3.6 %all-to-all-start.2 = ((bf16[8,16,4096]{2,1,0:T(8,128)(2,1)}), bf16[8,16,4096]{2,1,0:T(8,128)(2,1)S(1)}, u32[]{:S(2)}, u32[]{:S(2)}) async-start(bf16[8,16,4096]{2,1,0:T(8,128)(2,1)} %bitcast.27), calls=%async_computation.2 | async-start | bytes 2097152 | tf_op jit(solution)/shard_map/all_to_all | solution.py:272
  154.6 1.9 collective-permute-start.7
  156.5 7.3 %collective-permute-start.8 = (bf16[64,4096]{1,0:T(8,128)(2,1)S(1)}, bf16[64,4096]{1,0:T(8,128)(2,1)S(1)}, u32[]{:S(2)}, u32[]{:S(2)}) collective-permute-start(bf16[64,4096]{1,0:T(8,128)(2,1)S(1)} %bitcast.35), channel_id=1, source_target_pairs={{32,0},{64,32},{96,64},{128,96},{160,128},{192,160},{224,192},{256... | collective-permute-start | bytes 1572872 | tf_op jit(solution)/shard_map/ppermute | solution.py:259
  163.9 3.2 %collective-permute-start.9 = (f32[2,128]{1,0:T(2,128)S(1)}, f32[2,128]{1,0:T(2,128)S(1)}, u32[]{:S(2)}, u32[]{:S(2)}) collective-permute-start(f32[2,128]{1,0:T(2,128)S(1)} %copy-done.8), channel_id=1, source_target_pairs={{0,4},{4,0},{8,12},{12,8},{16,20},{20,16},{24,28},{28,24},{1,5},{5... | collective-permute-start | bytes 3080 | tf_op jit(solution)/shard_map/ppermute | solution.py:266
  167.1 12.0 %collective-permute-done.9 = f32[2,128]{1,0:T(2,128)S(1)} collective-permute-done((f32[2,128]{1,0:T(2,128)S(1)}, f32[2,128]{1,0:T(2,128)S(1)}, u32[]{:S(2)}, u32[]{:S(2)}) %collective-permute-start.9) | collective-permute-done | bytes 1056 | tf_op jit(solution)/shard_map/ppermute | solution.py:266
  179.1 2.7 %collective-permute-start.10 = (f32[2,128]{1,0:T(2,128)S(1)}, f32[2,128]{1,0:T(2,128)S(1)}, u32[]{:S(2)}, u32[]{:S(2)}) collective-permute-start(f32[2,128]{1,0:T(2,128)S(1)} %add.15), channel_id=1, source_target_pairs={{0,8},{4,12},{8,0},{12,4},{16,24},{20,28},{24,16},{28,20},{1,9},{5... | collective-permute-start | bytes 3080 | tf_op jit(solution)/shard_map/ppermute | solution.py:266
  181.8 2.8 %collective-permute-done.10 = f32[2,128]{1,0:T(2,128)S(1)} collective-permute-done((f32[2,128]{1,0:T(2,128)S(1)}, f32[2,128]{1,0:T(2,128)S(1)}, u32[]{:S(2)}, u32[]{:S(2)}) %collective-permute-start.10) | collective-permute-done | bytes 1056 | tf_op jit(solution)/shard_map/ppermute | solution.py:266
  184.6 6.1 %collective-permute-start.11 = (f32[2,128]{1,0:T(2,128)S(1)}, f32[2,128]{1,0:T(2,128)S(1)}, u32[]{:S(2)}, u32[]{:S(2)}) collective-permute-start(f32[2,128]{1,0:T(2,128)S(1)} %add.16), channel_id=1, source_target_pairs={{0,16},{4,20},{8,24},{12,28},{16,0},{20,4},{24,8},{28,12},{1,17},{... | collective-permute-start | bytes 3080 | tf_op jit(solution)/shard_map/ppermute | solution.py:266
  190.7 2.1 %collective-permute-done.11 = f32[2,128]{1,0:T(2,128)S(1)} collective-permute-done((f32[2,128]{1,0:T(2,128)S(1)}, f32[2,128]{1,0:T(2,128)S(1)}, u32[]{:S(2)}, u32[]{:S(2)}) %collective-permute-start.11) | collective-permute-done | bytes 1056 | tf_op jit(solution)/shard_map/ppermute | solution.py:266
  192.8 2.2 %collective-permute-start.12 = (f32[2,128]{1,0:T(2,128)S(1)}, f32[2,128]{1,0:T(2,128)S(1)}, u32[]{:S(2)}, u32[]{:S(2)}) collective-permute-start(f32[2,128]{1,0:T(2,128)S(1)} %add.17), channel_id=1, source_target_pairs={{0,2},{2,0},{1,3},{3,1},{4,6},{6,4},{5,7},{7,5},{8,10},{10,8},{9,1... | collective-permute-start | bytes 3080 | tf_op jit(solution)/shard_map/ppermute | solution.py:266
  195.0 2.1 %collective-permute-done.12 = f32[2,128]{1,0:T(2,128)S(1)} collective-permute-done((f32[2,128]{1,0:T(2,128)S(1)}, f32[2,128]{1,0:T(2,128)S(1)}, u32[]{:S(2)}, u32[]{:S(2)}) %collective-permute-start.12) | collective-permute-done | bytes 1056 | tf_op jit(solution)/shard_map/ppermute | solution.py:266
  197.1 6.3 %collective-permute-start.13 = (f32[2,128]{1,0:T(2,128)S(1)}, f32[2,128]{1,0:T(2,128)S(1)}, u32[]{:S(2)}, u32[]{:S(2)}) collective-permute-start(f32[2,128]{1,0:T(2,128)S(1)} %add.18), channel_id=1, source_target_pairs={{0,1},{1,0},{2,3},{3,2},{4,5},{5,4},{6,7},{7,6},{8,9},{9,8},{10,11... | collective-permute-start | bytes 3080 | tf_op jit(solution)/shard_map/ppermute | solution.py:266
  203.4 0.8 collective-permute-done.13
  204.2 0.5 multiply_multiply_fusion
  204.7 0.0 collective-permute-done.7.x_in
  204.7 0.0 collective-permute-done.8.upstream
  204.7 0.0 all-to-all-done.2.parts
  204.7 2.9 %shard_map.135 = (bf16[64,4096]{1,0:T(8,128)(2,1)}, bf16[64,4096]{1,0:T(8,128)(2,1)}) custom-call(bf16[8,16,4096]{2,1,0:T(8,128)(2,1)S(1)} %all-to-all-done.2.parts, bf16[2,64,16]{2,1,0:T(8,128)(2,1)} %get-tuple-element.26.columns_h, f32[3,16,128]{2,1,0:T(8,128)} %get-tuple-element.21.rows16_h, bf16[16,4096]{1,0:T(8,128)(2,1)} %get-tuple-element.27.picked_h, ...), custom_call_target="tpu_custom_call" | custom-call | tf_op jit(solution)/shard_map/pallas_call | solution.py:82
  (16 shorter events, 0.0 us)
Async XLA Ops:
  3.4 89.0 %all-to-all-start = ((bf16[8,8,4096]{2,1,0:T(8,128)(2,1)}), bf16[8,8,4096]{2,1,0:T(8,128)(2,1)S(1)}, u32[]{:S(2)}, u32[]{:S(2)}) async-start(bf16[8,8,4096]{2,1,0:T(8,128)(2,1)} %get-tuple-element.18), calls=%async_computation | async-start | bytes 1048576 | tf_op jit(solution)/shard_map/all_to_all | solution.py:272
  11.1 8.4 %copy-start.4 = (s32[1,64,8]{1,2,0:T(8,128)S(1)}, s32[1,64,8]{1,2,0:T(8,128)}, u32[]{:S(2)}) copy-start(s32[1,64,8]{1,2,0:T(8,128)} %param.14) | copy-start | bytes 6148
  11.1 20.7 %copy-start.5 = (s32[1,64,8]{1,2,0:T(8,128)S(1)}, s32[1,64,8]{1,2,0:T(8,128)}, u32[]{:S(2)}) copy-start(s32[1,64,8]{1,2,0:T(8,128)} %param.15) | copy-start | bytes 6148
  12.9 112.3 %copy-start = (bf16[288,4096]{1,0:T(8,128)(2,1)}, bf16[288,4096]{1,0:T(8,128)(2,1)S(1)}, u32[]{:S(2)}) copy-start(bf16[288,4096]{1,0:T(8,128)(2,1)S(1)} %pad_maximum_fusion.slab_h) | copy-start | bytes 7077892
  12.9 112.3 %collective-permute-start.5 = (bf16[288,4096]{1,0:T(8,128)(2,1)S(1)}, bf16[288,4096]{1,0:T(8,128)(2,1)}, u32[]{:S(2)}, u32[]{:S(2)}) collective-permute-start(bf16[288,4096]{1,0:T(8,128)(2,1)S(1)} %pad_maximum_fusion.slab_h), channel_id=1, source_target_pairs={{1,0},{0,1},{3,2},{2,3},{5,4},{4,5},{7,6},{6,7},{9,8},{8,9},{11,10... | collective-permute-start | bytes 7077896 | tf_op jit(solution)/shard_map/ppermute | solution.py:259
  17.5 115.7 %collective-permute-start.4 = (bf16[288,4096]{1,0:T(8,128)(2,1)S(1)}, bf16[288,4096]{1,0:T(8,128)(2,1)}, u32[]{:S(2)}, u32[]{:S(2)}) collective-permute-start(bf16[288,4096]{1,0:T(8,128)(2,1)S(1)} %pad_maximum_fusion.slab_h), channel_id=1, source_target_pairs={{2,0},{0,2},{3,1},{1,3},{6,4},{4,6},{7,5},{5,7},{10,8},{8,10},{11,... | collective-permute-start | bytes 7077896 | tf_op jit(solution)/shard_map/ppermute | solution.py:259
  19.5 53.1 %collective-permute-start = (s32[8,64]{1,0:T(8,128)S(1)}, s32[8,64]{1,0:T(8,128)S(1)}, u32[]{:S(2)}, u32[]{:S(2)}) collective-permute-start(s32[8,64]{1,0:T(8,128)S(1)} %bitcast.39), channel_id=1, source_target_pairs={{32,0},{64,32},{96,64},{128,96},{160,128},{192,160},{224,192},{256... | collective-permute-start | bytes 6152 | tf_op jit(solution)/shard_map/ppermute | solution.py:259
  31.7 40.9 %collective-permute-start.1 = (s32[8,64]{1,0:T(8,128)S(1)}, s32[8,64]{1,0:T(8,128)S(1)}, u32[]{:S(2)}, u32[]{:S(2)}) collective-permute-start(s32[8,64]{1,0:T(8,128)S(1)} %bitcast.41), channel_id=1, source_target_pairs={{480,0},{0,32},{32,64},{64,96},{96,128},{128,160},{160,192},{192,2... | collective-permute-start | bytes 6152 | tf_op jit(solution)/shard_map/ppermute | solution.py:259
  72.6 0.6 copy-start.6
  72.6 0.6 copy-start.7
  75.4 13.9 %collective-permute-start.2 = (bf16[16,4096]{1,0:T(8,128)(2,1)}, bf16[16,4096]{1,0:T(8,128)(2,1)S(1)}, u32[]{:S(2)}, u32[]{:S(2)}) collective-permute-start(bf16[16,4096]{1,0:T(8,128)(2,1)} %get-tuple-element.19), channel_id=1, source_target_pairs={{480,0},{0,32},{32,64},{64,96},{96,128},{128,160},{160,192},{192,2... | collective-permute-start | bytes 393224 | tf_op jit(solution)/shard_map/ppermute | solution.py:259
  78.6 11.9 %collective-permute-start.3 = (bf16[16,4096]{1,0:T(8,128)(2,1)}, bf16[16,4096]{1,0:T(8,128)(2,1)S(1)}, u32[]{:S(2)}, u32[]{:S(2)}) collective-permute-start(bf16[16,4096]{1,0:T(8,128)(2,1)} %get-tuple-element.20), channel_id=1, source_target_pairs={{32,0},{64,32},{96,64},{128,96},{160,128},{192,160},{224,192},{256... | collective-permute-start | bytes 393224 | tf_op jit(solution)/shard_map/ppermute | solution.py:259
  92.4 32.8 %copy-start.1 = (bf16[8,8,4096]{2,1,0:T(8,128)(2,1)}, bf16[8,8,4096]{2,1,0:T(8,128)(2,1)S(1)}, u32[]{:S(2)}) copy-start(bf16[8,8,4096]{2,1,0:T(8,128)(2,1)S(1)} %all-to-all-done) | copy-start | bytes 1572868
  133.3 21.3 %copy-start.2 = (bf16[1,64,4096]{2,1,0:T(8,128)(2,1)S(1)}, bf16[1,64,4096]{2,1,0:T(8,128)(2,1)}, u32[]{:S(2)}) copy-start(bf16[1,64,4096]{2,1,0:T(8,128)(2,1)} %param.11) | copy-start | bytes 1572868
  133.3 30.6 %copy-start.8 = (f32[2,128]{1,0:T(2,128)S(1)}, f32[2,128]{1,0:T(2,128)}, u32[]{:S(2)}) copy-start(f32[2,128]{1,0:T(2,128)} %get-tuple-element.32) | copy-start | bytes 3076
  133.3 23.2 %copy-start.3 = (bf16[1,64,4096]{2,1,0:T(8,128)(2,1)S(1)}, bf16[1,64,4096]{2,1,0:T(8,128)(2,1)}, u32[]{:S(2)}) copy-start(bf16[1,64,4096]{2,1,0:T(8,128)(2,1)} %param.12) | copy-start | bytes 1572868
  133.3 10.4 %collective-permute-start.6 = (bf16[288,4096]{1,0:T(8,128)(2,1)}, bf16[288,4096]{1,0:T(8,128)(2,1)S(1)}, u32[]{:S(2)}, u32[]{:S(2)}) collective-permute-start(bf16[288,4096]{1,0:T(8,128)(2,1)} %collective-permute-done.4.slab_h), channel_id=1, source_target_pairs={{1,0},{0,1},{3,2},{2,3},{5,4},{4,5},{7,6},{6,7},{9,8},{8,9},{11,10... | collective-permute-start | bytes 7077896 | tf_op jit(solution)/shard_map/ppermute | solution.py:259
  151.0 53.7 %all-to-all-start.2 = ((bf16[8,16,4096]{2,1,0:T(8,128)(2,1)}), bf16[8,16,4096]{2,1,0:T(8,128)(2,1)S(1)}, u32[]{:S(2)}, u32[]{:S(2)}) async-start(bf16[8,16,4096]{2,1,0:T(8,128)(2,1)} %bitcast.27), calls=%async_computation.2 | async-start | bytes 2097152 | tf_op jit(solution)/shard_map/all_to_all | solution.py:272
  154.6 50.1 %collective-permute-start.7 = (bf16[64,4096]{1,0:T(8,128)(2,1)S(1)}, bf16[64,4096]{1,0:T(8,128)(2,1)S(1)}, u32[]{:S(2)}, u32[]{:S(2)}) collective-permute-start(bf16[64,4096]{1,0:T(8,128)(2,1)S(1)} %bitcast.33), channel_id=1, source_target_pairs={{480,0},{0,32},{32,64},{64,96},{96,128},{128,160},{160,192},{192,2... | collective-permute-start | bytes 1572872 | tf_op jit(solution)/shard_map/ppermute | solution.py:259
  156.5 48.2 %collective-permute-start.8 = (bf16[64,4096]{1,0:T(8,128)(2,1)S(1)}, bf16[64,4096]{1,0:T(8,128)(2,1)S(1)}, u32[]{:S(2)}, u32[]{:S(2)}) collective-permute-start(bf16[64,4096]{1,0:T(8,128)(2,1)S(1)} %bitcast.35), channel_id=1, source_target_pairs={{32,0},{64,32},{96,64},{128,96},{160,128},{192,160},{224,192},{256... | collective-permute-start | bytes 1572872 | tf_op jit(solution)/shard_map/ppermute | solution.py:259
  163.9 15.2 %collective-permute-start.9 = (f32[2,128]{1,0:T(2,128)S(1)}, f32[2,128]{1,0:T(2,128)S(1)}, u32[]{:S(2)}, u32[]{:S(2)}) collective-permute-start(f32[2,128]{1,0:T(2,128)S(1)} %copy-done.8), channel_id=1, source_target_pairs={{0,4},{4,0},{8,12},{12,8},{16,20},{20,16},{24,28},{28,24},{1,5},{5... | collective-permute-start | bytes 3080 | tf_op jit(solution)/shard_map/ppermute | solution.py:266
  179.1 5.5 %collective-permute-start.10 = (f32[2,128]{1,0:T(2,128)S(1)}, f32[2,128]{1,0:T(2,128)S(1)}, u32[]{:S(2)}, u32[]{:S(2)}) collective-permute-start(f32[2,128]{1,0:T(2,128)S(1)} %add.15), channel_id=1, source_target_pairs={{0,8},{4,12},{8,0},{12,4},{16,24},{20,28},{24,16},{28,20},{1,9},{5... | collective-permute-start | bytes 3080 | tf_op jit(solution)/shard_map/ppermute | solution.py:266
  184.6 8.2 %collective-permute-start.11 = (f32[2,128]{1,0:T(2,128)S(1)}, f32[2,128]{1,0:T(2,128)S(1)}, u32[]{:S(2)}, u32[]{:S(2)}) collective-permute-start(f32[2,128]{1,0:T(2,128)S(1)} %add.16), channel_id=1, source_target_pairs={{0,16},{4,20},{8,24},{12,28},{16,0},{20,4},{24,8},{28,12},{1,17},{... | collective-permute-start | bytes 3080 | tf_op jit(solution)/shard_map/ppermute | solution.py:266
  192.8 4.3 %collective-permute-start.12 = (f32[2,128]{1,0:T(2,128)S(1)}, f32[2,128]{1,0:T(2,128)S(1)}, u32[]{:S(2)}, u32[]{:S(2)}) collective-permute-start(f32[2,128]{1,0:T(2,128)S(1)} %add.17), channel_id=1, source_target_pairs={{0,2},{2,0},{1,3},{3,1},{4,6},{6,4},{5,7},{7,5},{8,10},{10,8},{9,1... | collective-permute-start | bytes 3080 | tf_op jit(solution)/shard_map/ppermute | solution.py:266
  197.1 7.1 %collective-permute-start.13 = (f32[2,128]{1,0:T(2,128)S(1)}, f32[2,128]{1,0:T(2,128)S(1)}, u32[]{:S(2)}, u32[]{:S(2)}) collective-permute-start(f32[2,128]{1,0:T(2,128)S(1)} %add.18), channel_id=1, source_target_pairs={{0,1},{1,0},{2,3},{3,2},{4,5},{5,4},{6,7},{7,6},{8,9},{9,8},{10,11... | collective-permute-start | bytes 3080 | tf_op jit(solution)/shard_map/ppermute | solution.py:266

commit v4 on v2

v4 whole, which is shorter than its diff:
```python
import jax
import jax.numpy as jnp
from jax import lax
from jax.experimental import pallas as pl
from jax.experimental.pallas import tpu as pltpu
from jax.sharding import Mesh, PartitionSpec as P

EXPERTS = 128
TOPK = 8
EXP_WIN = 2
CAP = 8
SLOTS = EXP_WIN * CAP
EPS = 1e-06
exact = lax.Precision.HIGHEST
f32 = jnp.float32
bf16 = jnp.bfloat16
NT = (((1,), (1,)), ((), ()))
PARAMS = pltpu.CompilerParams(vmem_limit_bytes=48 << 20)
EXPERT_AXES = ("y", "xl", "core")


def shape(dims, dtype):
    return jax.ShapeDtypeStruct(dims, dtype)


def iota(dims, axis):
    return lax.broadcasted_iota(jnp.int32, dims, axis)


def hot_columns(routes_t, experts):
    ids = iota((experts, routes_t.shape[1]), 0)
    hot_t = jnp.zeros(ids.shape, f32)
    for k in range(TOPK):
        hot_t = hot_t + jnp.where(ids == routes_t[k : k + 1, :], 1.0, 0.0)
    return hot_t


def selection(hot_t):
    tokens = hot_t.shape[1]
    first = hot_t[0:8, :]
    before = jnp.where(iota((tokens, tokens), 0) < iota((tokens, tokens), 1), 1.0, 0.0)
    earlier = jnp.dot(first.astype(bf16), before.astype(bf16), preferred_element_type=f32)
    slot = iota((CAP, tokens), 0).astype(f32)
    return jnp.concatenate(
        [
            jnp.where((earlier[e : e + 1, :] == slot) & (first[e : e + 1, :] > 0.5), 1.0, 0.0)
            for e in range(EXP_WIN)
        ],
        axis=0,
    ).astype(bf16)


def slot_tables(routes_t, logits):
    tokens, experts = logits.shape
    hot_t = hot_columns(routes_t, experts)
    eye = jnp.where(iota((tokens, tokens), 0) == iota((tokens, tokens), 1), 1.0, 0.0).astype(bf16)
    hot = lax.dot_general(eye, hot_t.astype(bf16), NT, preferred_element_type=f32)
    chosen = jnp.where(hot > 0.5, logits, -jnp.inf)
    powers = jnp.exp(chosen - jnp.max(chosen, axis=1, keepdims=True))
    gates = powers / jnp.sum(powers, axis=1, keepdims=True)
    select = selection(hot_t)
    select_t = lax.dot_general(eye, select, NT, preferred_element_type=f32)
    picked = jnp.dot(select.astype(f32), gates, precision=exact, preferred_element_type=f32)
    own = iota((SLOTS, experts), 1) == iota((SLOTS, experts), 0) // CAP
    gate_slot = jnp.sum(jnp.where(own, picked, 0.0), axis=1, keepdims=True)
    return hot, select, select_t.astype(bf16), gate_slot


HBM = pl.BlockSpec(memory_space=pltpu.HBM)
VMEM = pl.BlockSpec(memory_space=pltpu.VMEM)


def in_hbm(dims, dtype):
    return pltpu.HBM(dims, dtype)


def kernel_call(body, outs, in_specs, out_specs, scratch, *args):
    args = [
        pltpu.with_memory_space_constraint(v, pltpu.HBM) if spec is HBM else v
        for v, spec in zip(args, in_specs)
    ]
    return pl.pallas_call(
        body, out_shape=outs, in_specs=in_specs, out_specs=out_specs, scratch_shapes=scratch,
        compiler_params=PARAMS,
    )(*args)


def started(sems, *pairs):
    copies = [pltpu.make_async_copy(src, dst, sems.at[i]) for i, (src, dst) in enumerate(pairs)]
    for copy in copies:
        copy.start()
    return copies


def wait_all(copies):
    for copy in copies:
        copy.wait()


def in_parts(value):
    high = value.astype(bf16)
    rest = value - high.astype(f32)
    mid = rest.astype(bf16)
    return (rest - mid.astype(f32)).astype(bf16), mid, high


def normed_rows(rows, gain):
    inverse = lax.rsqrt(jnp.mean(rows * rows, axis=1, keepdims=True) + EPS)
    return (rows * inverse * gain).astype(bf16), inverse


def by_expert(stops):
    return [(i, i * EXP_WIN // stops * CAP) for i in range(stops)]


def prepare_body(
    saved_h, gain_h, broutes_h, blogits_h, froutes_h, flogits_h,
    send, picked, columns, rows16,
    saved, gain, broutes, blogits, froutes, flogits, sems,
):
    copies = started(
        sems, (broutes_h, broutes), (blogits_h, blogits), (froutes_h, froutes),
        (flogits_h, flogits), (gain_h, gain), (saved_h, saved),
    )
    wait_all(copies[:4])
    _, select, bselect_t, bgate = slot_tables(broutes[...], blogits[...])
    logits = flogits[...]
    hot, _, fselect_t, fgate = slot_tables(froutes[...], logits)
    powers = jnp.exp(logits - jnp.max(logits, axis=1, keepdims=True))
    probs = powers / jnp.sum(powers, axis=1, keepdims=True)
    usage = [jnp.sum(hot, axis=0, keepdims=True)]
    usage += [p.astype(f32) for p in in_parts(jnp.sum(probs, axis=0, keepdims=True))]
    usage += [jnp.zeros((CAP - len(usage), EXPERTS), f32)]
    usage = jnp.concatenate(usage, axis=0).astype(bf16)
    width = saved.shape[1]
    wait_all(copies[4:])
    rows = jnp.dot(select, saved[...], preferred_element_type=f32)
    normed, inverse = normed_rows(rows, gain[...].astype(f32))
    picked[...] = rows.astype(bf16)
    columns[0, :, :] = bselect_t
    columns[1, :, :] = fselect_t
    wide = (SLOTS, EXPERTS)
    rows16[0, :, :] = jnp.broadcast_to(bgate, wide)
    rows16[1, :, :] = jnp.broadcast_to(fgate, wide)
    rows16[2, :, :] = jnp.broadcast_to(inverse, wide)
    for i, r in by_expert(send.shape[0]):
        send[i, :, 0:width] = normed[r : r + CAP, :]
        send[i, :, width:] = usage


def rows_body(x_in, upstream, columns_h, rows16_h, gain_h, send, columns, gates, gain, sems):
    copies = started(sems, (columns_h, columns), (rows16_h.at[0], gates), (gain_h, gain))
    copies[0].wait()

    def chosen(i, block):
        return lax.dot_general(
            columns[i, :, :], block[...], (((0,), (0,)), ((), ())), preferred_element_type=f32
        )

    rows = chosen(1, x_in)
    grads = chosen(0, upstream)
    wait_all(copies[1:])
    normed = normed_rows(rows, gain[...].astype(f32))[0]
    grads = (grads * gates[:, 0:1]).astype(bf16)
    for i, r in by_expert(send.shape[0]):
        send[i, 0:CAP, :] = normed[r : r + CAP, :]
        send[i, CAP : 2 * CAP, :] = grads[r : r + CAP, :]


COLS = 512


def nt(a, b):
    return lax.dot_general(a, b, NT, preferred_element_type=f32)


def row_blocks(mixed_h, start, dst):
    return [
        (mixed_h.at[i, start : start + CAP, :], dst.at[i * CAP : (i + 1) * CAP, :])
        for i in range(mixed_h.shape[0])
    ]


def stacked(dst, *blocks):
    pairs, row = [], 0
    for block in blocks:
        pairs.append((block, dst.at[row : row + block.shape[0], :]))
        row += block.shape[0]
    return pairs


def hidden_of(pre):
    half, hid = pre.shape[0] // 2, pre.shape[1] // 2
    a, b = pre[:half, :hid], pre[:half, hid:]
    return (jax.nn.silu(a) * b).astype(bf16), pre[half:, :hid], pre[half:, hid:]


def hidden_grads(a, b, d_hidden):
    sigma = jax.nn.sigmoid(a)
    d_gate = d_hidden * b * sigma * (1.0 + a * (1.0 - sigma))
    d_up = d_hidden * a * sigma
    return jnp.concatenate([d_gate, d_up], axis=1).astype(bf16)


def slab_pairs(slabs, gu, down):
    hid = down.shape[0] // len(slabs)
    pieces = [w.at[m * hid : (m + 1) * hid, :] for m in range(3) for w in slabs]
    gates = len(slabs) * 2
    return stacked(gu, *pieces[:gates]), stacked(down, *pieces[gates:])


def expert_own_body(
    mixed_h, saved_h, slab0, slab1, first, usage, both, grads, tail, gu, down, sems
):
    rows, width = both.shape
    gates, downs = slab_pairs((slab0, slab1), gu, down)
    pairs = row_blocks(mixed_h, 0, both) + gates
    pairs.append((saved_h.at[:, 0:width], both.at[rows // 2 :, :]))
    early = len(pairs)
    pairs += row_blocks(mixed_h, CAP, grads) + downs
    pairs.append((saved_h.at[:, width:], tail))
    copies = started(sems, *pairs)
    wait_all(copies[:early])
    h, a, b = hidden_of(nt(both[...], gu[...]))
    wait_all(copies[early:])
    terms = hidden_grads(a, b, nt(grads[...], down[...]))
    for c in range(0, width, COLS):
        cut = slice(c, c + COLS)
        first[0, :, cut] = jnp.dot(h, down[:, cut], preferred_element_type=f32)
        first[1, :, cut] = jnp.dot(terms, gu[:, cut], preferred_element_type=f32)
    shares = sum(
        tail[i * CAP : (i + 1) * CAP, :].astype(f32) for i in range(mixed_h.shape[0])
    )
    usage[...] = jnp.concatenate(
        [shares[0:1, :], shares[1:2, :] + shares[2:3, :] + shares[3:4, :]], axis=0
    )


def expert_beside_body(
    mixed_h, saved_h, first_h, slab0, slab1, out, both, grads, first, gu, down, sems
):
    rows, width = both.shape
    gates, downs = slab_pairs((slab0, slab1), gu, down)
    pairs = row_blocks(mixed_h, 0, both) + gates
    pairs.append((saved_h.at[:, 0:width], both.at[rows // 2 :, :]))
    early = len(pairs)
    copies = started(sems, *pairs, *row_blocks(mixed_h, CAP, grads), *downs, (first_h, first))
    wait_all(copies[:early])
    h, a, b = hidden_of(nt(both[...], gu[...]))
    wait_all(copies[early:])
    terms = hidden_grads(a, b, nt(grads[...], down[...]))
    for c in range(0, width, COLS):
        cut = slice(c, c + COLS)
        fwd = first[0, :, cut] + jnp.dot(h, down[:, cut], preferred_element_type=f32)
        bwd = first[1, :, cut] + jnp.dot(terms, gu[:, cut], preferred_element_type=f32)
        for i in range(out.shape[0]):
            out[i, 0:CAP, cut] = fwd[i * CAP : (i + 1) * CAP, :].astype(bf16)
            out[i, CAP : 2 * CAP, cut] = bwd[i * CAP : (i + 1) * CAP, :].astype(bf16)


def placed(select_t, rows):
    return sum(jnp.dot(select_t, p, preferred_element_type=f32) for p in in_parts(rows))


def combine_body(
    parts, columns_h, rows16_h, picked_h, gain_h, x_in, upstream, fwd_out, bwd_out,
    columns, rows16, picked, gain, sems,
):
    wait_all(
        started(
            sems, (columns_h, columns), (rows16_h, rows16), (picked_h, picked), (gain_h, gain)
        )
    )
    half = parts.shape[0] // EXP_WIN

    def summed(start):
        return jnp.concatenate(
            [
                sum(
                    parts[e * half + i, start : start + CAP, :].astype(f32) for i in range(half)
                )
                for e in range(EXP_WIN)
            ],
            axis=0,
        )

    rows = summed(0) * rows16[1, :, 0:1]
    fwd_out[...] = (x_in[...].astype(f32) + placed(columns[1, :, :], rows)).astype(bf16)
    weighted = gain[...].astype(f32) * summed(CAP)
    inv = rows16[2, :, 0:1]
    x = picked[...].astype(f32)
    rows = inv * weighted - x * (inv * inv * inv) * jnp.mean(x * weighted, axis=1, keepdims=True)
    bwd_out[...] = (upstream[...].astype(f32) + placed(columns[0, :, :], rows)).astype(bf16)


def shifted(block, axis, distance):
    n = lax.axis_size(axis)
    return lax.ppermute(block, axis, [((i - distance) % n, i) for i in range(n)])


def over_y(block):
    return lax.all_to_all(block, "y", split_axis=0, concat_axis=0, tiled=True)


def body(
    fwd_sent, bwd_sent, bwd_saved, fwd_routes, bwd_routes, fwd_logits, bwd_logits,
    norm_gain, w_gate, w_up, w_down,
):
    stops = lax.axis_size("y")
    tokens, width = fwd_sent.shape[1:]
    dma = pltpu.SemaphoreType.DMA
    upstream = shifted(bwd_sent[0], "section", -1)
    x_in = shifted(fwd_sent[0], "section", 1)
    slab = jnp.concatenate([w_gate[0].T, w_up[0].T, w_down[0]], axis=0)
    slab_x = shifted(slab, "xl", 1)
    slab_core = shifted(slab, "core", 1)
    saved_send, picked, columns, rows16 = kernel_call(
        prepare_body,
        (in_hbm((stops, CAP, width + EXPERTS), bf16), in_hbm((SLOTS, width), bf16),
         in_hbm((EXP_WIN, tokens, SLOTS), bf16), in_hbm((3, SLOTS, EXPERTS), f32)),
        [HBM] * 6, [VMEM] * 4,
        [pltpu.VMEM((tokens, width), bf16), pltpu.VMEM((1, width), bf16),
         pltpu.VMEM((TOPK, tokens), jnp.int32), pltpu.VMEM((tokens, EXPERTS), f32),
         pltpu.VMEM((TOPK, tokens), jnp.int32), pltpu.VMEM((tokens, EXPERTS), f32), dma((6,))],
        bwd_saved[0], norm_gain, bwd_routes[0].T, bwd_logits[0], fwd_routes[0].T, fwd_logits[0],
    )
    saved_all = over_y(saved_send).reshape(-1, width + EXPERTS)
    mixed_send = kernel_call(
        rows_body, in_hbm((stops, 2 * CAP, width), bf16), [VMEM, VMEM, HBM, HBM, HBM], VMEM,
        [pltpu.VMEM((EXP_WIN, tokens, SLOTS), bf16), pltpu.VMEM((SLOTS, EXPERTS), f32),
         pltpu.VMEM((1, width), bf16), dma((3,))],
        x_in, upstream, columns, rows16, norm_gain,
    )
    mixed_all = over_y(mixed_send)
    count, hid = stops * CAP, slab.shape[0] // 3
    vmem = pltpu.VMEM
    both, grads = vmem((2 * count, width), bf16), vmem((count, width), bf16)
    gu, down = vmem((4 * hid, width), bf16), vmem((2 * hid, width), bf16)
    sums = in_hbm((2, count, width), f32)
    first, usage = kernel_call(
        expert_own_body, (sums, in_hbm((2, EXPERTS), f32)), [HBM] * 4, [VMEM] * 2,
        [both, grads, vmem((count, EXPERTS), bf16), gu, down, dma((2 * stops + 8,))],
        mixed_all, saved_all, slab, slab_core,
    )
    slab_x, first = lax.optimization_barrier((slab_x, first))
    result = kernel_call(
        expert_beside_body, in_hbm((stops, 2 * CAP, width), bf16), [HBM] * 4 + [VMEM], VMEM,
        [both, grads, vmem(sums.shape, f32), gu, down, dma((2 * stops + 8,))],
        mixed_all, saved_all, first, slab_x, shifted(slab_x, "core", 1),
    )
    result, usage = lax.optimization_barrier((result, usage))
    parts = over_y(result)
    full = in_hbm((tokens, width), bf16)
    fwd_out, bwd_out = kernel_call(
        combine_body, (full, full), [VMEM] + [HBM] * 4 + [VMEM] * 2, [VMEM] * 2,
        [pltpu.VMEM(columns.shape, bf16),
         pltpu.VMEM(rows16.shape, f32), pltpu.VMEM(picked.shape, bf16),
         pltpu.VMEM((1, width), bf16), dma((4,))],
        parts, columns, rows16, picked, norm_gain, x_in, upstream,
    )
    for axis in ("xl", "core"):
        usage = usage + shifted(usage, axis, 1)
    counts, prob_sums = usage
    tokens_all = tokens * lax.axis_size(EXPERT_AXES)
    balance = EXPERTS * (counts / (tokens_all * TOPK)) * (prob_sums / tokens_all)
    return (fwd_out[None], bwd_out[None], balance[None])


def solution(mesh):
    sections = mesh.shape["section"]
    grid = mesh.devices.reshape(sections, -1, 2, 2)
    inner = Mesh(grid, ("section",) + EXPERT_AXES)
    rows = P("section", EXPERT_AXES, None)
    return jax.shard_map(
        body,
        mesh=inner,
        in_specs=(
            rows, rows, rows, rows, rows, rows, rows,
            P("section", None),
            P("section", None, EXPERT_AXES),
            P("section", None, EXPERT_AXES),
            rows,
        ),
        out_specs=(rows, rows, P("section", None)),
        check_vma=False,
    )
```

time: 153 us -> 141 us (0.922)
  local copies, waits for them, and re-layouts: 2.64 us -> 0.01 us
  starting transfers between devices: 46 us -> 43.5 us
  blocking collectives: 33.2 us -> 30.9 us
  Pallas kernels: 23.6 us -> 21.3 us
  waiting for transfers between devices: 42.1 us -> 39.9 us
    all_to_all x1 -> x0, starting transfers between devices: 10.4 us -> none  [body(): lax.all_to_all(jnp.broadcast_to(usage[None], (devices, 2, EXPERTS)), EXPE...]
    ppermute x5 -> x7, starting transfers between devices: 22.1 us -> 29.7 us  [shifted(): lax.ppermute(block, axis, [((i - distance) % n, i) for i in range(n)])]
    all_to_all x2, waiting for transfers between devices: 33.6 us -> 26.4 us  [over_y(): return lax.all_to_all(block, 'y', split_axis=0, concat_axis=0, tiled=True)]
    ppermute x5 -> x7, waiting for transfers between devices: 8.52 us -> 13.6 us  [shifted(): lax.ppermute(block, axis, [((i - distance) % n, i) for i in range(n)])]
    all_to_all x1, blocking collectives: 33.2 us -> 30.9 us  [over_y(): return lax.all_to_all(block, 'y', split_axis=0, concat_axis=0, tiled=True)]
    pallas_call x5, Pallas kernels: 23.6 us -> 21.3 us  [kernel_call(): pl.pallas_call(body, out_shape=outs, in_specs=in_specs, out_specs=out_spe...]
  transfers between devices with their start and end apart: 8 -> 9, of which waited for: 5 -> 6; matrix products, arithmetic and copies ran while one was open for 3% -> 3% of each run, Pallas kernels for 7% -> 9%
where the time goes in v4:
time: 141 us; the launch traced here: 140 us
  starting transfers between devices  43.5 us (31%)
  waiting for transfers between devices  39.9 us (28%)
  blocking collectives  30.9 us (22%)
  Pallas kernels  21.3 us (15%)
  other arithmetic  3.81 us (3%)
    all_to_all x1, blocking collectives, over_y(): return lax.all_to_all(block, 'y', split_axis=0, concat_axis=0, tiled=True)  30.9 us
    ppermute x7, starting transfers between devices, shifted(): lax.ppermute(block, axis, [((i - distance) % n, i) for i in range(n)])  29.7 us
    all_to_all x2, waiting for transfers between devices, over_y(): return lax.all_to_all(block, 'y', split_axis=0, concat_axis=0, tiled=True)  26.4 us
    pallas_call x5, Pallas kernels, kernel_call(): pl.pallas_call(body, out_shape=outs, in_specs=in_specs, out_specs=out_spe...  21.3 us
    all_to_all x2, starting transfers between devices, over_y(): return lax.all_to_all(block, 'y', split_axis=0, concat_axis=0, tiled=True)  13.8 us
    ppermute x7, waiting for transfers between devices, shifted(): lax.ppermute(block, axis, [((i - distance) % n, i) for i in range(n)])  13.6 us
    concatenate x1, other arithmetic, body(): slab = jnp.concatenate([w_gate[0].T, w_up[0].T, w_down[0]], axis=0)  3.28 us
  transfers between devices with their start and end apart: 9, of which 6 were waited for; matrix products, arithmetic and copies ran while one was open for 3% of the time, Pallas kernels for 9%

profile of v4, /device:TPU:1, one launch (start us, length us, event | category | flops | bytes accessed | tf_op | source)
XLA Modules:
  0.0 140.2 jit_solution(4410828469034981521)
XLA Ops:
  0.6 5.5 %collective-permute-start = (bf16[64,4096]{1,0:T(8,128)(2,1)}, bf16[64,4096]{1,0:T(8,128)(2,1)S(1)}, u32[]{:S(2)}, u32[]{:S(2)}) collective-permute-start(bf16[64,4096]{1,0:T(8,128)(2,1)} %bitcast.31), channel_id=1, source_target_pairs={{480,0},{0,32},{32,64},{64,96},{96,128},{128,160},{160,192},{192,2... | collective-permute-start | bytes 1572872 | tf_op jit(solution)/shard_map/ppermute | solution.py:298
  6.1 10.4 %collective-permute-start.1 = (bf16[64,4096]{1,0:T(8,128)(2,1)}, bf16[64,4096]{1,0:T(8,128)(2,1)S(1)}, u32[]{:S(2)}, u32[]{:S(2)}) collective-permute-start(bf16[64,4096]{1,0:T(8,128)(2,1)} %bitcast.32), channel_id=1, source_target_pairs={{32,0},{64,32},{96,64},{128,96},{160,128},{192,160},{224,192},{256... | collective-permute-start | bytes 1572872 | tf_op jit(solution)/shard_map/ppermute | solution.py:298
  16.5 2.8 %shard_map.130 = (bf16[8,8,4224]{2,1,0:T(8,128)(2,1)}, bf16[16,4096]{1,0:T(8,128)(2,1)}, bf16[2,64,16]{2,1,0:T(8,128)(2,1)}, f32[3,16,128]{2,1,0:T(8,128)}) custom-call(bf16[64,4096]{1,0:T(8,128)(2,1)} %bitcast.26, bf16[1,4096]{1,0:T(2,128)(2,1)} %gain_h.5, s32[8,64]{1,0:T(8,128)} %bitcast.29, f32[64,128]{1,0:T(8,128)} %bitcast.27, s32[8,64]{1,0:T(8,128)} %bitcast.30, ...), custom_call_target="tpu_custom_call" | custom-call | tf_op jit(solution)/shard_map/pallas_call | solution.py:82
  19.4 6.8 %all-to-all-start.1 = ((bf16[8,8,4224]{2,1,0:T(8,128)(2,1)}), bf16[8,8,4224]{2,1,0:T(8,128)(2,1)S(1)}, u32[]{:S(2)}, u32[]{:S(2)}) async-start(bf16[8,8,4224]{2,1,0:T(8,128)(2,1)} %get-tuple-element.17), calls=%async_computation.1 | async-start | bytes 1081344 | tf_op jit(solution)/shard_map/all_to_all | solution.py:302
  26.2 3.3 %pad_maximum_fusion.slab0 = bf16[288,4096]{1,0:T(8,128)(2,1)} fusion(bf16[96,4096]{1,0:T(8,128)(2,1)} %bitcast.23, bf16[96,4096]{1,0:T(8,128)(2,1)} %bitcast.24, bf16[96,4096]{1,0:T(8,128)(2,1)} %bitcast.25), kind=kLoop, calls=%fused_computation | loop fusion | flops 7077888 | bytes 4718592 | tf_op jit(solution)/shard_map/concatenate | solution.py:314
  29.5 3.1 %collective-permute-start.3 = (bf16[288,4096]{1,0:T(8,128)(2,1)}, bf16[288,4096]{1,0:T(8,128)(2,1)}, u32[]{:S(2)}, u32[]{:S(2)}) collective-permute-start(bf16[288,4096]{1,0:T(8,128)(2,1)} %pad_maximum_fusion.slab0), channel_id=1, source_target_pairs={{1,0},{0,1},{3,2},{2,3},{5,4},{4,5},{7,6},{6,7},{9,8},{8,9},{11,10... | collective-permute-start | bytes 7077896 | tf_op jit(solution)/shard_map/ppermute | solution.py:298
  32.6 2.2 %collective-permute-start.2 = (bf16[288,4096]{1,0:T(8,128)(2,1)}, bf16[288,4096]{1,0:T(8,128)(2,1)}, u32[]{:S(2)}, u32[]{:S(2)}) collective-permute-start(bf16[288,4096]{1,0:T(8,128)(2,1)} %pad_maximum_fusion.slab0), channel_id=1, source_target_pairs={{2,0},{0,2},{3,1},{1,3},{6,4},{4,6},{7,5},{5,7},{10,8},{8,10},{11,... | collective-permute-start | bytes 7077896 | tf_op jit(solution)/shard_map/ppermute | solution.py:298
  34.8 0.0 collective-permute-done.x_in
  34.9 0.0 collective-permute-done.1.upstream
  34.9 2.2 %shard_map.131 = bf16[8,16,4096]{2,1,0:T(8,128)(2,1)} custom-call(bf16[64,4096]{1,0:T(8,128)(2,1)S(1)} %collective-permute-done.x_in, bf16[64,4096]{1,0:T(8,128)(2,1)S(1)} %collective-permute-done.1.upstream, bf16[2,64,16]{2,1,0:T(8,128)(2,1)} %get-tuple-element.15.columns_h, f32[3,16,128]{2,1,0:T(8,128)} %get-tuple-element.16.rows16_h, bf16[1,4096]{1,0:T(2,128)(2,1)} %gain_h.5), custom_call_target="tpu_custom_call" | custom-call | tf_op jit(solution)/shard_map/pallas_call | solution.py:82
  37.1 6.5 %all-to-all-done.1 = bf16[8,8,4224]{2,1,0:T(8,128)(2,1)S(1)} async-done(((bf16[8,8,4224]{2,1,0:T(8,128)(2,1)}), bf16[8,8,4224]{2,1,0:T(8,128)(2,1)S(1)}, u32[]{:S(2)}, u32[]{:S(2)}) %all-to-all-start.1) | async-done | bytes 540704 | tf_op jit(solution)/shard_map/all_to_all | solution.py:302
  43.6 0.0 copy-start
  43.6 30.9 %all_to_all.15.mixed_h = bf16[8,16,4096]{2,1,0:T(8,128)(2,1)} all-to-all(bf16[8,16,4096]{2,1,0:T(8,128)(2,1)} %shard_map.131), channel_id=1, replica_groups=mesh['section'=16,'y'=8,'xl'=2,'core'=2] {'y'}, dimensions={0} | all-to-all | bytes 2097152 | tf_op jit(solution)/shard_map/all_to_all | solution.py:302
  74.5 0.0 collective-permute-done.3.slab1
  74.5 0.0 copy-done
  74.5 7.1 %shard_map.132 = (f32[2,64,4096]{2,1,0:T(8,128)}, f32[2,128]{1,0:T(2,128)}) custom-call(bf16[8,16,4096]{2,1,0:T(8,128)(2,1)} %all_to_all.15.mixed_h, bf16[64,4224]{1,0:T(8,128)(2,1)} %bitcast.21, bf16[288,4096]{1,0:T(8,128)(2,1)} %pad_maximum_fusion.slab0, bf16[288,4096]{1,0:T(8,128)(2,1)} %collective-permute-done.3.slab1), custom_call_target="tpu_custom_call" | custom-call | tf_op jit(solution)/shard_map/pallas_call | solution.py:82
  81.6 6.0 %collective-permute-done.2.slab0 = bf16[288,4096]{1,0:T(8,128)(2,1)} collective-permute-done((bf16[288,4096]{1,0:T(8,128)(2,1)}, bf16[288,4096]{1,0:T(8,128)(2,1)}, u32[]{:S(2)}, u32[]{:S(2)}) %collective-permute-start.2) | collective-permute-done | bytes 2359328 | tf_op jit(solution)/shard_map/ppermute | solution.py:298
  87.7 0.0 copy-start.1
  87.7 2.8 %collective-permute-start.4 = (bf16[288,4096]{1,0:T(8,128)(2,1)}, bf16[288,4096]{1,0:T(8,128)(2,1)S(1)}, u32[]{:S(2)}, u32[]{:S(2)}) collective-permute-start(bf16[288,4096]{1,0:T(8,128)(2,1)} %collective-permute-done.2.slab0), channel_id=1, source_target_pairs={{1,0},{0,1},{3,2},{2,3},{5,4},{4,5},{7,6},{6,7},{9,8},{8,9},{11,10... | collective-permute-start | bytes 7077896 | tf_op jit(solution)/shard_map/ppermute | solution.py:298
  90.5 4.3 %collective-permute-done.4.slab1 = bf16[288,4096]{1,0:T(8,128)(2,1)S(1)} collective-permute-done((bf16[288,4096]{1,0:T(8,128)(2,1)}, bf16[288,4096]{1,0:T(8,128)(2,1)S(1)}, u32[]{:S(2)}, u32[]{:S(2)}) %collective-permute-start.4) | collective-permute-done | bytes 2359328 | tf_op jit(solution)/shard_map/ppermute | solution.py:298
  94.9 6.3 %shard_map.133 = bf16[8,16,4096]{2,1,0:T(8,128)(2,1)} custom-call(bf16[8,16,4096]{2,1,0:T(8,128)(2,1)} %all_to_all.15.mixed_h, bf16[64,4224]{1,0:T(8,128)(2,1)} %bitcast.22, f32[2,64,4096]{2,1,0:T(8,128)} %get-tuple-element.19.first_h, bf16[288,4096]{1,0:T(8,128)(2,1)} %collective-permute-done.2.slab0, bf16[288,4096]{1,0:T(8,128)(2,1)S(1)} %collective-permute-done.4.slab1), custom_call_target="tpu_custom_call" | custom-call | tf_op jit(solution)/shard_map/pallas_call | solution.py:82
  101.1 6.9 %all-to-all-start.2 = ((bf16[8,16,4096]{2,1,0:T(8,128)(2,1)}), bf16[8,16,4096]{2,1,0:T(8,128)(2,1)S(1)}, u32[]{:S(2)}, u32[]{:S(2)}) async-start(bf16[8,16,4096]{2,1,0:T(8,128)(2,1)} %shard_map.133), calls=%async_computation.2 | async-start | bytes 2097152 | tf_op jit(solution)/shard_map/all_to_all | solution.py:302
  108.1 0.0 copy-done.1
  108.1 2.2 %collective-permute-start.5 = (f32[2,128]{1,0:T(2,128)S(1)}, f32[2,128]{1,0:T(2,128)S(1)}, u32[]{:S(2)}, u32[]{:S(2)}) collective-permute-start(f32[2,128]{1,0:T(2,128)S(1)} %copy-done.1), channel_id=1, source_target_pairs={{2,0},{0,2},{3,1},{1,3},{6,4},{4,6},{7,5},{5,7},{10,8},{8,10},{11,... | collective-permute-start | bytes 3080 | tf_op jit(solution)/shard_map/ppermute | solution.py:298
  110.3 2.4 %collective-permute-done.5 = f32[2,128]{1,0:T(2,128)S(1)} collective-permute-done((f32[2,128]{1,0:T(2,128)S(1)}, f32[2,128]{1,0:T(2,128)S(1)}, u32[]{:S(2)}, u32[]{:S(2)}) %collective-permute-start.5) | collective-permute-done | bytes 1056 | tf_op jit(solution)/shard_map/ppermute | solution.py:298
  112.7 3.4 %collective-permute-start.6 = (f32[2,128]{1,0:T(2,128)S(1)}, f32[2,128]{1,0:T(2,128)S(1)}, u32[]{:S(2)}, u32[]{:S(2)}) collective-permute-start(f32[2,128]{1,0:T(2,128)S(1)} %add.6), channel_id=1, source_target_pairs={{1,0},{0,1},{3,2},{2,3},{5,4},{4,5},{7,6},{6,7},{9,8},{8,9},{11,10... | collective-permute-start | bytes 3080 | tf_op jit(solution)/shard_map/ppermute | solution.py:298
  116.1 0.8 collective-permute-done.6
  116.9 0.5 multiply_multiply_fusion
  117.4 19.9 %all-to-all-done.2.parts = bf16[8,16,4096]{2,1,0:T(8,128)(2,1)S(1)} async-done(((bf16[8,16,4096]{2,1,0:T(8,128)(2,1)}), bf16[8,16,4096]{2,1,0:T(8,128)(2,1)S(1)}, u32[]{:S(2)}, u32[]{:S(2)}) %all-to-all-start.2) | async-done | bytes 1048608 | tf_op jit(solution)/shard_map/all_to_all | solution.py:302
  137.3 2.9 %shard_map.134 = (bf16[64,4096]{1,0:T(8,128)(2,1)}, bf16[64,4096]{1,0:T(8,128)(2,1)}) custom-call(bf16[8,16,4096]{2,1,0:T(8,128)(2,1)S(1)} %all-to-all-done.2.parts, bf16[2,64,16]{2,1,0:T(8,128)(2,1)} %get-tuple-element.15.columns_h, f32[3,16,128]{2,1,0:T(8,128)} %get-tuple-element.16.rows16_h, bf16[16,4096]{1,0:T(8,128)(2,1)} %get-tuple-element.23.picked_h, ...), custom_call_target="tpu_custom_call" | custom-call | tf_op jit(solution)/shard_map/pallas_call | solution.py:82
  (2 shorter events, 0.0 us)
Async XLA Ops:
  0.6 34.2 %collective-permute-start = (bf16[64,4096]{1,0:T(8,128)(2,1)}, bf16[64,4096]{1,0:T(8,128)(2,1)S(1)}, u32[]{:S(2)}, u32[]{:S(2)}) collective-permute-start(bf16[64,4096]{1,0:T(8,128)(2,1)} %bitcast.31), channel_id=1, source_target_pairs={{480,0},{0,32},{32,64},{64,96},{96,128},{128,160},{160,192},{192,2... | collective-permute-start | bytes 1572872 | tf_op jit(solution)/shard_map/ppermute | solution.py:298
  6.1 28.7 %collective-permute-start.1 = (bf16[64,4096]{1,0:T(8,128)(2,1)}, bf16[64,4096]{1,0:T(8,128)(2,1)S(1)}, u32[]{:S(2)}, u32[]{:S(2)}) collective-permute-start(bf16[64,4096]{1,0:T(8,128)(2,1)} %bitcast.32), channel_id=1, source_target_pairs={{32,0},{64,32},{96,64},{128,96},{160,128},{192,160},{224,192},{256... | collective-permute-start | bytes 1572872 | tf_op jit(solution)/shard_map/ppermute | solution.py:298
  19.4 24.2 %all-to-all-start.1 = ((bf16[8,8,4224]{2,1,0:T(8,128)(2,1)}), bf16[8,8,4224]{2,1,0:T(8,128)(2,1)S(1)}, u32[]{:S(2)}, u32[]{:S(2)}) async-start(bf16[8,8,4224]{2,1,0:T(8,128)(2,1)} %get-tuple-element.17), calls=%async_computation.1 | async-start | bytes 1081344 | tf_op jit(solution)/shard_map/all_to_all | solution.py:302
  29.5 45.0 %collective-permute-start.3 = (bf16[288,4096]{1,0:T(8,128)(2,1)}, bf16[288,4096]{1,0:T(8,128)(2,1)}, u32[]{:S(2)}, u32[]{:S(2)}) collective-permute-start(bf16[288,4096]{1,0:T(8,128)(2,1)} %pad_maximum_fusion.slab0), channel_id=1, source_target_pairs={{1,0},{0,1},{3,2},{2,3},{5,4},{4,5},{7,6},{6,7},{9,8},{8,9},{11,10... | collective-permute-start | bytes 7077896 | tf_op jit(solution)/shard_map/ppermute | solution.py:298
  32.6 55.1 %collective-permute-start.2 = (bf16[288,4096]{1,0:T(8,128)(2,1)}, bf16[288,4096]{1,0:T(8,128)(2,1)}, u32[]{:S(2)}, u32[]{:S(2)}) collective-permute-start(bf16[288,4096]{1,0:T(8,128)(2,1)} %pad_maximum_fusion.slab0), channel_id=1, source_target_pairs={{2,0},{0,2},{3,1},{1,3},{6,4},{4,6},{7,5},{5,7},{10,8},{8,10},{11,... | collective-permute-start | bytes 7077896 | tf_op jit(solution)/shard_map/ppermute | solution.py:298
  43.6 30.9 %copy-start = (bf16[8,8,4224]{2,1,0:T(8,128)(2,1)}, bf16[8,8,4224]{2,1,0:T(8,128)(2,1)S(1)}, u32[]{:S(2)}) copy-start(bf16[8,8,4224]{2,1,0:T(8,128)(2,1)S(1)} %all-to-all-done.1) | copy-start | bytes 1622020
  87.7 20.4 %copy-start.1 = (f32[2,128]{1,0:T(2,128)S(1)}, f32[2,128]{1,0:T(2,128)}, u32[]{:S(2)}) copy-start(f32[2,128]{1,0:T(2,128)} %get-tuple-element.26) | copy-start | bytes 3076
  87.7 7.2 %collective-permute-start.4 = (bf16[288,4096]{1,0:T(8,128)(2,1)}, bf16[288,4096]{1,0:T(8,128)(2,1)S(1)}, u32[]{:S(2)}, u32[]{:S(2)}) collective-permute-start(bf16[288,4096]{1,0:T(8,128)(2,1)} %collective-permute-done.2.slab0), channel_id=1, source_target_pairs={{1,0},{0,1},{3,2},{2,3},{5,4},{4,5},{7,6},{6,7},{9,8},{8,9},{11,10... | collective-permute-start | bytes 7077896 | tf_op jit(solution)/shard_map/ppermute | solution.py:298
  101.1 36.2 %all-to-all-start.2 = ((bf16[8,16,4096]{2,1,0:T(8,128)(2,1)}), bf16[8,16,4096]{2,1,0:T(8,128)(2,1)S(1)}, u32[]{:S(2)}, u32[]{:S(2)}) async-start(bf16[8,16,4096]{2,1,0:T(8,128)(2,1)} %shard_map.133), calls=%async_computation.2 | async-start | bytes 2097152 | tf_op jit(solution)/shard_map/all_to_all | solution.py:302
  108.1 4.6 %collective-permute-start.5 = (f32[2,128]{1,0:T(2,128)S(1)}, f32[2,128]{1,0:T(2,128)S(1)}, u32[]{:S(2)}, u32[]{:S(2)}) collective-permute-start(f32[2,128]{1,0:T(2,128)S(1)} %copy-done.1), channel_id=1, source_target_pairs={{2,0},{0,2},{3,1},{1,3},{6,4},{4,6},{7,5},{5,7},{10,8},{8,10},{11,... | collective-permute-start | bytes 3080 | tf_op jit(solution)/shard_map/ppermute | solution.py:298
  112.7 4.2 %collective-permute-start.6 = (f32[2,128]{1,0:T(2,128)S(1)}, f32[2,128]{1,0:T(2,128)S(1)}, u32[]{:S(2)}, u32[]{:S(2)}) collective-permute-start(f32[2,128]{1,0:T(2,128)S(1)} %add.6), channel_id=1, source_target_pairs={{1,0},{0,1},{3,2},{2,3},{5,4},{4,5},{7,6},{6,7},{9,8},{8,9},{11,10... | collective-permute-start | bytes 3080 | tf_op jit(solution)/shard_map/ppermute | solution.py:298

commit v5 on v4

--- a/solution.py
+++ b/solution.py
@@ -17,6 +17,7 @@
 NT = (((1,), (1,)), ((), ()))
 PARAMS = pltpu.CompilerParams(vmem_limit_bytes=48 << 20)
 EXPERT_AXES = ("y", "xl", "core")
+PAIR_DEVICES = 4
 
 
 def shape(dims, dtype):
@@ -74,13 +75,14 @@
     return pltpu.HBM(dims, dtype)
 
 
-def kernel_call(body, outs, in_specs, out_specs, scratch, *args):
+def kernel_call(body, outs, in_specs, out_specs, scratch, *args, us=2):
     args = [
         pltpu.with_memory_space_constraint(v, pltpu.HBM) if spec is HBM else v
         for v, spec in zip(args, in_specs)
     ]
     return pl.pallas_call(
         body, out_shape=outs, in_specs=in_specs, out_specs=out_specs, scratch_shapes=scratch,
+        cost_estimate=pl.CostEstimate(flops=int(us * 1e9), transcendentals=0, bytes_accessed=0),
         compiler_params=PARAMS,
     )(*args)
 
@@ -113,14 +115,27 @@
     return [(i, i * EXP_WIN // stops * CAP) for i in range(stops)]
 
 
+def usage_rows(counts, prob_sums):
+    rows = [counts] + [p.astype(f32) for p in in_parts(prob_sums)]
+    rows.append(jnp.zeros((CAP - len(rows), EXPERTS), f32))
+    return jnp.concatenate(rows, axis=0).astype(bf16)
+
+
+def usage_of(rows):
+    rows = rows.astype(f32)
+    return jnp.concatenate([rows[0:1, :], rows[1:2, :] + rows[2:3, :] + rows[3:4, :]], axis=0)
+
+
 def prepare_body(
-    saved_h, gain_h, broutes_h, blogits_h, froutes_h, flogits_h,
-    send, picked, columns, rows16,
-    saved, gain, broutes, blogits, froutes, flogits, sems,
+    saved_h, gain_h, broutes_h, blogits_h, froutes_h, flogits_h, gate_h, up_h, down_h,
+    send, picked, columns, rows16, slab_h,
+    saved, gain, broutes, blogits, froutes, flogits, usage, sems,
 ):
+    hid = gate_h.shape[0]
     copies = started(
         sems, (broutes_h, broutes), (blogits_h, blogits), (froutes_h, froutes),
         (flogits_h, flogits), (gain_h, gain), (saved_h, saved),
+        *[(w, slab_h.at[m * hid : (m + 1) * hid, :]) for m, w in enumerate((gate_h, up_h, down_h))],
     )
     wait_all(copies[:4])
     _, select, bselect_t, bgate = slot_tables(broutes[...], blogits[...])
@@ -128,12 +143,14 @@
     hot, _, fselect_t, fgate = slot_tables(froutes[...], logits)
     powers = jnp.exp(logits - jnp.max(logits, axis=1, keepdims=True))
     probs = powers / jnp.sum(powers, axis=1, keepdims=True)
-    usage = [jnp.sum(hot, axis=0, keepdims=True)]
-    usage += [p.astype(f32) for p in in_parts(jnp.sum(probs, axis=0, keepdims=True))]
-    usage += [jnp.zeros((CAP - len(usage), EXPERTS), f32)]
-    usage = jnp.concatenate(usage, axis=0).astype(bf16)
-    width = saved.shape[1]
-    wait_all(copies[4:])
+    usage[...] = usage_rows(
+        jnp.sum(hot, axis=0, keepdims=True), jnp.sum(probs, axis=0, keepdims=True)
+    )
+    last = pltpu.make_async_copy(
+        usage, slab_h.at[3 * hid : 3 * hid + CAP, 0:EXPERTS], sems.at[len(copies)]
+    )
+    last.start()
+    wait_all(copies[4:6])
     rows = jnp.dot(select, saved[...], preferred_element_type=f32)
     normed, inverse = normed_rows(rows, gain[...].astype(f32))
     picked[...] = rows.astype(bf16)
@@ -144,8 +161,8 @@
     rows16[1, :, :] = jnp.broadcast_to(fgate, wide)
     rows16[2, :, :] = jnp.broadcast_to(inverse, wide)
     for i, r in by_expert(send.shape[0]):
-        send[i, :, 0:width] = normed[r : r + CAP, :]
-        send[i, :, width:] = usage
+        send[i, :, :] = normed[r : r + CAP, :]
+    wait_all(copies[6:] + [last])
 
 
 def rows_body(x_in, upstream, columns_h, rows16_h, gain_h, send, columns, gates, gain, sems):
@@ -204,51 +221,71 @@
 
 def slab_pairs(slabs, gu, down):
     hid = down.shape[0] // len(slabs)
-    pieces = [w.at[m * hid : (m + 1) * hid, :] for m in range(3) for w in slabs]
-    gates = len(slabs) * 2
-    return stacked(gu, *pieces[:gates]), stacked(down, *pieces[gates:])
+    return (
+        stacked(gu, *[w.at[0 : 2 * hid, :] for w in slabs]),
+        stacked(down, *[w.at[2 * hid : 3 * hid, :] for w in slabs]),
+    )
+
+
+def tail_of(slab):
+    return slab.at[slab.shape[0] - CAP :, 0:EXPERTS]
+
+
+def row_pairs(mixed_h, saved_h, both, grads):
+    first = row_blocks(mixed_h, 0, both) + [(saved_h, both.at[both.shape[0] // 2 :, :])]
+    return first, row_blocks(mixed_h, CAP, grads)
+
+
+def terms_of(both, grads, gate_up, down):
+    h, a, b = hidden_of(nt(both[...], gate_up))
+    return h, hidden_grads(a, b, nt(grads[...], down))
 
 
 def expert_own_body(
-    mixed_h, saved_h, slab0, slab1, first, usage, both, grads, tail, gu, down, sems
+    mixed_h, saved_h, slab0, slab1, first, usage, both, grads, tails, gu, down, sems
 ):
-    rows, width = both.shape
+    width, hid = both.shape[1], down.shape[0] // 2
+    early, late = row_pairs(mixed_h, saved_h, both, grads)
     gates, downs = slab_pairs((slab0, slab1), gu, down)
-    pairs = row_blocks(mixed_h, 0, both) + gates
-    pairs.append((saved_h.at[:, 0:width], both.at[rows // 2 :, :]))
-    early = len(pairs)
-    pairs += row_blocks(mixed_h, CAP, grads) + downs
-    pairs.append((saved_h.at[:, width:], tail))
-    copies = started(sems, *pairs)
-    wait_all(copies[:early])
-    h, a, b = hidden_of(nt(both[...], gu[...]))
-    wait_all(copies[early:])
-    terms = hidden_grads(a, b, nt(grads[...], down[...]))
+    early, late = early + gates, late + downs
+    late += [(tail_of(w), tails.at[m]) for m, w in enumerate((slab0, slab1))]
+    copies = started(sems, *early, *late)
+    wait_all(copies)
+    sides = [
+        terms_of(both, grads, gu[2 * hid * m : 2 * hid * (m + 1), :], down[hid * m : hid * (m + 1), :])
+        for m in range(2)
+    ]
+    h, terms = (jnp.concatenate(v, axis=1) for v in zip(*sides))
     for c in range(0, width, COLS):
         cut = slice(c, c + COLS)
         first[0, :, cut] = jnp.dot(h, down[:, cut], preferred_element_type=f32)
         first[1, :, cut] = jnp.dot(terms, gu[:, cut], preferred_element_type=f32)
-    shares = sum(
-        tail[i * CAP : (i + 1) * CAP, :].astype(f32) for i in range(mixed_h.shape[0])
-    )
-    usage[...] = jnp.concatenate(
-        [shares[0:1, :], shares[1:2, :] + shares[2:3, :] + shares[3:4, :]], axis=0
-    )
+    usage[...] = usage_of(tails[0]) + usage_of(tails[1])
+
+
+def expert_terms_body(mixed_h, saved_h, slab, h, terms, both, grads, gu, down, sems):
+    early, late = row_pairs(mixed_h, saved_h, both, grads)
+    gates, downs = slab_pairs((slab,), gu, down)
+    wait_all(started(sems, *early, *gates, *late, *downs))
+    h[...], terms[...] = terms_of(both, grads, gu[...], down[...])
 
 
 def expert_beside_body(
-    mixed_h, saved_h, first_h, slab0, slab1, out, both, grads, first, gu, down, sems
+    mixed_h, saved_h, slab0, slab1, h0, terms0, usage, first_h, out,
+    both, grads, tails, first, gu, down, sems,
 ):
-    rows, width = both.shape
+    width, hid = both.shape[1], down.shape[0] // 2
+    early, late = row_pairs(mixed_h, saved_h, both, grads)
     gates, downs = slab_pairs((slab0, slab1), gu, down)
-    pairs = row_blocks(mixed_h, 0, both) + gates
-    pairs.append((saved_h.at[:, 0:width], both.at[rows // 2 :, :]))
-    early = len(pairs)
-    copies = started(sems, *pairs, *row_blocks(mixed_h, CAP, grads), *downs, (first_h, first))
-    wait_all(copies[:early])
-    h, a, b = hidden_of(nt(both[...], gu[...]))
-    wait_all(copies[early:])
-    terms = hidden_grads(a, b, nt(grads[...], down[...]))
+    early += gates[1:] + late + downs[1:]
+    late = gates[:1] + downs[:1] + [(first_h, first)]
+    late += [(tail_of(w), tails.at[m]) for m, w in enumerate((slab0, slab1))]
+    copies = started(sems, *early, *late)
+    wait_all(copies[: len(early)])
+    h1, terms1 = terms_of(both, grads, gu[2 * hid :, :], down[hid:, :])
+    h = jnp.concatenate([h0[...], h1], axis=1)
+    terms = jnp.concatenate([terms0[...], terms1], axis=1)
+    wait_all(copies[len(early) :])
     for c in range(0, width, COLS):
         cut = slice(c, c + COLS)
         fwd = first[0, :, cut] + jnp.dot(h, down[:, cut], preferred_element_type=f32)
@@ -256,6 +293,11 @@
         for i in range(out.shape[0]):
             out[i, 0:CAP, cut] = fwd[i * CAP : (i + 1) * CAP, :].astype(bf16)
             out[i, CAP : 2 * CAP, cut] = bwd[i * CAP : (i + 1) * CAP, :].astype(bf16)
+    total = usage[...] + (usage_of(tails[0]) + usage_of(tails[1]))
+    rows = usage_rows(total[0:1, :], total[1:2, :])
+    for i in range(out.shape[0]):
+        out[i, 0:CAP, width:] = rows
+        out[i, CAP : 2 * CAP, width:] = jnp.zeros_like(rows)
 
 
 def placed(select_t, rows):
@@ -263,7 +305,7 @@
 
 
 def combine_body(
-    parts, columns_h, rows16_h, picked_h, gain_h, x_in, upstream, fwd_out, bwd_out,
+    parts, columns_h, rows16_h, picked_h, gain_h, x_in, upstream, fwd_out, bwd_out, balance,
     columns, rows16, picked, gain, sems,
 ):
     wait_all(
@@ -271,13 +313,14 @@
             sems, (columns_h, columns), (rows16_h, rows16), (picked_h, picked), (gain_h, gain)
         )
     )
-    half = parts.shape[0] // EXP_WIN
+    half, width = parts.shape[0] // EXP_WIN, x_in.shape[1]
 
     def summed(start):
         return jnp.concatenate(
             [
                 sum(
-                    parts[e * half + i, start : start + CAP, :].astype(f32) for i in range(half)
+                    parts[e * half + i, start : start + CAP, 0:width].astype(f32)
+                    for i in range(half)
                 )
                 for e in range(EXP_WIN)
             ],
@@ -291,6 +334,11 @@
     x = picked[...].astype(f32)
     rows = inv * weighted - x * (inv * inv * inv) * jnp.mean(x * weighted, axis=1, keepdims=True)
     bwd_out[...] = (upstream[...].astype(f32) + placed(columns[0, :, :], rows)).astype(bf16)
+    usage = usage_of(parts[0, 0:CAP, width:])
+    for i in range(1, parts.shape[0]):
+        usage = usage + usage_of(parts[i, 0:CAP, width:])
+    tokens_all = x_in.shape[0] * parts.shape[0] * PAIR_DEVICES
+    balance[...] = EXPERTS * (usage[0:1, :] / (tokens_all * TOPK)) * (usage[1:2, :] / tokens_all)
 
 
 def shifted(block, axis, distance):
@@ -311,59 +359,66 @@
     dma = pltpu.SemaphoreType.DMA
     upstream = shifted(bwd_sent[0], "section", -1)
     x_in = shifted(fwd_sent[0], "section", 1)
-    slab = jnp.concatenate([w_gate[0].T, w_up[0].T, w_down[0]], axis=0)
+    hid = w_down.shape[1]
+    saved_send, picked, columns, rows16, slab = kernel_call(
+        prepare_body,
+        (in_hbm((stops, CAP, width), bf16), in_hbm((SLOTS, width), bf16),
+         in_hbm((EXP_WIN, tokens, SLOTS), bf16), in_hbm((3, SLOTS, EXPERTS), f32),
+         in_hbm((3 * hid + CAP, width), bf16)),
+        [HBM] * 9, [VMEM] * 4 + [HBM],
+        [pltpu.VMEM((tokens, width), bf16), pltpu.VMEM((1, width), bf16),
+         pltpu.VMEM((TOPK, tokens), jnp.int32), pltpu.VMEM((tokens, EXPERTS), f32),
+         pltpu.VMEM((TOPK, tokens), jnp.int32), pltpu.VMEM((tokens, EXPERTS), f32),
+         pltpu.VMEM((CAP, EXPERTS), bf16), dma((10,))],
+        bwd_saved[0], norm_gain, bwd_routes[0].T, bwd_logits[0], fwd_routes[0].T, fwd_logits[0],
+        w_gate[0].T, w_up[0].T, w_down[0],
+    )
     slab_x = shifted(slab, "xl", 1)
     slab_core = shifted(slab, "core", 1)
-    saved_send, picked, columns, rows16 = kernel_call(
-        prepare_body,
-        (in_hbm((stops, CAP, width + EXPERTS), bf16), in_hbm((SLOTS, width), bf16),
-         in_hbm((EXP_WIN, tokens, SLOTS), bf16), in_hbm((3, SLOTS, EXPERTS), f32)),
-        [HBM] * 6, [VMEM] * 4,
-        [pltpu.VMEM((tokens, width), bf16), pltpu.VMEM((1, width), bf16),
-         pltpu.VMEM((TOPK, tokens), jnp.int32), pltpu.VMEM((tokens, EXPERTS), f32),
-         pltpu.VMEM((TOPK, tokens), jnp.int32), pltpu.VMEM((tokens, EXPERTS), f32), dma((6,))],
-        bwd_saved[0], norm_gain, bwd_routes[0].T, bwd_logits[0], fwd_routes[0].T, fwd_logits[0],
-    )
-    saved_all = over_y(saved_send).reshape(-1, width + EXPERTS)
+    saved_all = over_y(saved_send).reshape(-1, width)
     mixed_send = kernel_call(
         rows_body, in_hbm((stops, 2 * CAP, width), bf16), [VMEM, VMEM, HBM, HBM, HBM], VMEM,
         [pltpu.VMEM((EXP_WIN, tokens, SLOTS), bf16), pltpu.VMEM((SLOTS, EXPERTS), f32),
          pltpu.VMEM((1, width), bf16), dma((3,))],
-        x_in, upstream, columns, rows16, norm_gain,
+        x_in, upstream, columns, rows16, norm_gain, us=5,
     )
     mixed_all = over_y(mixed_send)
-    count, hid = stops * CAP, slab.shape[0] // 3
+    count = stops * CAP
     vmem = pltpu.VMEM
     both, grads = vmem((2 * count, width), bf16), vmem((count, width), bf16)
     gu, down = vmem((4 * hid, width), bf16), vmem((2 * hid, width), bf16)
+    tails = vmem((2, CAP, EXPERTS), bf16)
     sums = in_hbm((2, count, width), f32)
     first, usage = kernel_call(
         expert_own_body, (sums, in_hbm((2, EXPERTS), f32)), [HBM] * 4, [VMEM] * 2,
-        [both, grads, vmem((count, EXPERTS), bf16), gu, down, dma((2 * stops + 8,))],
-        mixed_all, saved_all, slab, slab_core,
+        [both, grads, tails, gu, down, dma((2 * stops + 8,))],
+        mixed_all, saved_all, slab, slab_core, us=2,
     )
     slab_x, first = lax.optimization_barrier((slab_x, first))
+    slab_x_core = shifted(slab_x, "core", 1)
+    h, terms = kernel_call(
+        expert_terms_body, (shape((count, hid), bf16), shape((count, 2 * hid), bf16)),
+        [HBM] * 3, [VMEM] * 2,
+        [both, grads, vmem((2 * hid, width), bf16), vmem((hid, width), bf16),
+         dma((2 * stops + 8,))],
+        mixed_all, saved_all, slab_x,
+    )
     result = kernel_call(
-        expert_beside_body, in_hbm((stops, 2 * CAP, width), bf16), [HBM] * 4 + [VMEM], VMEM,
-        [both, grads, vmem(sums.shape, f32), gu, down, dma((2 * stops + 8,))],
-        mixed_all, saved_all, first, slab_x, shifted(slab_x, "core", 1),
-    )
-    result, usage = lax.optimization_barrier((result, usage))
+        expert_beside_body, in_hbm((stops, 2 * CAP, width + EXPERTS), bf16),
+        [HBM] * 3 + [VMEM] * 4 + [HBM], VMEM,
+        [both, grads, tails, vmem(sums.shape, f32), gu, down, dma((2 * stops + 8,))],
+        mixed_all, saved_all, slab_x, slab_x_core, h, terms, usage, first,
+    )
     parts = over_y(result)
     full = in_hbm((tokens, width), bf16)
-    fwd_out, bwd_out = kernel_call(
-        combine_body, (full, full), [VMEM] + [HBM] * 4 + [VMEM] * 2, [VMEM] * 2,
+    fwd_out, bwd_out, balance = kernel_call(
+        combine_body, (full, full, in_hbm((1, EXPERTS), f32)), [VMEM] + [HBM] * 4 + [VMEM] * 2, [VMEM] * 3,
         [pltpu.VMEM(columns.shape, bf16),
          pltpu.VMEM(rows16.shape, f32), pltpu.VMEM(picked.shape, bf16),
          pltpu.VMEM((1, width), bf16), dma((4,))],
         parts, columns, rows16, picked, norm_gain, x_in, upstream,
     )
-    for axis in ("xl", "core"):
-        usage = usage + shifted(usage, axis, 1)
-    counts, prob_sums = usage
-    tokens_all = tokens * lax.axis_size(EXPERT_AXES)
-    balance = EXPERTS * (counts / (tokens_all * TOPK)) * (prob_sums / tokens_all)
-    return (fwd_out[None], bwd_out[None], balance[None])
+    return (fwd_out[None], bwd_out[None], balance)
 
 
 def solution(mesh):

time: 141 us -> 208 us (1.48)
  Pallas kernels: 21.3 us -> 94.2 us
  blocking collectives: 30.9 us -> 66.8 us
  waiting for transfers between devices: 39.9 us -> 14.8 us
  starting transfers between devices: 43.5 us -> 30.9 us
  other arithmetic: 3.81 us -> 0 us
    pallas_call x5 -> x6, Pallas kernels: 21.3 us -> 94.2 us  [kernel_call(): pl.pallas_call(body, out_shape=outs, in_specs=in_specs, out_specs=out_spe...]
    all_to_all x1 -> x2, blocking collectives: 30.9 us -> 66.8 us  [over_y(): return lax.all_to_all(block, 'y', split_axis=0, concat_axis=0, tiled=True)]
    all_to_all x2 -> x1, waiting for transfers between devices: 26.4 us -> 9.47 us  [over_y(): return lax.all_to_all(block, 'y', split_axis=0, concat_axis=0, tiled=True)]
    ppermute x7 -> x5, waiting for transfers between devices: 13.6 us -> 5.3 us  [shifted(): lax.ppermute(block, axis, [((i - distance) % n, i) for i in range(n)])]
    all_to_all x2 -> x1, starting transfers between devices: 13.8 us -> 6.83 us  [over_y(): return lax.all_to_all(block, 'y', split_axis=0, concat_axis=0, tiled=True)]
    ppermute x7 -> x5, starting transfers between devices: 29.7 us -> 24.1 us  [shifted(): lax.ppermute(block, axis, [((i - distance) % n, i) for i in range(n)])]
    concatenate x1 -> x0, other arithmetic: 3.28 us -> none  [body(): slab = jnp.concatenate([w_gate[0].T, w_up[0].T, w_down[0]], axis=0)]
  transfers between devices with their start and end apart: 9 -> 6, of which waited for: 6 -> 3; matrix products, arithmetic and copies ran while one was open for 3% -> 0% of each run, Pallas kernels for 9% -> 42%
where the time goes in v5:
time: 208 us; the launch traced here: 207 us
  Pallas kernels  94.2 us (45%)
  blocking collectives  66.8 us (32%)
  starting transfers between devices  30.9 us (15%)
  waiting for transfers between devices  14.8 us (7%)
    pallas_call x6, Pallas kernels, kernel_call(): pl.pallas_call(body, out_shape=outs, in_specs=in_specs, out_specs=out_spe...  94.2 us
    all_to_all x2, blocking collectives, over_y(): return lax.all_to_all(block, 'y', split_axis=0, concat_axis=0, tiled=True)  66.8 us
    ppermute x5, starting transfers between devices, shifted(): lax.ppermute(block, axis, [((i - distance) % n, i) for i in range(n)])  24.1 us
    all_to_all x1, waiting for transfers between devices, over_y(): return lax.all_to_all(block, 'y', split_axis=0, concat_axis=0, tiled=True)  9.47 us
    all_to_all x1, starting transfers between devices, over_y(): return lax.all_to_all(block, 'y', split_axis=0, concat_axis=0, tiled=True)  6.83 us
    ppermute x5, waiting for transfers between devices, shifted(): lax.ppermute(block, axis, [((i - distance) % n, i) for i in range(n)])  5.3 us
  transfers between devices with their start and end apart: 6, of which 3 were waited for; matrix products, arithmetic and copies ran while one was open for 0% of the time, Pallas kernels for 42%

profile of v5, /device:TPU:1, one launch (start us, length us, event | category | flops | bytes accessed | tf_op | source)
XLA Modules:
  0.0 207.4 jit_solution(12786121422588008313)
XLA Ops:
  0.6 5.5 %collective-permute-start = (bf16[64,4096]{1,0:T(8,128)(2,1)}, bf16[64,4096]{1,0:T(8,128)(2,1)S(1)}, u32[]{:S(2)}, u32[]{:S(2)}) collective-permute-start(bf16[64,4096]{1,0:T(8,128)(2,1)} %bitcast.25), channel_id=1, source_target_pairs={{480,0},{0,32},{32,64},{64,96},{96,128},{128,160},{160,192},{192,2... | collective-permute-start | bytes 1572872 | tf_op jit(solution)/shard_map/ppermute | solution.py:346
  6.1 10.4 %collective-permute-start.1 = (bf16[64,4096]{1,0:T(8,128)(2,1)}, bf16[64,4096]{1,0:T(8,128)(2,1)S(1)}, u32[]{:S(2)}, u32[]{:S(2)}) collective-permute-start(bf16[64,4096]{1,0:T(8,128)(2,1)} %bitcast.26), channel_id=1, source_target_pairs={{32,0},{64,32},{96,64},{128,96},{160,128},{192,160},{224,192},{256... | collective-permute-start | bytes 1572872 | tf_op jit(solution)/shard_map/ppermute | solution.py:346
  16.5 73.5 %shard_map.130 = (bf16[8,8,4096]{2,1,0:T(8,128)(2,1)}, bf16[16,4096]{1,0:T(8,128)(2,1)}, bf16[2,64,16]{2,1,0:T(8,128)(2,1)}, f32[3,16,128]{2,1,0:T(8,128)}, bf16[296,4096]{1,0:T(8,128)(2,1)}) custom-call(bf16[64,4096]{1,0:T(8,128)(2,1)} %bitcast.24, bf16[1,4096]{1,0:T(2,128)(2,1)} %gain_h.5, s32[8,64]{1,0:T(8,128)} %bitcast.29, f32[64,128]{1,0:T(8,128)} %bitcast.27, ...), custom_call_target="tpu_custom_call" | custom-call | flops 2000000000 | tf_op jit(solution)/shard_map/pallas_call | solution.py:83
  90.0 6.8 %all-to-all-start.1 = ((bf16[8,8,4096]{2,1,0:T(8,128)(2,1)}), bf16[8,8,4096]{2,1,0:T(8,128)(2,1)}, u32[]{:S(2)}, u32[]{:S(2)}) async-start(bf16[8,8,4096]{2,1,0:T(8,128)(2,1)} %get-tuple-element.19), calls=%async_computation.1 | async-start | bytes 1048576 | tf_op jit(solution)/shard_map/all_to_all | solution.py:350
  96.9 3.1 %collective-permute-start.3 = (bf16[296,4096]{1,0:T(8,128)(2,1)}, bf16[296,4096]{1,0:T(8,128)(2,1)}, u32[]{:S(2)}, u32[]{:S(2)}) collective-permute-start(bf16[296,4096]{1,0:T(8,128)(2,1)} %get-tuple-element.20.slab0), channel_id=1, source_target_pairs={{1,0},{0,1},{3,2},{2,3},{5,4},{4,5},{7,6},{6,7},{9,8},{8,9},{11,10... | collective-permute-start | bytes 7274504 | tf_op jit(solution)/shard_map/ppermute | solution.py:346
  100.0 2.2 %collective-permute-start.2 = (bf16[296,4096]{1,0:T(8,128)(2,1)}, bf16[296,4096]{1,0:T(8,128)(2,1)S(1)}, u32[]{:S(2)}, u32[]{:S(2)}) collective-permute-start(bf16[296,4096]{1,0:T(8,128)(2,1)} %get-tuple-element.20.slab0), channel_id=1, source_target_pairs={{2,0},{0,2},{3,1},{1,3},{6,4},{4,6},{7,5},{5,7},{10,8},{8,10},{11,... | collective-permute-start | bytes 7274504 | tf_op jit(solution)/shard_map/ppermute | solution.py:346
  102.2 0.0 collective-permute-done.x_in
  102.3 0.0 collective-permute-done.1.upstream
  102.3 2.3 %shard_map.131 = bf16[8,16,4096]{2,1,0:T(8,128)(2,1)} custom-call(bf16[64,4096]{1,0:T(8,128)(2,1)S(1)} %collective-permute-done.x_in, bf16[64,4096]{1,0:T(8,128)(2,1)S(1)} %collective-permute-done.1.upstream, bf16[2,64,16]{2,1,0:T(8,128)(2,1)} %get-tuple-element.17.columns_h, f32[3,16,128]{2,1,0:T(8,128)} %get-tuple-element.18.rows16_h, bf16[1,4096]{1,0:T(2,128)(2,1)} %gain_h.5), custom_call_target="tpu_custom_call" | custom-call | flops 5000000000 | tf_op jit(solution)/shard_map/pallas_call | solution.py:83
  104.5 9.5 %all-to-all-done.1 = bf16[8,8,4096]{2,1,0:T(8,128)(2,1)} async-done(((bf16[8,8,4096]{2,1,0:T(8,128)(2,1)}), bf16[8,8,4096]{2,1,0:T(8,128)(2,1)}, u32[]{:S(2)}, u32[]{:S(2)}) %all-to-all-start.1) | async-done | bytes 524320 | tf_op jit(solution)/shard_map/all_to_all | solution.py:350
  114.0 30.9 %all_to_all.15.mixed_h = bf16[8,16,4096]{2,1,0:T(8,128)(2,1)} all-to-all(bf16[8,16,4096]{2,1,0:T(8,128)(2,1)} %shard_map.131), channel_id=1, replica_groups=mesh['section'=16,'y'=8,'xl'=2,'core'=2] {'y'}, dimensions={0} | all-to-all | bytes 2097152 | tf_op jit(solution)/shard_map/all_to_all | solution.py:350
  144.9 0.0 collective-permute-done.3.slab1
  144.9 7.1 %shard_map.132 = (f32[2,64,4096]{2,1,0:T(8,128)}, f32[2,128]{1,0:T(2,128)}) custom-call(bf16[8,16,4096]{2,1,0:T(8,128)(2,1)} %all_to_all.15.mixed_h, bf16[64,4096]{1,0:T(8,128)(2,1)} %bitcast.14.saved_h, bf16[296,4096]{1,0:T(8,128)(2,1)} %get-tuple-element.20.slab0, bf16[296,4096]{1,0:T(8,128)(2,1)} %collective-permute-done.3.slab1), custom_call_target="tpu_custom_call" | custom-call | flops 2000000000 | tf_op jit(solution)/shard_map/pallas_call | solution.py:83
  152.0 4.4 %collective-permute-done.2.slab.slab0 = bf16[296,4096]{1,0:T(8,128)(2,1)S(1)} collective-permute-done((bf16[296,4096]{1,0:T(8,128)(2,1)}, bf16[296,4096]{1,0:T(8,128)(2,1)S(1)}, u32[]{:S(2)}, u32[]{:S(2)}) %collective-permute-start.2) | collective-permute-done | bytes 2424864 | tf_op jit(solution)/shard_map/ppermute | solution.py:346
  156.4 0.0 copy-start.1
  156.4 0.0 copy-start
  156.4 2.8 %collective-permute-start.4 = (bf16[296,4096]{1,0:T(8,128)(2,1)S(1)}, bf16[296,4096]{1,0:T(8,128)(2,1)S(1)}, u32[]{:S(2)}, u32[]{:S(2)}) collective-permute-start(bf16[296,4096]{1,0:T(8,128)(2,1)S(1)} %collective-permute-done.2.slab.slab0), channel_id=1, source_target_pairs={{1,0},{0,1},{3,2},{2,3},{5,4},{4,5},{7,6},{6,7},{9,8},{8,9},{11,10... | collective-permute-start | bytes 7274504 | tf_op jit(solution)/shard_map/ppermute | solution.py:346
  159.2 0.0 copy-done.1
  159.2 3.3 %shard_map.133 = (bf16[64,96]{1,0:T(8,128)(2,1)S(1)}, bf16[64,192]{1,0:T(8,128)(2,1)S(1)}) custom-call(bf16[8,16,4096]{2,1,0:T(8,128)(2,1)} %all_to_all.15.mixed_h, bf16[64,4096]{1,0:T(8,128)(2,1)} %bitcast.14.saved_h, bf16[296,4096]{1,0:T(8,128)(2,1)} %copy-done.1), custom_call_target="tpu_custom_call" | custom-call | flops 2000000000 | tf_op jit(solution)/shard_map/pallas_call | solution.py:83
  162.6 0.9 collective-permute-done.4.slab1
  163.5 0.0 copy-done
  163.5 5.2 %shard_map.134 = bf16[8,16,4224]{2,1,0:T(8,128)(2,1)} custom-call(bf16[8,16,4096]{2,1,0:T(8,128)(2,1)} %all_to_all.15.mixed_h, bf16[64,4096]{1,0:T(8,128)(2,1)} %bitcast.14.saved_h, bf16[296,4096]{1,0:T(8,128)(2,1)} %copy-done.1, bf16[296,4096]{1,0:T(8,128)(2,1)S(1)} %collective-permute-done.4.slab1, bf16[64,96]{1,0:T(8,128)(2,1)S(1)} %get-tuple-element.23.h0, ...), custom_call_target="tpu_custom_call" | custom-call | flops 2000000000 | tf_op jit(solution)/shard_map/pallas_call | solution.py:83
  168.6 35.9 %all_to_all.16.parts = bf16[8,16,4224]{2,1,0:T(8,128)(2,1)S(1)} all-to-all(bf16[8,16,4224]{2,1,0:T(8,128)(2,1)} %shard_map.134), channel_id=1, replica_groups=mesh['section'=16,'y'=8,'xl'=2,'core'=2] {'y'}, dimensions={0} | all-to-all | bytes 2162688 | tf_op jit(solution)/shard_map/all_to_all | solution.py:350
  204.5 2.9 %shard_map.135 = (bf16[64,4096]{1,0:T(8,128)(2,1)}, bf16[64,4096]{1,0:T(8,128)(2,1)}, f32[1,128]{1,0:T(1,128)}) custom-call(bf16[8,16,4224]{2,1,0:T(8,128)(2,1)S(1)} %all_to_all.16.parts, bf16[2,64,16]{2,1,0:T(8,128)(2,1)} %get-tuple-element.17.columns_h, f32[3,16,128]{2,1,0:T(8,128)} %get-tuple-element.18.rows16_h, ...), custom_call_target="tpu_custom_call" | custom-call | flops 2000000000 | tf_op jit(solution)/shard_map/pallas_call | solution.py:83
Async XLA Ops:
  0.6 101.6 %collective-permute-start = (bf16[64,4096]{1,0:T(8,128)(2,1)}, bf16[64,4096]{1,0:T(8,128)(2,1)S(1)}, u32[]{:S(2)}, u32[]{:S(2)}) collective-permute-start(bf16[64,4096]{1,0:T(8,128)(2,1)} %bitcast.25), channel_id=1, source_target_pairs={{480,0},{0,32},{32,64},{64,96},{96,128},{128,160},{160,192},{192,2... | collective-permute-start | bytes 1572872 | tf_op jit(solution)/shard_map/ppermute | solution.py:346
  6.1 96.1 %collective-permute-start.1 = (bf16[64,4096]{1,0:T(8,128)(2,1)}, bf16[64,4096]{1,0:T(8,128)(2,1)S(1)}, u32[]{:S(2)}, u32[]{:S(2)}) collective-permute-start(bf16[64,4096]{1,0:T(8,128)(2,1)} %bitcast.26), channel_id=1, source_target_pairs={{32,0},{64,32},{96,64},{128,96},{160,128},{192,160},{224,192},{256... | collective-permute-start | bytes 1572872 | tf_op jit(solution)/shard_map/ppermute | solution.py:346
  90.0 24.0 %all-to-all-start.1 = ((bf16[8,8,4096]{2,1,0:T(8,128)(2,1)}), bf16[8,8,4096]{2,1,0:T(8,128)(2,1)}, u32[]{:S(2)}, u32[]{:S(2)}) async-start(bf16[8,8,4096]{2,1,0:T(8,128)(2,1)} %get-tuple-element.19), calls=%async_computation.1 | async-start | bytes 1048576 | tf_op jit(solution)/shard_map/all_to_all | solution.py:350
  96.9 48.0 %collective-permute-start.3 = (bf16[296,4096]{1,0:T(8,128)(2,1)}, bf16[296,4096]{1,0:T(8,128)(2,1)}, u32[]{:S(2)}, u32[]{:S(2)}) collective-permute-start(bf16[296,4096]{1,0:T(8,128)(2,1)} %get-tuple-element.20.slab0), channel_id=1, source_target_pairs={{1,0},{0,1},{3,2},{2,3},{5,4},{4,5},{7,6},{6,7},{9,8},{8,9},{11,10... | collective-permute-start | bytes 7274504 | tf_op jit(solution)/shard_map/ppermute | solution.py:346
  100.0 56.4 %collective-permute-start.2 = (bf16[296,4096]{1,0:T(8,128)(2,1)}, bf16[296,4096]{1,0:T(8,128)(2,1)S(1)}, u32[]{:S(2)}, u32[]{:S(2)}) collective-permute-start(bf16[296,4096]{1,0:T(8,128)(2,1)} %get-tuple-element.20.slab0), channel_id=1, source_target_pairs={{2,0},{0,2},{3,1},{1,3},{6,4},{4,6},{7,5},{5,7},{10,8},{8,10},{11,... | collective-permute-start | bytes 7274504 | tf_op jit(solution)/shard_map/ppermute | solution.py:346
  156.4 2.8 %copy-start.1 = (bf16[296,4096]{1,0:T(8,128)(2,1)}, bf16[296,4096]{1,0:T(8,128)(2,1)S(1)}, u32[]{:S(2)}) copy-start(bf16[296,4096]{1,0:T(8,128)(2,1)S(1)} %collective-permute-done.2.slab.slab0) | copy-start | bytes 7274500
  156.4 7.1 %copy-start = (f32[2,128]{1,0:T(2,128)S(1)}, f32[2,128]{1,0:T(2,128)}, u32[]{:S(2)}) copy-start(f32[2,128]{1,0:T(2,128)} %get-tuple-element.25.usage) | copy-start | bytes 3076
  156.4 7.1 %collective-permute-start.4 = (bf16[296,4096]{1,0:T(8,128)(2,1)S(1)}, bf16[296,4096]{1,0:T(8,128)(2,1)S(1)}, u32[]{:S(2)}, u32[]{:S(2)}) collective-permute-start(bf16[296,4096]{1,0:T(8,128)(2,1)S(1)} %collective-permute-done.2.slab.slab0), channel_id=1, source_target_pairs={{1,0},{0,1},{3,2},{2,3},{5,4},{4,5},{7,6},{6,7},{9,8},{8,9},{11,10... | collective-permute-start | bytes 7274504 | tf_op jit(solution)/shard_map/ppermute | solution.py:346

commit v6 on v5

--- a/solution.py
+++ b/solution.py
@@ -15,7 +15,7 @@
 f32 = jnp.float32
 bf16 = jnp.bfloat16
 NT = (((1,), (1,)), ((), ()))
-PARAMS = pltpu.CompilerParams(vmem_limit_bytes=48 << 20)
+PARAMS = pltpu.CompilerParams(vmem_limit_bytes=32 << 20)
 EXPERT_AXES = ("y", "xl", "core")
 PAIR_DEVICES = 4
 
@@ -69,15 +69,21 @@
 
 HBM = pl.BlockSpec(memory_space=pltpu.HBM)
 VMEM = pl.BlockSpec(memory_space=pltpu.VMEM)
+PINNED = pl.BlockSpec(memory_space=pltpu.VMEM)
 
 
 def in_hbm(dims, dtype):
     return pltpu.HBM(dims, dtype)
 
 
+def in_vmem(dims, dtype):
+    return pltpu.VMEM(dims, dtype)
+
+
 def kernel_call(body, outs, in_specs, out_specs, scratch, *args, us=2):
     args = [
-        pltpu.with_memory_space_constraint(v, pltpu.HBM) if spec is HBM else v
+        v if spec is VMEM
+        else pltpu.with_memory_space_constraint(v, pltpu.HBM if spec is HBM else pltpu.VMEM)
         for v, spec in zip(args, in_specs)
     ]
     return pl.pallas_call(
@@ -128,14 +134,14 @@
 
 def prepare_body(
     saved_h, gain_h, broutes_h, blogits_h, froutes_h, flogits_h, gate_h, up_h, down_h,
-    send, picked, columns, rows16, slab_h,
-    saved, gain, broutes, blogits, froutes, flogits, usage, sems,
+    send, picked, columns, rows16, slab,
+    saved, gain, broutes, blogits, froutes, flogits, sems,
 ):
     hid = gate_h.shape[0]
     copies = started(
         sems, (broutes_h, broutes), (blogits_h, blogits), (froutes_h, froutes),
         (flogits_h, flogits), (gain_h, gain), (saved_h, saved),
-        *[(w, slab_h.at[m * hid : (m + 1) * hid, :]) for m, w in enumerate((gate_h, up_h, down_h))],
+        *[(w, slab.at[m * hid : (m + 1) * hid, :]) for m, w in enumerate((gate_h, up_h, down_h))],
     )
     wait_all(copies[:4])
     _, select, bselect_t, bgate = slot_tables(broutes[...], blogits[...])
@@ -143,13 +149,9 @@
     hot, _, fselect_t, fgate = slot_tables(froutes[...], logits)
     powers = jnp.exp(logits - jnp.max(logits, axis=1, keepdims=True))
     probs = powers / jnp.sum(powers, axis=1, keepdims=True)
-    usage[...] = usage_rows(
+    slab[3 * hid :, 0:EXPERTS] = usage_rows(
         jnp.sum(hot, axis=0, keepdims=True), jnp.sum(probs, axis=0, keepdims=True)
     )
-    last = pltpu.make_async_copy(
-        usage, slab_h.at[3 * hid : 3 * hid + CAP, 0:EXPERTS], sems.at[len(copies)]
-    )
-    last.start()
     wait_all(copies[4:6])
     rows = jnp.dot(select, saved[...], preferred_element_type=f32)
     normed, inverse = normed_rows(rows, gain[...].astype(f32))
@@ -162,7 +164,7 @@
     rows16[2, :, :] = jnp.broadcast_to(inverse, wide)
     for i, r in by_expert(send.shape[0]):
         send[i, :, :] = normed[r : r + CAP, :]
-    wait_all(copies[6:] + [last])
+    wait_all(copies[6:])
 
 
 def rows_body(x_in, upstream, columns_h, rows16_h, gain_h, send, columns, gates, gain, sems):
@@ -362,14 +364,13 @@
     hid = w_down.shape[1]
     saved_send, picked, columns, rows16, slab = kernel_call(
         prepare_body,
-        (in_hbm((stops, CAP, width), bf16), in_hbm((SLOTS, width), bf16),
+        (in_vmem((stops, CAP, width), bf16), in_hbm((SLOTS, width), bf16),
          in_hbm((EXP_WIN, tokens, SLOTS), bf16), in_hbm((3, SLOTS, EXPERTS), f32),
          in_hbm((3 * hid + CAP, width), bf16)),
-        [HBM] * 9, [VMEM] * 4 + [HBM],
+        [HBM] * 9, [VMEM] * 5,
         [pltpu.VMEM((tokens, width), bf16), pltpu.VMEM((1, width), bf16),
          pltpu.VMEM((TOPK, tokens), jnp.int32), pltpu.VMEM((tokens, EXPERTS), f32),
-         pltpu.VMEM((TOPK, tokens), jnp.int32), pltpu.VMEM((tokens, EXPERTS), f32),
-         pltpu.VMEM((CAP, EXPERTS), bf16), dma((10,))],
+         pltpu.VMEM((TOPK, tokens), jnp.int32), pltpu.VMEM((tokens, EXPERTS), f32), dma((9,))],
         bwd_saved[0], norm_gain, bwd_routes[0].T, bwd_logits[0], fwd_routes[0].T, fwd_logits[0],
         w_gate[0].T, w_up[0].T, w_down[0],
     )
@@ -377,7 +378,7 @@
     slab_core = shifted(slab, "core", 1)
     saved_all = over_y(saved_send).reshape(-1, width)
     mixed_send = kernel_call(
-        rows_body, in_hbm((stops, 2 * CAP, width), bf16), [VMEM, VMEM, HBM, HBM, HBM], VMEM,
+        rows_body, in_vmem((stops, 2 * CAP, width), bf16), [VMEM, VMEM, HBM, HBM, HBM], VMEM,
         [pltpu.VMEM((EXP_WIN, tokens, SLOTS), bf16), pltpu.VMEM((SLOTS, EXPERTS), f32),
          pltpu.VMEM((1, width), bf16), dma((3,))],
         x_in, upstream, columns, rows16, norm_gain, us=5,
@@ -390,7 +391,7 @@
     tails = vmem((2, CAP, EXPERTS), bf16)
     sums = in_hbm((2, count, width), f32)
     first, usage = kernel_call(
-        expert_own_body, (sums, in_hbm((2, EXPERTS), f32)), [HBM] * 4, [VMEM] * 2,
+        expert_own_body, (sums, in_hbm((2, EXPERTS), f32)), [PINNED, PINNED, HBM, HBM], [VMEM] * 2,
         [both, grads, tails, gu, down, dma((2 * stops + 8,))],
         mixed_all, saved_all, slab, slab_core, us=2,
     )
@@ -398,14 +399,14 @@
     slab_x_core = shifted(slab_x, "core", 1)
     h, terms = kernel_call(
         expert_terms_body, (shape((count, hid), bf16), shape((count, 2 * hid), bf16)),
-        [HBM] * 3, [VMEM] * 2,
+        [PINNED, PINNED, HBM], [VMEM] * 2,
         [both, grads, vmem((2 * hid, width), bf16), vmem((hid, width), bf16),
          dma((2 * stops + 8,))],
         mixed_all, saved_all, slab_x,
     )
     result = kernel_call(
-        expert_beside_body, in_hbm((stops, 2 * CAP, width + EXPERTS), bf16),
-        [HBM] * 3 + [VMEM] * 4 + [HBM], VMEM,
+        expert_beside_body, in_vmem((stops, 2 * CAP, width + EXPERTS), bf16),
+        [PINNED, PINNED, HBM] + [VMEM] * 4 + [HBM], VMEM,
         [both, grads, tails, vmem(sums.shape, f32), gu, down, dma((2 * stops + 8,))],
         mixed_all, saved_all, slab_x, slab_x_core, h, terms, usage, first,
     )

time: 208 us -> 138 us (0.66)
  Pallas kernels: 94.2 us -> 24.1 us
  waiting for transfers between devices: 14.8 us -> 17.2 us
  blocking collectives: 66.8 us -> 64.7 us
    pallas_call x6, Pallas kernels: 94.2 us -> 24.1 us  [kernel_call(): pl.pallas_call(body, out_shape=outs, in_specs=in_specs, out_specs=out_spe...]
  transfers between devices with their start and end apart: 6 -> 6, of which waited for: 3 -> 3; matrix products, arithmetic and copies ran while one was open for 0% -> 0% of each run, Pallas kernels for 42% -> 12%
where the time goes in v6:
time: 138 us
  blocking collectives  64.7 us (47%)
  starting transfers between devices  30.9 us (22%)
  Pallas kernels  24.1 us (17%)
  waiting for transfers between devices  17.2 us (12%)
    all_to_all x2, blocking collectives, over_y(): return lax.all_to_all(block, 'y', split_axis=0, concat_axis=0, tiled=True)  64.7 us
    ppermute x5, starting transfers between devices, shifted(): lax.ppermute(block, axis, [((i - distance) % n, i) for i in range(n)])  24.1 us
    pallas_call x6, Pallas kernels, kernel_call(): pl.pallas_call(body, out_shape=outs, in_specs=in_specs, out_specs=out_spe...  24.1 us
    all_to_all x1, waiting for transfers between devices, over_y(): return lax.all_to_all(block, 'y', split_axis=0, concat_axis=0, tiled=True)  10.4 us
    all_to_all x1, starting transfers between devices, over_y(): return lax.all_to_all(block, 'y', split_axis=0, concat_axis=0, tiled=True)  6.83 us
    ppermute x5, waiting for transfers between devices, shifted(): lax.ppermute(block, axis, [((i - distance) % n, i) for i in range(n)])  6.82 us
  transfers between devices with their start and end apart: 6, of which 3 were waited for; matrix products, arithmetic and copies ran while one was open for 0% of the time, Pallas kernels for 12%

profile of v6, /device:TPU:1, one launch (start us, length us, event | category | flops | bytes accessed | tf_op | source)
XLA Modules:
  0.0 137.6 jit_solution(3085392788633729080)
XLA Ops:
  0.6 5.5 %collective-permute-start = (bf16[64,4096]{1,0:T(8,128)(2,1)}, bf16[64,4096]{1,0:T(8,128)(2,1)S(1)}, u32[]{:S(2)}, u32[]{:S(2)}) collective-permute-start(bf16[64,4096]{1,0:T(8,128)(2,1)} %bitcast.28), channel_id=1, source_target_pairs={{480,0},{0,32},{32,64},{64,96},{96,128},{128,160},{160,192},{192,2... | collective-permute-start | bytes 1572872 | tf_op jit(solution)/shard_map/ppermute | solution.py:348
  6.1 10.4 %collective-permute-start.1 = (bf16[64,4096]{1,0:T(8,128)(2,1)}, bf16[64,4096]{1,0:T(8,128)(2,1)S(1)}, u32[]{:S(2)}, u32[]{:S(2)}) collective-permute-start(bf16[64,4096]{1,0:T(8,128)(2,1)} %bitcast.29), channel_id=1, source_target_pairs={{32,0},{64,32},{96,64},{128,96},{160,128},{192,160},{224,192},{256... | collective-permute-start | bytes 1572872 | tf_op jit(solution)/shard_map/ppermute | solution.py:348
  16.5 3.7 %shard_map.130 = (bf16[8,8,4096]{2,1,0:T(8,128)(2,1)}, bf16[16,4096]{1,0:T(8,128)(2,1)}, bf16[2,64,16]{2,1,0:T(8,128)(2,1)}, f32[3,16,128]{2,1,0:T(8,128)}, bf16[296,4096]{1,0:T(8,128)(2,1)}) custom-call(bf16[64,4096]{1,0:T(8,128)(2,1)} %bitcast.27, bf16[1,4096]{1,0:T(2,128)(2,1)} %gain_h.5, s32[8,64]{1,0:T(8,128)} %bitcast.32, f32[64,128]{1,0:T(8,128)} %bitcast.30, ...), custom_call_target="tpu_custom_call" | custom-call | flops 2000000000 | tf_op jit(solution)/shard_map/pallas_call | solution.py:89
  20.2 6.8 %all-to-all-start.1 = ((bf16[8,8,4096]{2,1,0:T(8,128)(2,1)}), bf16[8,8,4096]{2,1,0:T(8,128)(2,1)S(1)}, u32[]{:S(2)}, u32[]{:S(2)}) async-start(bf16[8,8,4096]{2,1,0:T(8,128)(2,1)} %get-tuple-element.19), calls=%async_computation.1 | async-start | bytes 1048576 | tf_op jit(solution)/shard_map/all_to_all | solution.py:352
  27.0 3.1 %collective-permute-start.3 = (bf16[296,4096]{1,0:T(8,128)(2,1)}, bf16[296,4096]{1,0:T(8,128)(2,1)}, u32[]{:S(2)}, u32[]{:S(2)}) collective-permute-start(bf16[296,4096]{1,0:T(8,128)(2,1)} %get-tuple-element.20.slab0), channel_id=1, source_target_pairs={{1,0},{0,1},{3,2},{2,3},{5,4},{4,5},{7,6},{6,7},{9,8},{8,9},{11,10... | collective-permute-start | bytes 7274504 | tf_op jit(solution)/shard_map/ppermute | solution.py:348
  30.2 2.2 %collective-permute-start.2 = (bf16[296,4096]{1,0:T(8,128)(2,1)}, bf16[296,4096]{1,0:T(8,128)(2,1)}, u32[]{:S(2)}, u32[]{:S(2)}) collective-permute-start(bf16[296,4096]{1,0:T(8,128)(2,1)} %get-tuple-element.20.slab0), channel_id=1, source_target_pairs={{2,0},{0,2},{3,1},{1,3},{6,4},{4,6},{7,5},{5,7},{10,8},{8,10},{11,... | collective-permute-start | bytes 7274504 | tf_op jit(solution)/shard_map/ppermute | solution.py:348
  32.4 0.0 collective-permute-done.x_in
  32.4 0.0 collective-permute-done.1.upstream
  32.4 1.3 shard_map.131
  33.7 10.4 %all-to-all-done.1 = bf16[8,8,4096]{2,1,0:T(8,128)(2,1)S(1)} async-done(((bf16[8,8,4096]{2,1,0:T(8,128)(2,1)}), bf16[8,8,4096]{2,1,0:T(8,128)(2,1)S(1)}, u32[]{:S(2)}, u32[]{:S(2)}) %all-to-all-start.1) | async-done | bytes 524320 | tf_op jit(solution)/shard_map/all_to_all | solution.py:352
  44.1 29.0 %all_to_all.15.mixed_h = bf16[8,16,4096]{2,1,0:T(8,128)(2,1)S(1)} all-to-all(bf16[8,16,4096]{2,1,0:T(8,128)(2,1)S(1)} %shard_map.131), channel_id=1, replica_groups=mesh['section'=16,'y'=8,'xl'=2,'core'=2] {'y'}, dimensions={0} | all-to-all | bytes 2097152 | tf_op jit(solution)/shard_map/all_to_all | solution.py:352
  73.1 0.0 collective-permute-done.3.slab1
  73.1 7.4 %shard_map.132 = (f32[2,64,4096]{2,1,0:T(8,128)}, f32[2,128]{1,0:T(2,128)}) custom-call(bf16[8,16,4096]{2,1,0:T(8,128)(2,1)S(1)} %all_to_all.15.mixed_h, bf16[64,4096]{1,0:T(8,128)(2,1)S(1)} %bitcast.21, bf16[296,4096]{1,0:T(8,128)(2,1)} %get-tuple-element.20.slab0, bf16[296,4096]{1,0:T(8,128)(2,1)} %collective-permute-done.3.slab1), custom_call_target="tpu_custom_call" | custom-call | flops 2000000000 | tf_op jit(solution)/shard_map/pallas_call | solution.py:89
  80.5 6.1 %collective-permute-done.2.slab.slab0 = bf16[296,4096]{1,0:T(8,128)(2,1)} collective-permute-done((bf16[296,4096]{1,0:T(8,128)(2,1)}, bf16[296,4096]{1,0:T(8,128)(2,1)}, u32[]{:S(2)}, u32[]{:S(2)}) %collective-permute-start.2) | collective-permute-done | bytes 2424864 | tf_op jit(solution)/shard_map/ppermute | solution.py:348
  86.7 0.0 copy-start
  86.7 2.8 %collective-permute-start.4 = (bf16[296,4096]{1,0:T(8,128)(2,1)}, bf16[296,4096]{1,0:T(8,128)(2,1)S(1)}, u32[]{:S(2)}, u32[]{:S(2)}) collective-permute-start(bf16[296,4096]{1,0:T(8,128)(2,1)} %collective-permute-done.2.slab.slab0), channel_id=1, source_target_pairs={{1,0},{0,1},{3,2},{2,3},{5,4},{4,5},{7,6},{6,7},{9,8},{8,9},{11,10... | collective-permute-start | bytes 7274504 | tf_op jit(solution)/shard_map/ppermute | solution.py:348
  89.5 3.8 %shard_map.133 = (bf16[64,96]{1,0:T(8,128)(2,1)S(1)}, bf16[64,192]{1,0:T(8,128)(2,1)S(1)}) custom-call(bf16[8,16,4096]{2,1,0:T(8,128)(2,1)S(1)} %all_to_all.15.mixed_h, bf16[64,4096]{1,0:T(8,128)(2,1)S(1)} %bitcast.22, bf16[296,4096]{1,0:T(8,128)(2,1)} %collective-permute-done.2.slab.slab0), custom_call_target="tpu_custom_call" | custom-call | flops 2000000000 | tf_op jit(solution)/shard_map/pallas_call | solution.py:89
  93.3 0.7 collective-permute-done.4.slab1
  93.9 0.0 copy-done
  93.9 5.1 %shard_map.134 = bf16[8,16,4224]{2,1,0:T(8,128)(2,1)S(1)} custom-call(bf16[8,16,4096]{2,1,0:T(8,128)(2,1)S(1)} %all_to_all.15.mixed_h, bf16[64,4096]{1,0:T(8,128)(2,1)S(1)} %bitcast.23, bf16[296,4096]{1,0:T(8,128)(2,1)} %collective-permute-done.2.slab.slab0, bf16[296,4096]{1,0:T(8,128)(2,1)S(1)} %collective-permute-done.4.slab1, ...), custom_call_target="tpu_custom_call" | custom-call | flops 2000000000 | tf_op jit(solution)/shard_map/pallas_call | solution.py:89
  99.0 35.7 %all_to_all.16.parts = bf16[8,16,4224]{2,1,0:T(8,128)(2,1)S(1)} all-to-all(bf16[8,16,4224]{2,1,0:T(8,128)(2,1)S(1)} %shard_map.134), channel_id=1, replica_groups=mesh['section'=16,'y'=8,'xl'=2,'core'=2] {'y'}, dimensions={0} | all-to-all | bytes 2162688 | tf_op jit(solution)/shard_map/all_to_all | solution.py:352
  134.7 2.9 %shard_map.135 = (bf16[64,4096]{1,0:T(8,128)(2,1)}, bf16[64,4096]{1,0:T(8,128)(2,1)}, f32[1,128]{1,0:T(1,128)}) custom-call(bf16[8,16,4224]{2,1,0:T(8,128)(2,1)S(1)} %all_to_all.16.parts, bf16[2,64,16]{2,1,0:T(8,128)(2,1)} %get-tuple-element.17.columns_h, f32[3,16,128]{2,1,0:T(8,128)} %get-tuple-element.18.rows16_h, ...), custom_call_target="tpu_custom_call" | custom-call | flops 2000000000 | tf_op jit(solution)/shard_map/pallas_call | solution.py:89
Async XLA Ops:
  0.6 31.8 %collective-permute-start = (bf16[64,4096]{1,0:T(8,128)(2,1)}, bf16[64,4096]{1,0:T(8,128)(2,1)S(1)}, u32[]{:S(2)}, u32[]{:S(2)}) collective-permute-start(bf16[64,4096]{1,0:T(8,128)(2,1)} %bitcast.28), channel_id=1, source_target_pairs={{480,0},{0,32},{32,64},{64,96},{96,128},{128,160},{160,192},{192,2... | collective-permute-start | bytes 1572872 | tf_op jit(solution)/shard_map/ppermute | solution.py:348
  6.1 26.3 %collective-permute-start.1 = (bf16[64,4096]{1,0:T(8,128)(2,1)}, bf16[64,4096]{1,0:T(8,128)(2,1)S(1)}, u32[]{:S(2)}, u32[]{:S(2)}) collective-permute-start(bf16[64,4096]{1,0:T(8,128)(2,1)} %bitcast.29), channel_id=1, source_target_pairs={{32,0},{64,32},{96,64},{128,96},{160,128},{192,160},{224,192},{256... | collective-permute-start | bytes 1572872 | tf_op jit(solution)/shard_map/ppermute | solution.py:348
  20.2 23.9 %all-to-all-start.1 = ((bf16[8,8,4096]{2,1,0:T(8,128)(2,1)}), bf16[8,8,4096]{2,1,0:T(8,128)(2,1)S(1)}, u32[]{:S(2)}, u32[]{:S(2)}) async-start(bf16[8,8,4096]{2,1,0:T(8,128)(2,1)} %get-tuple-element.19), calls=%async_computation.1 | async-start | bytes 1048576 | tf_op jit(solution)/shard_map/all_to_all | solution.py:352
  27.0 46.1 %collective-permute-start.3 = (bf16[296,4096]{1,0:T(8,128)(2,1)}, bf16[296,4096]{1,0:T(8,128)(2,1)}, u32[]{:S(2)}, u32[]{:S(2)}) collective-permute-start(bf16[296,4096]{1,0:T(8,128)(2,1)} %get-tuple-element.20.slab0), channel_id=1, source_target_pairs={{1,0},{0,1},{3,2},{2,3},{5,4},{4,5},{7,6},{6,7},{9,8},{8,9},{11,10... | collective-permute-start | bytes 7274504 | tf_op jit(solution)/shard_map/ppermute | solution.py:348
  30.2 56.5 %collective-permute-start.2 = (bf16[296,4096]{1,0:T(8,128)(2,1)}, bf16[296,4096]{1,0:T(8,128)(2,1)}, u32[]{:S(2)}, u32[]{:S(2)}) collective-permute-start(bf16[296,4096]{1,0:T(8,128)(2,1)} %get-tuple-element.20.slab0), channel_id=1, source_target_pairs={{2,0},{0,2},{3,1},{1,3},{6,4},{4,6},{7,5},{5,7},{10,8},{8,10},{11,... | collective-permute-start | bytes 7274504 | tf_op jit(solution)/shard_map/ppermute | solution.py:348
  86.7 7.3 %copy-start = (f32[2,128]{1,0:T(2,128)S(1)}, f32[2,128]{1,0:T(2,128)}, u32[]{:S(2)}) copy-start(f32[2,128]{1,0:T(2,128)} %get-tuple-element.25.usage) | copy-start | bytes 3076
  86.7 7.3 %collective-permute-start.4 = (bf16[296,4096]{1,0:T(8,128)(2,1)}, bf16[296,4096]{1,0:T(8,128)(2,1)S(1)}, u32[]{:S(2)}, u32[]{:S(2)}) collective-permute-start(bf16[296,4096]{1,0:T(8,128)(2,1)} %collective-permute-done.2.slab.slab0), channel_id=1, source_target_pairs={{1,0},{0,1},{3,2},{2,3},{5,4},{4,5},{7,6},{6,7},{9,8},{8,9},{11,10... | collective-permute-start | bytes 7274504 | tf_op jit(solution)/shard_map/ppermute | solution.py:348

commit v7 on v6

--- a/solution.py
+++ b/solution.py
@@ -167,9 +167,15 @@
     wait_all(copies[6:])
 
 
-def rows_body(x_in, upstream, columns_h, rows16_h, gain_h, send, columns, gates, gain, sems):
-    copies = started(sems, (columns_h, columns), (rows16_h.at[0], gates), (gain_h, gain))
-    copies[0].wait()
+def rows_body(
+    x_in_h, upstream_h, columns_h, rows16_h, gain_h, send,
+    columns, gates, gain, x_in, upstream, sems,
+):
+    copies = started(
+        sems, (columns_h, columns), (rows16_h.at[0], gates), (gain_h, gain), (x_in_h, x_in),
+        (upstream_h, upstream),
+    )
+    wait_all(copies)
 
     def chosen(i, block):
         return lax.dot_general(
@@ -178,7 +184,6 @@
 
     rows = chosen(1, x_in)
     grads = chosen(0, upstream)
-    wait_all(copies[1:])
     normed = normed_rows(rows, gain[...].astype(f32))[0]
     grads = (grads * gates[:, 0:1]).astype(bf16)
     for i, r in by_expert(send.shape[0]):
@@ -265,37 +270,30 @@
     usage[...] = usage_of(tails[0]) + usage_of(tails[1])
 
 
-def expert_terms_body(mixed_h, saved_h, slab, h, terms, both, grads, gu, down, sems):
-    early, late = row_pairs(mixed_h, saved_h, both, grads)
-    gates, downs = slab_pairs((slab,), gu, down)
-    wait_all(started(sems, *early, *gates, *late, *downs))
-    h[...], terms[...] = terms_of(both, grads, gu[...], down[...])
-
-
-def expert_beside_body(
-    mixed_h, saved_h, slab0, slab1, h0, terms0, usage, first_h, out,
-    both, grads, tails, first, gu, down, sems,
-):
-    width, hid = both.shape[1], down.shape[0] // 2
-    early, late = row_pairs(mixed_h, saved_h, both, grads)
-    gates, downs = slab_pairs((slab0, slab1), gu, down)
-    early += gates[1:] + late + downs[1:]
-    late = gates[:1] + downs[:1] + [(first_h, first)]
-    late += [(tail_of(w), tails.at[m]) for m, w in enumerate((slab0, slab1))]
-    copies = started(sems, *early, *late)
-    wait_all(copies[: len(early)])
-    h1, terms1 = terms_of(both, grads, gu[2 * hid :, :], down[hid:, :])
-    h = jnp.concatenate([h0[...], h1], axis=1)
-    terms = jnp.concatenate([terms0[...], terms1], axis=1)
-    wait_all(copies[len(early) :])
-    for c in range(0, width, COLS):
+def added(both, grads, slab, sums):
+    hid = (slab.shape[0] - CAP) // 3
+    h, terms = terms_of(both, grads, slab[0 : 2 * hid, :], slab[2 * hid : 3 * hid, :])
+    for c in range(0, both.shape[1], COLS):
         cut = slice(c, c + COLS)
-        fwd = first[0, :, cut] + jnp.dot(h, down[:, cut], preferred_element_type=f32)
-        bwd = first[1, :, cut] + jnp.dot(terms, gu[:, cut], preferred_element_type=f32)
+        fwd = jnp.dot(h, slab[2 * hid : 3 * hid, cut], preferred_element_type=f32)
+        bwd = jnp.dot(terms, slab[0 : 2 * hid, cut], preferred_element_type=f32)
+        yield cut, sums[0, :, cut] + fwd, sums[1, :, cut] + bwd
+
+
+def expert_beside_body(both, grads, slab, first, second):
+    for cut, fwd, bwd in added(both, grads, slab, first):
+        second[0, :, cut] = fwd
+        second[1, :, cut] = bwd
+
+
+def expert_last_body(both, grads, slab0, slab1, second, usage, out):
+    width = both.shape[1]
+    for cut, fwd, bwd in added(both, grads, slab1, second):
         for i in range(out.shape[0]):
             out[i, 0:CAP, cut] = fwd[i * CAP : (i + 1) * CAP, :].astype(bf16)
             out[i, CAP : 2 * CAP, cut] = bwd[i * CAP : (i + 1) * CAP, :].astype(bf16)
-    total = usage[...] + (usage_of(tails[0]) + usage_of(tails[1]))
+    beside = [usage_of(tail_of(w)[...]) for w in (slab0, slab1)]
+    total = usage[...] + (beside[0] + beside[1])
     rows = usage_rows(total[0:1, :], total[1:2, :])
     for i in range(out.shape[0]):
         out[i, 0:CAP, width:] = rows
@@ -303,18 +301,23 @@
 
 
 def placed(select_t, rows):
-    return sum(jnp.dot(select_t, p, preferred_element_type=f32) for p in in_parts(rows))
+    parts = in_parts(rows)
+    return jnp.dot(
+        jnp.concatenate([select_t] * len(parts), axis=1),
+        jnp.concatenate(parts, axis=0),
+        preferred_element_type=f32,
+    )
 
 
 def combine_body(
-    parts, columns_h, rows16_h, picked_h, gain_h, x_in, upstream, fwd_out, bwd_out, balance,
-    columns, rows16, picked, gain, sems,
+    parts, columns_h, rows16_h, picked_h, gain_h, x_in_h, upstream_h, fwd_out, bwd_out, balance,
+    columns, rows16, picked, gain, x_in, upstream, sems,
 ):
-    wait_all(
-        started(
-            sems, (columns_h, columns), (rows16_h, rows16), (picked_h, picked), (gain_h, gain)
-        )
-    )
+    copies = started(
+        sems, (columns_h, columns), (rows16_h, rows16), (picked_h, picked), (gain_h, gain),
+        (x_in_h, x_in), (upstream_h, upstream),
+    )
+    wait_all(copies[:4])
     half, width = parts.shape[0] // EXP_WIN, x_in.shape[1]
 
     def summed(start):
@@ -330,6 +333,7 @@
         )
 
     rows = summed(0) * rows16[1, :, 0:1]
+    wait_all(copies[4:])
     fwd_out[...] = (x_in[...].astype(f32) + placed(columns[1, :, :], rows)).astype(bf16)
     weighted = gain[...].astype(f32) * summed(CAP)
     inv = rows16[2, :, 0:1]
@@ -377,46 +381,43 @@
     slab_x = shifted(slab, "xl", 1)
     slab_core = shifted(slab, "core", 1)
     saved_all = over_y(saved_send).reshape(-1, width)
+    block = pltpu.VMEM((tokens, width), bf16)
     mixed_send = kernel_call(
-        rows_body, in_vmem((stops, 2 * CAP, width), bf16), [VMEM, VMEM, HBM, HBM, HBM], VMEM,
+        rows_body, in_vmem((stops, 2 * CAP, width), bf16), [HBM] * 5, VMEM,
         [pltpu.VMEM((EXP_WIN, tokens, SLOTS), bf16), pltpu.VMEM((SLOTS, EXPERTS), f32),
-         pltpu.VMEM((1, width), bf16), dma((3,))],
+         pltpu.VMEM((1, width), bf16), block, block, dma((5,))],
         x_in, upstream, columns, rows16, norm_gain, us=5,
     )
     mixed_all = over_y(mixed_send)
     count = stops * CAP
     vmem = pltpu.VMEM
-    both, grads = vmem((2 * count, width), bf16), vmem((count, width), bf16)
-    gu, down = vmem((4 * hid, width), bf16), vmem((2 * hid, width), bf16)
-    tails = vmem((2, CAP, EXPERTS), bf16)
-    sums = in_hbm((2, count, width), f32)
-    first, usage = kernel_call(
-        expert_own_body, (sums, in_hbm((2, EXPERTS), f32)), [PINNED, PINNED, HBM, HBM], [VMEM] * 2,
-        [both, grads, tails, gu, down, dma((2 * stops + 8,))],
+    sums = in_vmem((2, count, width), f32)
+    first, usage, both, grads = kernel_call(
+        expert_own_body,
+        (sums, in_hbm((2, EXPERTS), f32), in_vmem((2 * count, width), bf16),
+         in_vmem((count, width), bf16)),
+        [PINNED, PINNED, HBM, HBM], [VMEM] * 4,
+        [vmem((2, CAP, EXPERTS), bf16), vmem((4 * hid, width), bf16),
+         vmem((2 * hid, width), bf16), dma((2 * stops + 8,))],
         mixed_all, saved_all, slab, slab_core, us=2,
     )
     slab_x, first = lax.optimization_barrier((slab_x, first))
     slab_x_core = shifted(slab_x, "core", 1)
-    h, terms = kernel_call(
-        expert_terms_body, (shape((count, hid), bf16), shape((count, 2 * hid), bf16)),
-        [PINNED, PINNED, HBM], [VMEM] * 2,
-        [both, grads, vmem((2 * hid, width), bf16), vmem((hid, width), bf16),
-         dma((2 * stops + 8,))],
-        mixed_all, saved_all, slab_x,
+    second = kernel_call(
+        expert_beside_body, sums, [PINNED] * 4, VMEM, [], both, grads, slab_x, first
     )
     result = kernel_call(
-        expert_beside_body, in_vmem((stops, 2 * CAP, width + EXPERTS), bf16),
-        [PINNED, PINNED, HBM] + [VMEM] * 4 + [HBM], VMEM,
-        [both, grads, tails, vmem(sums.shape, f32), gu, down, dma((2 * stops + 8,))],
-        mixed_all, saved_all, slab_x, slab_x_core, h, terms, usage, first,
+        expert_last_body, in_vmem((stops, 2 * CAP, width + EXPERTS), bf16),
+        [PINNED] * 5 + [VMEM], VMEM, [],
+        both, grads, slab_x, slab_x_core, second, usage,
     )
     parts = over_y(result)
     full = in_hbm((tokens, width), bf16)
     fwd_out, bwd_out, balance = kernel_call(
-        combine_body, (full, full, in_hbm((1, EXPERTS), f32)), [VMEM] + [HBM] * 4 + [VMEM] * 2, [VMEM] * 3,
+        combine_body, (full, full, in_hbm((1, EXPERTS), f32)), [VMEM] + [HBM] * 6, [VMEM] * 3,
         [pltpu.VMEM(columns.shape, bf16),
          pltpu.VMEM(rows16.shape, f32), pltpu.VMEM(picked.shape, bf16),
-         pltpu.VMEM((1, width), bf16), dma((4,))],
+         pltpu.VMEM((1, width), bf16), block, block, dma((6,))],
         parts, columns, rows16, picked, norm_gain, x_in, upstream,
     )
     return (fwd_out[None], bwd_out[None], balance)

time: 138 us -> 134 us (0.971)
  Pallas kernels: 24.1 us -> 19.1 us
    pallas_call x6, Pallas kernels: 24.1 us -> 19.1 us  [kernel_call(): pl.pallas_call(body, out_shape=outs, in_specs=in_specs, out_specs=out_spe...]
    ppermute x5, waiting for transfers between devices: 6.82 us -> 8.32 us  [shifted(): lax.ppermute(block, axis, [((i - distance) % n, i) for i in range(n)])]
  transfers between devices with their start and end apart: 6 -> 6, of which waited for: 3 -> 3; matrix products, arithmetic and copies ran while one was open for 0% -> 0% of each run, Pallas kernels for 12% -> 11%
where the time goes in v7:
time: 134 us
  blocking collectives  64.7 us (48%)
  starting transfers between devices  30.8 us (23%)
  Pallas kernels  19.1 us (14%)
  waiting for transfers between devices  17.4 us (13%)
    all_to_all x2, blocking collectives, over_y(): return lax.all_to_all(block, 'y', split_axis=0, concat_axis=0, tiled=True)  64.7 us
    ppermute x5, starting transfers between devices, shifted(): lax.ppermute(block, axis, [((i - distance) % n, i) for i in range(n)])  23.9 us
    pallas_call x6, Pallas kernels, kernel_call(): pl.pallas_call(body, out_shape=outs, in_specs=in_specs, out_specs=out_spe...  19.1 us
    all_to_all x1, waiting for transfers between devices, over_y(): return lax.all_to_all(block, 'y', split_axis=0, concat_axis=0, tiled=True)  9.05 us
    ppermute x5, waiting for transfers between devices, shifted(): lax.ppermute(block, axis, [((i - distance) % n, i) for i in range(n)])  8.32 us
    all_to_all x1, starting transfers between devices, over_y(): return lax.all_to_all(block, 'y', split_axis=0, concat_axis=0, tiled=True)  6.83 us
  transfers between devices with their start and end apart: 6, of which 3 were waited for; matrix products, arithmetic and copies ran while one was open for 0% of the time, Pallas kernels for 11%

profile of v7, /device:TPU:1, one launch (start us, length us, event | category | flops | bytes accessed | tf_op | source)
XLA Modules:
  0.0 133.7 jit_solution(1202080512908711838)
XLA Ops:
  0.6 5.5 %collective-permute-start = (bf16[64,4096]{1,0:T(8,128)(2,1)}, bf16[64,4096]{1,0:T(8,128)(2,1)S(1)}, u32[]{:S(2)}, u32[]{:S(2)}) collective-permute-start(bf16[64,4096]{1,0:T(8,128)(2,1)} %bitcast.25), channel_id=1, source_target_pairs={{480,0},{0,32},{32,64},{64,96},{96,128},{128,160},{160,192},{192,2... | collective-permute-start | bytes 1572872 | tf_op jit(solution)/shard_map/ppermute | solution.py:352
  6.1 10.4 %collective-permute-start.1 = (bf16[64,4096]{1,0:T(8,128)(2,1)}, bf16[64,4096]{1,0:T(8,128)(2,1)S(1)}, u32[]{:S(2)}, u32[]{:S(2)}) collective-permute-start(bf16[64,4096]{1,0:T(8,128)(2,1)} %bitcast.26), channel_id=1, source_target_pairs={{32,0},{64,32},{96,64},{128,96},{160,128},{192,160},{224,192},{256... | collective-permute-start | bytes 1572872 | tf_op jit(solution)/shard_map/ppermute | solution.py:352
  16.5 3.7 %shard_map.130 = (bf16[8,8,4096]{2,1,0:T(8,128)(2,1)}, bf16[16,4096]{1,0:T(8,128)(2,1)}, bf16[2,64,16]{2,1,0:T(8,128)(2,1)}, f32[3,16,128]{2,1,0:T(8,128)}, bf16[296,4096]{1,0:T(8,128)(2,1)}) custom-call(bf16[64,4096]{1,0:T(8,128)(2,1)} %bitcast.24, bf16[1,4096]{1,0:T(2,128)(2,1)} %gain_h.5, s32[8,64]{1,0:T(8,128)} %bitcast.29, f32[64,128]{1,0:T(8,128)} %bitcast.27, ...), custom_call_target="tpu_custom_call" | custom-call | flops 2000000000 | tf_op jit(solution)/shard_map/pallas_call | solution.py:89
  20.2 6.8 %all-to-all-start.1 = ((bf16[8,8,4096]{2,1,0:T(8,128)(2,1)}), bf16[8,8,4096]{2,1,0:T(8,128)(2,1)}, u32[]{:S(2)}, u32[]{:S(2)}) async-start(bf16[8,8,4096]{2,1,0:T(8,128)(2,1)} %get-tuple-element.19), calls=%async_computation.1 | async-start | bytes 1048576 | tf_op jit(solution)/shard_map/all_to_all | solution.py:356
  27.1 3.1 %collective-permute-start.2 = (bf16[296,4096]{1,0:T(8,128)(2,1)}, bf16[296,4096]{1,0:T(8,128)(2,1)}, u32[]{:S(2)}, u32[]{:S(2)}) collective-permute-start(bf16[296,4096]{1,0:T(8,128)(2,1)} %get-tuple-element.20.slab0), channel_id=1, source_target_pairs={{1,0},{0,1},{3,2},{2,3},{5,4},{4,5},{7,6},{6,7},{9,8},{8,9},{11,10... | collective-permute-start | bytes 7274504 | tf_op jit(solution)/shard_map/ppermute | solution.py:352
  30.2 2.2 %collective-permute-start.3 = (bf16[296,4096]{1,0:T(8,128)(2,1)}, bf16[296,4096]{1,0:T(8,128)(2,1)S(1)}, u32[]{:S(2)}, u32[]{:S(2)}) collective-permute-start(bf16[296,4096]{1,0:T(8,128)(2,1)} %get-tuple-element.20.slab0), channel_id=1, source_target_pairs={{2,0},{0,2},{3,1},{1,3},{6,4},{4,6},{7,5},{5,7},{10,8},{8,10},{11,... | collective-permute-start | bytes 7274504 | tf_op jit(solution)/shard_map/ppermute | solution.py:352
  32.4 0.0 collective-permute-done.x_in_h
  32.4 0.0 copy-start.1
  32.4 0.0 collective-permute-done.1.upstream_h
  32.5 0.0 copy-start.2
  32.5 0.8 copy-done.1
  33.2 0.2 copy-done.2
  33.4 1.7 %shard_map.131 = bf16[8,16,4096]{2,1,0:T(8,128)(2,1)S(1)} custom-call(bf16[64,4096]{1,0:T(8,128)(2,1)} %copy-done.1, bf16[64,4096]{1,0:T(8,128)(2,1)} %copy-done.2, bf16[2,64,16]{2,1,0:T(8,128)(2,1)} %get-tuple-element.17.columns_h, f32[3,16,128]{2,1,0:T(8,128)} %get-tuple-element.18.rows16_h, bf16[1,4096]{1,0:T(2,128)(2,1)} %gain_h.5), custom_call_target="tpu_custom_call" | custom-call | flops 5000000000 | tf_op jit(solution)/shard_map/pallas_call | solution.py:89
  35.1 9.1 %all-to-all-done.1 = bf16[8,8,4096]{2,1,0:T(8,128)(2,1)} async-done(((bf16[8,8,4096]{2,1,0:T(8,128)(2,1)}), bf16[8,8,4096]{2,1,0:T(8,128)(2,1)}, u32[]{:S(2)}, u32[]{:S(2)}) %all-to-all-start.1) | async-done | bytes 524320 | tf_op jit(solution)/shard_map/all_to_all | solution.py:356
  44.2 29.0 %all_to_all.15.mixed_h = bf16[8,16,4096]{2,1,0:T(8,128)(2,1)S(1)} all-to-all(bf16[8,16,4096]{2,1,0:T(8,128)(2,1)S(1)} %shard_map.131), channel_id=1, replica_groups=mesh['section'=16,'y'=8,'xl'=2,'core'=2] {'y'}, dimensions={0} | all-to-all | bytes 2097152 | tf_op jit(solution)/shard_map/all_to_all | solution.py:356
  73.2 0.0 collective-permute-done.2.slab1
  73.2 7.5 %shard_map.132 = (f32[2,64,4096]{2,1,0:T(8,128)S(1)}, f32[2,128]{1,0:T(2,128)}, bf16[128,4096]{1,0:T(8,128)(2,1)S(1)}, bf16[64,4096]{1,0:T(8,128)(2,1)S(1)}) custom-call(bf16[8,16,4096]{2,1,0:T(8,128)(2,1)S(1)} %all_to_all.15.mixed_h, bf16[64,4096]{1,0:T(8,128)(2,1)} %bitcast.14.saved_h, bf16[296,4096]{1,0:T(8,128)(2,1)} %get-tuple-element.20.slab0, ...), custom_call_target="tpu_custom_call" | custom-call | flops 2000000000 | tf_op jit(solution)/shard_map/pallas_call | solution.py:89
  80.7 5.9 %collective-permute-done.3.slab.slab0 = bf16[296,4096]{1,0:T(8,128)(2,1)S(1)} collective-permute-done((bf16[296,4096]{1,0:T(8,128)(2,1)}, bf16[296,4096]{1,0:T(8,128)(2,1)S(1)}, u32[]{:S(2)}, u32[]{:S(2)}) %collective-permute-start.3) | collective-permute-done | bytes 2424864 | tf_op jit(solution)/shard_map/ppermute | solution.py:352
  86.6 2.7 %collective-permute-start.4 = (bf16[296,4096]{1,0:T(8,128)(2,1)S(1)}, bf16[296,4096]{1,0:T(8,128)(2,1)S(1)}, u32[]{:S(2)}, u32[]{:S(2)}) collective-permute-start(bf16[296,4096]{1,0:T(8,128)(2,1)S(1)} %collective-permute-done.3.slab.slab0), channel_id=1, source_target_pairs={{1,0},{0,1},{3,2},{2,3},{5,4},{4,5},{7,6},{6,7},{9,8},{8,9},{11,10... | collective-permute-start | bytes 7274504 | tf_op jit(solution)/shard_map/ppermute | solution.py:352
  89.3 0.0 copy-start
  89.3 1.8 %shard_map.133.second = f32[2,64,4096]{2,1,0:T(8,128)S(1)} custom-call(bf16[128,4096]{1,0:T(8,128)(2,1)S(1)} %get-tuple-element.21.both, bf16[64,4096]{1,0:T(8,128)(2,1)S(1)} %get-tuple-element.22.grads, bf16[296,4096]{1,0:T(8,128)(2,1)S(1)} %collective-permute-done.3.slab.slab0, f32[2,64,4096]{2,1,0:T(8,128)S(1)} %get-tuple-element.25.first), custom_call_target="tpu_custom_call" | custom-call | flops 2000000000 | tf_op jit(solution)/shard_map/pallas_call | solution.py:89
  91.0 2.5 %collective-permute-done.4.slab1 = bf16[296,4096]{1,0:T(8,128)(2,1)S(1)} collective-permute-done((bf16[296,4096]{1,0:T(8,128)(2,1)S(1)}, bf16[296,4096]{1,0:T(8,128)(2,1)S(1)}, u32[]{:S(2)}, u32[]{:S(2)}) %collective-permute-start.4) | collective-permute-done | bytes 2424864 | tf_op jit(solution)/shard_map/ppermute | solution.py:352
  93.5 0.0 copy-done
  93.5 1.8 %shard_map.134 = bf16[8,16,4224]{2,1,0:T(8,128)(2,1)S(1)} custom-call(bf16[128,4096]{1,0:T(8,128)(2,1)S(1)} %get-tuple-element.21.both, bf16[64,4096]{1,0:T(8,128)(2,1)S(1)} %get-tuple-element.22.grads, bf16[296,4096]{1,0:T(8,128)(2,1)S(1)} %collective-permute-done.3.slab.slab0, bf16[296,4096]{1,0:T(8,128)(2,1)S(1)} %collective-permute-done.4.slab1, ...), custom_call_target="tpu_custom_call" | custom-call | flops 2000000000 | tf_op jit(solution)/shard_map/pallas_call | solution.py:89
  95.3 35.7 %all_to_all.16.parts = bf16[8,16,4224]{2,1,0:T(8,128)(2,1)S(1)} all-to-all(bf16[8,16,4224]{2,1,0:T(8,128)(2,1)S(1)} %shard_map.134), channel_id=1, replica_groups=mesh['section'=16,'y'=8,'xl'=2,'core'=2] {'y'}, dimensions={0} | all-to-all | bytes 2162688 | tf_op jit(solution)/shard_map/all_to_all | solution.py:356
  131.0 2.8 %shard_map.135 = (bf16[64,4096]{1,0:T(8,128)(2,1)}, bf16[64,4096]{1,0:T(8,128)(2,1)}, f32[1,128]{1,0:T(1,128)}) custom-call(bf16[8,16,4224]{2,1,0:T(8,128)(2,1)S(1)} %all_to_all.16.parts, bf16[2,64,16]{2,1,0:T(8,128)(2,1)} %get-tuple-element.17.columns_h, f32[3,16,128]{2,1,0:T(8,128)} %get-tuple-element.18.rows16_h, ...), custom_call_target="tpu_custom_call" | custom-call | flops 2000000000 | tf_op jit(solution)/shard_map/pallas_call | solution.py:89
Async XLA Ops:
  0.6 31.8 %collective-permute-start = (bf16[64,4096]{1,0:T(8,128)(2,1)}, bf16[64,4096]{1,0:T(8,128)(2,1)S(1)}, u32[]{:S(2)}, u32[]{:S(2)}) collective-permute-start(bf16[64,4096]{1,0:T(8,128)(2,1)} %bitcast.25), channel_id=1, source_target_pairs={{480,0},{0,32},{32,64},{64,96},{96,128},{128,160},{160,192},{192,2... | collective-permute-start | bytes 1572872 | tf_op jit(solution)/shard_map/ppermute | solution.py:352
  6.1 26.3 %collective-permute-start.1 = (bf16[64,4096]{1,0:T(8,128)(2,1)}, bf16[64,4096]{1,0:T(8,128)(2,1)S(1)}, u32[]{:S(2)}, u32[]{:S(2)}) collective-permute-start(bf16[64,4096]{1,0:T(8,128)(2,1)} %bitcast.26), channel_id=1, source_target_pairs={{32,0},{64,32},{96,64},{128,96},{160,128},{192,160},{224,192},{256... | collective-permute-start | bytes 1572872 | tf_op jit(solution)/shard_map/ppermute | solution.py:352
  20.2 24.0 %all-to-all-start.1 = ((bf16[8,8,4096]{2,1,0:T(8,128)(2,1)}), bf16[8,8,4096]{2,1,0:T(8,128)(2,1)}, u32[]{:S(2)}, u32[]{:S(2)}) async-start(bf16[8,8,4096]{2,1,0:T(8,128)(2,1)} %get-tuple-element.19), calls=%async_computation.1 | async-start | bytes 1048576 | tf_op jit(solution)/shard_map/all_to_all | solution.py:356
  27.1 46.2 %collective-permute-start.2 = (bf16[296,4096]{1,0:T(8,128)(2,1)}, bf16[296,4096]{1,0:T(8,128)(2,1)}, u32[]{:S(2)}, u32[]{:S(2)}) collective-permute-start(bf16[296,4096]{1,0:T(8,128)(2,1)} %get-tuple-element.20.slab0), channel_id=1, source_target_pairs={{1,0},{0,1},{3,2},{2,3},{5,4},{4,5},{7,6},{6,7},{9,8},{8,9},{11,10... | collective-permute-start | bytes 7274504 | tf_op jit(solution)/shard_map/ppermute | solution.py:352
  30.2 56.4 %collective-permute-start.3 = (bf16[296,4096]{1,0:T(8,128)(2,1)}, bf16[296,4096]{1,0:T(8,128)(2,1)S(1)}, u32[]{:S(2)}, u32[]{:S(2)}) collective-permute-start(bf16[296,4096]{1,0:T(8,128)(2,1)} %get-tuple-element.20.slab0), channel_id=1, source_target_pairs={{2,0},{0,2},{3,1},{1,3},{6,4},{4,6},{7,5},{5,7},{10,8},{8,10},{11,... | collective-permute-start | bytes 7274504 | tf_op jit(solution)/shard_map/ppermute | solution.py:352
  32.4 0.8 copy-start.1
  32.5 1.0 copy-start.2
  86.6 6.9 %collective-permute-start.4 = (bf16[296,4096]{1,0:T(8,128)(2,1)S(1)}, bf16[296,4096]{1,0:T(8,128)(2,1)S(1)}, u32[]{:S(2)}, u32[]{:S(2)}) collective-permute-start(bf16[296,4096]{1,0:T(8,128)(2,1)S(1)} %collective-permute-done.3.slab.slab0), channel_id=1, source_target_pairs={{1,0},{0,1},{3,2},{2,3},{5,4},{4,5},{7,6},{6,7},{9,8},{8,9},{11,10... | collective-permute-start | bytes 7274504 | tf_op jit(solution)/shard_map/ppermute | solution.py:352
  89.3 4.2 %copy-start = (f32[2,128]{1,0:T(2,128)S(1)}, f32[2,128]{1,0:T(2,128)}, u32[]{:S(2)}) copy-start(f32[2,128]{1,0:T(2,128)} %get-tuple-element.26.usage) | copy-start | bytes 3076

commit v8 on v7

--- a/solution.py
+++ b/solution.py
@@ -134,7 +134,7 @@
 
 def prepare_body(
     saved_h, gain_h, broutes_h, blogits_h, froutes_h, flogits_h, gate_h, up_h, down_h,
-    send, picked, columns, rows16, slab,
+    send, picked, columns, rows16, slab, usage,
     saved, gain, broutes, blogits, froutes, flogits, sems,
 ):
     hid = gate_h.shape[0]
@@ -149,8 +149,8 @@
     hot, _, fselect_t, fgate = slot_tables(froutes[...], logits)
     powers = jnp.exp(logits - jnp.max(logits, axis=1, keepdims=True))
     probs = powers / jnp.sum(powers, axis=1, keepdims=True)
-    slab[3 * hid :, 0:EXPERTS] = usage_rows(
-        jnp.sum(hot, axis=0, keepdims=True), jnp.sum(probs, axis=0, keepdims=True)
+    usage[...] = jnp.concatenate(
+        [jnp.sum(hot, axis=0, keepdims=True), jnp.sum(probs, axis=0, keepdims=True)], axis=0
     )
     wait_all(copies[4:6])
     rows = jnp.dot(select, saved[...], preferred_element_type=f32)
@@ -226,18 +226,6 @@
     return jnp.concatenate([d_gate, d_up], axis=1).astype(bf16)
 
 
-def slab_pairs(slabs, gu, down):
-    hid = down.shape[0] // len(slabs)
-    return (
-        stacked(gu, *[w.at[0 : 2 * hid, :] for w in slabs]),
-        stacked(down, *[w.at[2 * hid : 3 * hid, :] for w in slabs]),
-    )
-
-
-def tail_of(slab):
-    return slab.at[slab.shape[0] - CAP :, 0:EXPERTS]
-
-
 def row_pairs(mixed_h, saved_h, both, grads):
     first = row_blocks(mixed_h, 0, both) + [(saved_h, both.at[both.shape[0] // 2 :, :])]
     return first, row_blocks(mixed_h, CAP, grads)
@@ -249,35 +237,30 @@
 
 
 def expert_own_body(
-    mixed_h, saved_h, slab0, slab1, first, usage, both, grads, tails, gu, down, sems
+    mixed_h, saved_h, slab0, slab1, usage0, usage1, first, usage, both, grads, sems
 ):
-    width, hid = both.shape[1], down.shape[0] // 2
     early, late = row_pairs(mixed_h, saved_h, both, grads)
-    gates, downs = slab_pairs((slab0, slab1), gu, down)
-    early, late = early + gates, late + downs
-    late += [(tail_of(w), tails.at[m]) for m, w in enumerate((slab0, slab1))]
-    copies = started(sems, *early, *late)
-    wait_all(copies)
-    sides = [
-        terms_of(both, grads, gu[2 * hid * m : 2 * hid * (m + 1), :], down[hid * m : hid * (m + 1), :])
-        for m in range(2)
-    ]
-    h, terms = (jnp.concatenate(v, axis=1) for v in zip(*sides))
-    for c in range(0, width, COLS):
-        cut = slice(c, c + COLS)
-        first[0, :, cut] = jnp.dot(h, down[:, cut], preferred_element_type=f32)
-        first[1, :, cut] = jnp.dot(terms, gu[:, cut], preferred_element_type=f32)
-    usage[...] = usage_of(tails[0]) + usage_of(tails[1])
+    wait_all(started(sems, *early, *late))
+    for cut, fwd, bwd in added(both, grads, slab0, None):
+        first[0, :, cut] = fwd
+        first[1, :, cut] = bwd
+    for cut, fwd, bwd in added(both, grads, slab1, first):
+        first[0, :, cut] = fwd
+        first[1, :, cut] = bwd
+    usage[...] = usage0[...] + usage1[...]
 
 
 def added(both, grads, slab, sums):
-    hid = (slab.shape[0] - CAP) // 3
+    hid = slab.shape[0] // 3
     h, terms = terms_of(both, grads, slab[0 : 2 * hid, :], slab[2 * hid : 3 * hid, :])
     for c in range(0, both.shape[1], COLS):
         cut = slice(c, c + COLS)
         fwd = jnp.dot(h, slab[2 * hid : 3 * hid, cut], preferred_element_type=f32)
         bwd = jnp.dot(terms, slab[0 : 2 * hid, cut], preferred_element_type=f32)
-        yield cut, sums[0, :, cut] + fwd, sums[1, :, cut] + bwd
+        if sums is None:
+            yield cut, fwd, bwd
+        else:
+            yield cut, sums[0, :, cut] + fwd, sums[1, :, cut] + bwd
 
 
 def expert_beside_body(both, grads, slab, first, second):
@@ -286,14 +269,13 @@
         second[1, :, cut] = bwd
 
 
-def expert_last_body(both, grads, slab0, slab1, second, usage, out):
+def expert_last_body(both, grads, slab, second, usage0, usage1, out):
     width = both.shape[1]
-    for cut, fwd, bwd in added(both, grads, slab1, second):
+    for cut, fwd, bwd in added(both, grads, slab, second):
         for i in range(out.shape[0]):
             out[i, 0:CAP, cut] = fwd[i * CAP : (i + 1) * CAP, :].astype(bf16)
             out[i, CAP : 2 * CAP, cut] = bwd[i * CAP : (i + 1) * CAP, :].astype(bf16)
-    beside = [usage_of(tail_of(w)[...]) for w in (slab0, slab1)]
-    total = usage[...] + (beside[0] + beside[1])
+    total = usage0[...] + usage1[...]
     rows = usage_rows(total[0:1, :], total[1:2, :])
     for i in range(out.shape[0]):
         out[i, 0:CAP, width:] = rows
@@ -366,12 +348,12 @@
     upstream = shifted(bwd_sent[0], "section", -1)
     x_in = shifted(fwd_sent[0], "section", 1)
     hid = w_down.shape[1]
-    saved_send, picked, columns, rows16, slab = kernel_call(
+    saved_send, picked, columns, rows16, slab, usage = kernel_call(
         prepare_body,
         (in_vmem((stops, CAP, width), bf16), in_hbm((SLOTS, width), bf16),
          in_hbm((EXP_WIN, tokens, SLOTS), bf16), in_hbm((3, SLOTS, EXPERTS), f32),
-         in_hbm((3 * hid + CAP, width), bf16)),
-        [HBM] * 9, [VMEM] * 5,
+         in_vmem((3 * hid, width), bf16), in_hbm((2, EXPERTS), f32)),
+        [HBM] * 9, [VMEM] * 6,
         [pltpu.VMEM((tokens, width), bf16), pltpu.VMEM((1, width), bf16),
          pltpu.VMEM((TOPK, tokens), jnp.int32), pltpu.VMEM((tokens, EXPERTS), f32),
          pltpu.VMEM((TOPK, tokens), jnp.int32), pltpu.VMEM((tokens, EXPERTS), f32), dma((9,))],
@@ -379,9 +361,10 @@
         w_gate[0].T, w_up[0].T, w_down[0],
     )
     slab_x = shifted(slab, "xl", 1)
-    slab_core = shifted(slab, "core", 1)
+    slab_core, usage_core = shifted(slab, "core", 1), shifted(usage, "core", 1)
     saved_all = over_y(saved_send).reshape(-1, width)
     block = pltpu.VMEM((tokens, width), bf16)
+    rows16, usage_core = lax.optimization_barrier((rows16, usage_core))
     mixed_send = kernel_call(
         rows_body, in_vmem((stops, 2 * CAP, width), bf16), [HBM] * 5, VMEM,
         [pltpu.VMEM((EXP_WIN, tokens, SLOTS), bf16), pltpu.VMEM((SLOTS, EXPERTS), f32),
@@ -392,14 +375,12 @@
     count = stops * CAP
     vmem = pltpu.VMEM
     sums = in_vmem((2, count, width), f32)
-    first, usage, both, grads = kernel_call(
+    first, usage_pair, both, grads = kernel_call(
         expert_own_body,
         (sums, in_hbm((2, EXPERTS), f32), in_vmem((2 * count, width), bf16),
          in_vmem((count, width), bf16)),
-        [PINNED, PINNED, HBM, HBM], [VMEM] * 4,
-        [vmem((2, CAP, EXPERTS), bf16), vmem((4 * hid, width), bf16),
-         vmem((2 * hid, width), bf16), dma((2 * stops + 8,))],
-        mixed_all, saved_all, slab, slab_core, us=2,
+        [PINNED] * 4 + [VMEM] * 2, [VMEM] * 4, [dma((2 * stops + 1,))],
+        mixed_all, saved_all, slab, slab_core, usage, usage_core, us=2,
     )
     slab_x, first = lax.optimization_barrier((slab_x, first))
     slab_x_core = shifted(slab_x, "core", 1)
@@ -408,8 +389,8 @@
     )
     result = kernel_call(
         expert_last_body, in_vmem((stops, 2 * CAP, width + EXPERTS), bf16),
-        [PINNED] * 5 + [VMEM], VMEM, [],
-        both, grads, slab_x, slab_x_core, second, usage,
+        [PINNED] * 4 + [VMEM] * 2, VMEM, [],
+        both, grads, slab_x_core, second, usage_pair, shifted(usage_pair, "xl", 1),
     )
     parts = over_y(result)
     full = in_hbm((tokens, width), bf16)

time: 134 us -> 134 us (level)
  starting transfers between devices: 30.8 us -> 35.4 us
  waiting for transfers between devices: 17.4 us -> 12.8 us
  blocking collectives: 64.7 us -> 63.1 us
    ppermute x5 -> x7, starting transfers between devices: 23.9 us -> 28.6 us  [shifted(): lax.ppermute(block, axis, [((i - distance) % n, i) for i in range(n)])]
    all_to_all x1, waiting for transfers between devices: 9.05 us -> 6.29 us  [over_y(): return lax.all_to_all(block, 'y', split_axis=0, concat_axis=0, tiled=True)]
    ppermute x5 -> x7, waiting for transfers between devices: 8.32 us -> 6.49 us  [shifted(): lax.ppermute(block, axis, [((i - distance) % n, i) for i in range(n)])]
    all_to_all x2, blocking collectives: 64.7 us -> 63.1 us  [over_y(): return lax.all_to_all(block, 'y', split_axis=0, concat_axis=0, tiled=True)]
  transfers between devices with their start and end apart: 6 -> 8, of which waited for: 3 -> 4; matrix products, arithmetic and copies ran while one was open for 0% -> 0% of each run, Pallas kernels for 11% -> 11%
where the time goes in v8:
time: 134 us; the launch traced here: 133 us
  blocking collectives  63.1 us (47%)
  starting transfers between devices  35.4 us (26%)
  Pallas kernels  19.2 us (14%)
  waiting for transfers between devices  12.8 us (10%)
  local copies, waits for them, and re-layouts  1.64 us (1%)
    all_to_all x2, blocking collectives, over_y(): return lax.all_to_all(block, 'y', split_axis=0, concat_axis=0, tiled=True)  63.1 us
    ppermute x7, starting transfers between devices, shifted(): lax.ppermute(block, axis, [((i - distance) % n, i) for i in range(n)])  28.6 us
    pallas_call x6, Pallas kernels, kernel_call(): pl.pallas_call(body, out_shape=outs, in_specs=in_specs, out_specs=out_spe...  19.2 us
    all_to_all x1, starting transfers between devices, over_y(): return lax.all_to_all(block, 'y', split_axis=0, concat_axis=0, tiled=True)  6.83 us
    ppermute x7, waiting for transfers between devices, shifted(): lax.ppermute(block, axis, [((i - distance) % n, i) for i in range(n)])  6.49 us
    all_to_all x1, waiting for transfers between devices, over_y(): return lax.all_to_all(block, 'y', split_axis=0, concat_axis=0, tiled=True)  6.29 us
  transfers between devices with their start and end apart: 8, of which 4 were waited for; matrix products, arithmetic and copies ran while one was open for 0% of the time, Pallas kernels for 11%

profile of v8, /device:TPU:1, one launch (start us, length us, event | category | flops | bytes accessed | tf_op | source)
XLA Modules:
  0.0 132.9 jit_solution(15967896031056112967)
XLA Ops:
  0.6 5.5 %collective-permute-start = (bf16[64,4096]{1,0:T(8,128)(2,1)}, bf16[64,4096]{1,0:T(8,128)(2,1)S(1)}, u32[]{:S(2)}, u32[]{:S(2)}) collective-permute-start(bf16[64,4096]{1,0:T(8,128)(2,1)} %bitcast.25), channel_id=1, source_target_pairs={{480,0},{0,32},{32,64},{64,96},{96,128},{128,160},{160,192},{192,2... | collective-permute-start | bytes 1572872 | tf_op jit(solution)/shard_map/ppermute | solution.py:334
  6.1 10.4 %collective-permute-start.1 = (bf16[64,4096]{1,0:T(8,128)(2,1)}, bf16[64,4096]{1,0:T(8,128)(2,1)S(1)}, u32[]{:S(2)}, u32[]{:S(2)}) collective-permute-start(bf16[64,4096]{1,0:T(8,128)(2,1)} %bitcast.26), channel_id=1, source_target_pairs={{32,0},{64,32},{96,64},{128,96},{160,128},{192,160},{224,192},{256... | collective-permute-start | bytes 1572872 | tf_op jit(solution)/shard_map/ppermute | solution.py:334
  16.5 3.7 %shard_map.130 = (bf16[8,8,4096]{2,1,0:T(8,128)(2,1)}, bf16[16,4096]{1,0:T(8,128)(2,1)}, bf16[2,64,16]{2,1,0:T(8,128)(2,1)}, f32[3,16,128]{2,1,0:T(8,128)}, bf16[288,4096]{1,0:T(8,128)(2,1)}, /*index=5*/f32[2,128]{1,0:T(2,128)}) custom-call(bf16[64,4096]{1,0:T(8,128)(2,1)} %bitcast.24, bf16[1,4096]{1,0:T(2,128)(2,1)} %gain_h.5, s32[8,64]{1,0:T(8,128)} %bitcast.29, ...), custom_call_target="tpu_custom_call" | custom-call | flops 2000000000 | tf_op jit(solution)/shard_map/pallas_call | solution.py:89
  20.2 6.8 %all-to-all-start.1 = ((bf16[8,8,4096]{2,1,0:T(8,128)(2,1)}), bf16[8,8,4096]{2,1,0:T(8,128)(2,1)}, u32[]{:S(2)}, u32[]{:S(2)}) async-start(bf16[8,8,4096]{2,1,0:T(8,128)(2,1)} %get-tuple-element.24), calls=%async_computation.1 | async-start | bytes 1048576 | tf_op jit(solution)/shard_map/all_to_all | solution.py:338
  27.0 3.1 %collective-permute-start.3 = (bf16[288,4096]{1,0:T(8,128)(2,1)}, bf16[288,4096]{1,0:T(8,128)(2,1)}, u32[]{:S(2)}, u32[]{:S(2)}) collective-permute-start(bf16[288,4096]{1,0:T(8,128)(2,1)} %get-tuple-element.25.slab0), channel_id=1, source_target_pairs={{1,0},{0,1},{3,2},{2,3},{5,4},{4,5},{7,6},{6,7},{9,8},{8,9},{11,10... | collective-permute-start | bytes 7077896 | tf_op jit(solution)/shard_map/ppermute | solution.py:334
  30.2 1.9 %collective-permute-start.2 = (f32[2,128]{1,0:T(2,128)}, f32[2,128]{1,0:T(2,128)S(1)}, u32[]{:S(2)}, u32[]{:S(2)}) collective-permute-start(f32[2,128]{1,0:T(2,128)} %get-tuple-element.22.usage0), channel_id=1, source_target_pairs={{1,0},{0,1},{3,2},{2,3},{5,4},{4,5},{7,6},{6,7},{9,8},{8,9},{11,10... | collective-permute-start | bytes 3080 | tf_op jit(solution)/shard_map/ppermute | solution.py:334
  32.1 2.2 %collective-permute-start.4 = (bf16[288,4096]{1,0:T(8,128)(2,1)}, bf16[288,4096]{1,0:T(8,128)(2,1)S(1)}, u32[]{:S(2)}, u32[]{:S(2)}) collective-permute-start(bf16[288,4096]{1,0:T(8,128)(2,1)} %get-tuple-element.25.slab0), channel_id=1, source_target_pairs={{2,0},{0,2},{3,1},{1,3},{6,4},{4,6},{7,5},{5,7},{10,8},{8,10},{11,... | collective-permute-start | bytes 7077896 | tf_op jit(solution)/shard_map/ppermute | solution.py:334
  34.3 0.2 collective-permute-done.2.usage1
  34.5 0.0 collective-permute-done.x_in_h
  34.5 0.0 copy-start.2
  34.5 0.0 collective-permute-done.1.upstream_h
  34.5 0.8 copy-done.2
  35.3 0.0 copy-start.3
  35.3 0.8 copy-done.3
  36.2 0.0 copy-start
  36.2 1.7 %shard_map.131 = bf16[8,16,4096]{2,1,0:T(8,128)(2,1)S(1)} custom-call(bf16[64,4096]{1,0:T(8,128)(2,1)} %copy-done.2, bf16[64,4096]{1,0:T(8,128)(2,1)} %copy-done.3, bf16[2,64,16]{2,1,0:T(8,128)(2,1)} %get-tuple-element.20.columns_h, f32[3,16,128]{2,1,0:T(8,128)} %get-tuple-element.23.rows16_h, bf16[1,4096]{1,0:T(2,128)(2,1)} %gain_h.5), custom_call_target="tpu_custom_call" | custom-call | flops 5000000000 | tf_op jit(solution)/shard_map/pallas_call | solution.py:89
  37.9 6.3 %all-to-all-done.1 = bf16[8,8,4096]{2,1,0:T(8,128)(2,1)} async-done(((bf16[8,8,4096]{2,1,0:T(8,128)(2,1)}), bf16[8,8,4096]{2,1,0:T(8,128)(2,1)}, u32[]{:S(2)}, u32[]{:S(2)}) %all-to-all-start.1) | async-done | bytes 524320 | tf_op jit(solution)/shard_map/all_to_all | solution.py:338
  44.2 29.0 %all_to_all.15.mixed_h = bf16[8,16,4096]{2,1,0:T(8,128)(2,1)S(1)} all-to-all(bf16[8,16,4096]{2,1,0:T(8,128)(2,1)S(1)} %shard_map.131), channel_id=1, replica_groups=mesh['section'=16,'y'=8,'xl'=2,'core'=2] {'y'}, dimensions={0} | all-to-all | bytes 2097152 | tf_op jit(solution)/shard_map/all_to_all | solution.py:338
  73.2 0.0 collective-permute-done.3.slab1
  73.2 0.0 copy-done
  73.2 7.5 %shard_map.132 = (f32[2,64,4096]{2,1,0:T(8,128)S(1)}, f32[2,128]{1,0:T(2,128)}, bf16[128,4096]{1,0:T(8,128)(2,1)S(1)}, bf16[64,4096]{1,0:T(8,128)(2,1)S(1)}) custom-call(bf16[8,16,4096]{2,1,0:T(8,128)(2,1)S(1)} %all_to_all.15.mixed_h, bf16[64,4096]{1,0:T(8,128)(2,1)} %bitcast.14.saved_h, bf16[288,4096]{1,0:T(8,128)(2,1)} %get-tuple-element.25.slab0, ...), custom_call_target="tpu_custom_call" | custom-call | flops 2000000000 | tf_op jit(solution)/shard_map/pallas_call | solution.py:89
  80.7 5.8 %collective-permute-done.4.slab = bf16[288,4096]{1,0:T(8,128)(2,1)S(1)} collective-permute-done((bf16[288,4096]{1,0:T(8,128)(2,1)}, bf16[288,4096]{1,0:T(8,128)(2,1)S(1)}, u32[]{:S(2)}, u32[]{:S(2)}) %collective-permute-start.4) | collective-permute-done | bytes 2359328 | tf_op jit(solution)/shard_map/ppermute | solution.py:334
  86.5 3.2 %collective-permute-start.5 = (bf16[288,4096]{1,0:T(8,128)(2,1)S(1)}, bf16[288,4096]{1,0:T(8,128)(2,1)S(1)}, u32[]{:S(2)}, u32[]{:S(2)}) collective-permute-start(bf16[288,4096]{1,0:T(8,128)(2,1)S(1)} %collective-permute-done.4.slab), channel_id=1, source_target_pairs={{1,0},{0,1},{3,2},{2,3},{5,4},{4,5},{7,6},{6,7},{9,8},{8,9},{11,10... | collective-permute-start | bytes 7077896 | tf_op jit(solution)/shard_map/ppermute | solution.py:334
  89.8 2.2 %collective-permute-start.6 = (f32[2,128]{1,0:T(2,128)}, f32[2,128]{1,0:T(2,128)S(1)}, u32[]{:S(2)}, u32[]{:S(2)}) collective-permute-start(f32[2,128]{1,0:T(2,128)} %get-tuple-element.32.usage0), channel_id=1, source_target_pairs={{2,0},{0,2},{3,1},{1,3},{6,4},{4,6},{7,5},{5,7},{10,8},{8,10},{11,... | collective-permute-start | bytes 3080 | tf_op jit(solution)/shard_map/ppermute | solution.py:334
  92.0 0.0 copy-start.1
  92.0 1.8 %shard_map.133.second = f32[2,64,4096]{2,1,0:T(8,128)S(1)} custom-call(bf16[128,4096]{1,0:T(8,128)(2,1)S(1)} %get-tuple-element.27.both, bf16[64,4096]{1,0:T(8,128)(2,1)S(1)} %get-tuple-element.28.grads, bf16[288,4096]{1,0:T(8,128)(2,1)S(1)} %collective-permute-done.4.slab, f32[2,64,4096]{2,1,0:T(8,128)S(1)} %get-tuple-element.31.first), custom_call_target="tpu_custom_call" | custom-call | flops 2000000000 | tf_op jit(solution)/shard_map/pallas_call | solution.py:89
  93.8 0.5 collective-permute-done.6.usage1
  94.3 0.0 collective-permute-done.5.slab
  94.3 0.0 copy-done.1
  94.3 1.8 %shard_map.134 = bf16[8,16,4224]{2,1,0:T(8,128)(2,1)S(1)} custom-call(bf16[128,4096]{1,0:T(8,128)(2,1)S(1)} %get-tuple-element.27.both, bf16[64,4096]{1,0:T(8,128)(2,1)S(1)} %get-tuple-element.28.grads, bf16[288,4096]{1,0:T(8,128)(2,1)S(1)} %collective-permute-done.5.slab, f32[2,64,4096]{2,1,0:T(8,128)S(1)} %shard_map.133.second, f32[2,128]{1,0:T(2,128)S(1)} %copy-done.1, ...), custom_call_target="tpu_custom_call" | custom-call | flops 2000000000 | tf_op jit(solution)/shard_map/pallas_call | solution.py:89
  96.1 34.1 %all_to_all.16.parts = bf16[8,16,4224]{2,1,0:T(8,128)(2,1)S(1)} all-to-all(bf16[8,16,4224]{2,1,0:T(8,128)(2,1)S(1)} %shard_map.134), channel_id=1, replica_groups=mesh['section'=16,'y'=8,'xl'=2,'core'=2] {'y'}, dimensions={0} | all-to-all | bytes 2162688 | tf_op jit(solution)/shard_map/all_to_all | solution.py:338
  130.2 2.8 %shard_map.135 = (bf16[64,4096]{1,0:T(8,128)(2,1)}, bf16[64,4096]{1,0:T(8,128)(2,1)}, f32[1,128]{1,0:T(1,128)}) custom-call(bf16[8,16,4224]{2,1,0:T(8,128)(2,1)S(1)} %all_to_all.16.parts, bf16[2,64,16]{2,1,0:T(8,128)(2,1)} %get-tuple-element.20.columns_h, f32[3,16,128]{2,1,0:T(8,128)} %get-tuple-element.23.rows16_h, ...), custom_call_target="tpu_custom_call" | custom-call | flops 2000000000 | tf_op jit(solution)/shard_map/pallas_call | solution.py:89
Async XLA Ops:
  0.6 33.9 %collective-permute-start = (bf16[64,4096]{1,0:T(8,128)(2,1)}, bf16[64,4096]{1,0:T(8,128)(2,1)S(1)}, u32[]{:S(2)}, u32[]{:S(2)}) collective-permute-start(bf16[64,4096]{1,0:T(8,128)(2,1)} %bitcast.25), channel_id=1, source_target_pairs={{480,0},{0,32},{32,64},{64,96},{96,128},{128,160},{160,192},{192,2... | collective-permute-start | bytes 1572872 | tf_op jit(solution)/shard_map/ppermute | solution.py:334
  6.1 28.4 %collective-permute-start.1 = (bf16[64,4096]{1,0:T(8,128)(2,1)}, bf16[64,4096]{1,0:T(8,128)(2,1)S(1)}, u32[]{:S(2)}, u32[]{:S(2)}) collective-permute-start(bf16[64,4096]{1,0:T(8,128)(2,1)} %bitcast.26), channel_id=1, source_target_pairs={{32,0},{64,32},{96,64},{128,96},{160,128},{192,160},{224,192},{256... | collective-permute-start | bytes 1572872 | tf_op jit(solution)/shard_map/ppermute | solution.py:334
  20.2 24.0 %all-to-all-start.1 = ((bf16[8,8,4096]{2,1,0:T(8,128)(2,1)}), bf16[8,8,4096]{2,1,0:T(8,128)(2,1)}, u32[]{:S(2)}, u32[]{:S(2)}) async-start(bf16[8,8,4096]{2,1,0:T(8,128)(2,1)} %get-tuple-element.24), calls=%async_computation.1 | async-start | bytes 1048576 | tf_op jit(solution)/shard_map/all_to_all | solution.py:338
  27.0 46.2 %collective-permute-start.3 = (bf16[288,4096]{1,0:T(8,128)(2,1)}, bf16[288,4096]{1,0:T(8,128)(2,1)}, u32[]{:S(2)}, u32[]{:S(2)}) collective-permute-start(bf16[288,4096]{1,0:T(8,128)(2,1)} %get-tuple-element.25.slab0), channel_id=1, source_target_pairs={{1,0},{0,1},{3,2},{2,3},{5,4},{4,5},{7,6},{6,7},{9,8},{8,9},{11,10... | collective-permute-start | bytes 7077896 | tf_op jit(solution)/shard_map/ppermute | solution.py:334
  30.2 4.4 %collective-permute-start.2 = (f32[2,128]{1,0:T(2,128)}, f32[2,128]{1,0:T(2,128)S(1)}, u32[]{:S(2)}, u32[]{:S(2)}) collective-permute-start(f32[2,128]{1,0:T(2,128)} %get-tuple-element.22.usage0), channel_id=1, source_target_pairs={{1,0},{0,1},{3,2},{2,3},{5,4},{4,5},{7,6},{6,7},{9,8},{8,9},{11,10... | collective-permute-start | bytes 3080 | tf_op jit(solution)/shard_map/ppermute | solution.py:334
  32.1 54.4 %collective-permute-start.4 = (bf16[288,4096]{1,0:T(8,128)(2,1)}, bf16[288,4096]{1,0:T(8,128)(2,1)S(1)}, u32[]{:S(2)}, u32[]{:S(2)}) collective-permute-start(bf16[288,4096]{1,0:T(8,128)(2,1)} %get-tuple-element.25.slab0), channel_id=1, source_target_pairs={{2,0},{0,2},{3,1},{1,3},{6,4},{4,6},{7,5},{5,7},{10,8},{8,10},{11,... | collective-permute-start | bytes 7077896 | tf_op jit(solution)/shard_map/ppermute | solution.py:334
  34.5 0.8 copy-start.2
  35.3 0.8 copy-start.3
  36.2 37.1 %copy-start = (f32[2,128]{1,0:T(2,128)S(1)}, f32[2,128]{1,0:T(2,128)}, u32[]{:S(2)}) copy-start(f32[2,128]{1,0:T(2,128)} %get-tuple-element.22.usage0) | copy-start | bytes 3076
  86.5 7.8 %collective-permute-start.5 = (bf16[288,4096]{1,0:T(8,128)(2,1)S(1)}, bf16[288,4096]{1,0:T(8,128)(2,1)S(1)}, u32[]{:S(2)}, u32[]{:S(2)}) collective-permute-start(bf16[288,4096]{1,0:T(8,128)(2,1)S(1)} %collective-permute-done.4.slab), channel_id=1, source_target_pairs={{1,0},{0,1},{3,2},{2,3},{5,4},{4,5},{7,6},{6,7},{9,8},{8,9},{11,10... | collective-permute-start | bytes 7077896 | tf_op jit(solution)/shard_map/ppermute | solution.py:334
  89.8 4.5 %collective-permute-start.6 = (f32[2,128]{1,0:T(2,128)}, f32[2,128]{1,0:T(2,128)S(1)}, u32[]{:S(2)}, u32[]{:S(2)}) collective-permute-start(f32[2,128]{1,0:T(2,128)} %get-tuple-element.32.usage0), channel_id=1, source_target_pairs={{2,0},{0,2},{3,1},{1,3},{6,4},{4,6},{7,5},{5,7},{10,8},{8,10},{11,... | collective-permute-start | bytes 3080 | tf_op jit(solution)/shard_map/ppermute | solution.py:334
  92.0 2.3 %copy-start.1 = (f32[2,128]{1,0:T(2,128)S(1)}, f32[2,128]{1,0:T(2,128)}, u32[]{:S(2)}) copy-start(f32[2,128]{1,0:T(2,128)} %get-tuple-element.32.usage0) | copy-start | bytes 3076

commit v9 on v8

--- a/solution.py
+++ b/solution.py
@@ -191,7 +191,7 @@
         send[i, CAP : 2 * CAP, :] = grads[r : r + CAP, :]
 
 
-COLS = 512
+COLS = 1024
 
 
 def nt(a, b):

time: 134 us -> 134 us (level)
  no operation moved by 1% of the time
where the time goes in v9:
time: 134 us; the launch traced here: 133 us
  blocking collectives  63.1 us (47%)
  starting transfers between devices  35.4 us (26%)
  Pallas kernels  19.2 us (14%)
  waiting for transfers between devices  12.8 us (10%)
  local copies, waits for them, and re-layouts  1.64 us (1%)
    all_to_all x2, blocking collectives, over_y(): return lax.all_to_all(block, 'y', split_axis=0, concat_axis=0, tiled=True)  63.1 us
    ppermute x7, starting transfers between devices, shifted(): lax.ppermute(block, axis, [((i - distance) % n, i) for i in range(n)])  28.6 us
    pallas_call x6, Pallas kernels, kernel_call(): pl.pallas_call(body, out_shape=outs, in_specs=in_specs, out_specs=out_spe...  19.2 us
    all_to_all x1, starting transfers between devices, over_y(): return lax.all_to_all(block, 'y', split_axis=0, concat_axis=0, tiled=True)  6.83 us
    ppermute x7, waiting for transfers between devices, shifted(): lax.ppermute(block, axis, [((i - distance) % n, i) for i in range(n)])  6.5 us
    all_to_all x1, waiting for transfers between devices, over_y(): return lax.all_to_all(block, 'y', split_axis=0, concat_axis=0, tiled=True)  6.29 us
  transfers between devices with their start and end apart: 8, of which 4 were waited for; matrix products, arithmetic and copies ran while one was open for 0% of the time, Pallas kernels for 11%

profile of v9, /device:TPU:1, one launch (start us, length us, event | category | flops | bytes accessed | tf_op | source)
XLA Modules:
  0.0 132.9 jit_solution(11004236492673114620)
XLA Ops:
  0.6 5.5 %collective-permute-start = (bf16[64,4096]{1,0:T(8,128)(2,1)}, bf16[64,4096]{1,0:T(8,128)(2,1)S(1)}, u32[]{:S(2)}, u32[]{:S(2)}) collective-permute-start(bf16[64,4096]{1,0:T(8,128)(2,1)} %bitcast.25), channel_id=1, source_target_pairs={{480,0},{0,32},{32,64},{64,96},{96,128},{128,160},{160,192},{192,2... | collective-permute-start | bytes 1572872 | tf_op jit(solution)/shard_map/ppermute | solution.py:334
  6.1 10.4 %collective-permute-start.1 = (bf16[64,4096]{1,0:T(8,128)(2,1)}, bf16[64,4096]{1,0:T(8,128)(2,1)S(1)}, u32[]{:S(2)}, u32[]{:S(2)}) collective-permute-start(bf16[64,4096]{1,0:T(8,128)(2,1)} %bitcast.26), channel_id=1, source_target_pairs={{32,0},{64,32},{96,64},{128,96},{160,128},{192,160},{224,192},{256... | collective-permute-start | bytes 1572872 | tf_op jit(solution)/shard_map/ppermute | solution.py:334
  16.5 3.7 %shard_map.130 = (bf16[8,8,4096]{2,1,0:T(8,128)(2,1)}, bf16[16,4096]{1,0:T(8,128)(2,1)}, bf16[2,64,16]{2,1,0:T(8,128)(2,1)}, f32[3,16,128]{2,1,0:T(8,128)}, bf16[288,4096]{1,0:T(8,128)(2,1)}, /*index=5*/f32[2,128]{1,0:T(2,128)}) custom-call(bf16[64,4096]{1,0:T(8,128)(2,1)} %bitcast.24, bf16[1,4096]{1,0:T(2,128)(2,1)} %gain_h.5, s32[8,64]{1,0:T(8,128)} %bitcast.29, ...), custom_call_target="tpu_custom_call" | custom-call | flops 2000000000 | tf_op jit(solution)/shard_map/pallas_call | solution.py:89
  20.2 6.8 %all-to-all-start.1 = ((bf16[8,8,4096]{2,1,0:T(8,128)(2,1)}), bf16[8,8,4096]{2,1,0:T(8,128)(2,1)}, u32[]{:S(2)}, u32[]{:S(2)}) async-start(bf16[8,8,4096]{2,1,0:T(8,128)(2,1)} %get-tuple-element.24), calls=%async_computation.1 | async-start | bytes 1048576 | tf_op jit(solution)/shard_map/all_to_all | solution.py:338
  27.0 3.1 %collective-permute-start.3 = (bf16[288,4096]{1,0:T(8,128)(2,1)}, bf16[288,4096]{1,0:T(8,128)(2,1)}, u32[]{:S(2)}, u32[]{:S(2)}) collective-permute-start(bf16[288,4096]{1,0:T(8,128)(2,1)} %get-tuple-element.25.slab0), channel_id=1, source_target_pairs={{1,0},{0,1},{3,2},{2,3},{5,4},{4,5},{7,6},{6,7},{9,8},{8,9},{11,10... | collective-permute-start | bytes 7077896 | tf_op jit(solution)/shard_map/ppermute | solution.py:334
  30.2 1.9 %collective-permute-start.2 = (f32[2,128]{1,0:T(2,128)}, f32[2,128]{1,0:T(2,128)S(1)}, u32[]{:S(2)}, u32[]{:S(2)}) collective-permute-start(f32[2,128]{1,0:T(2,128)} %get-tuple-element.22.usage0), channel_id=1, source_target_pairs={{1,0},{0,1},{3,2},{2,3},{5,4},{4,5},{7,6},{6,7},{9,8},{8,9},{11,10... | collective-permute-start | bytes 3080 | tf_op jit(solution)/shard_map/ppermute | solution.py:334
  32.1 2.2 %collective-permute-start.4 = (bf16[288,4096]{1,0:T(8,128)(2,1)}, bf16[288,4096]{1,0:T(8,128)(2,1)S(1)}, u32[]{:S(2)}, u32[]{:S(2)}) collective-permute-start(bf16[288,4096]{1,0:T(8,128)(2,1)} %get-tuple-element.25.slab0), channel_id=1, source_target_pairs={{2,0},{0,2},{3,1},{1,3},{6,4},{4,6},{7,5},{5,7},{10,8},{8,10},{11,... | collective-permute-start | bytes 7077896 | tf_op jit(solution)/shard_map/ppermute | solution.py:334
  34.3 0.2 collective-permute-done.2.usage1
  34.5 0.0 collective-permute-done.x_in_h
  34.5 0.0 copy-start.2
  34.5 0.0 collective-permute-done.1.upstream_h
  34.5 0.8 copy-done.2
  35.3 0.0 copy-start.3
  35.3 0.8 copy-done.3
  36.2 0.0 copy-start
  36.2 1.7 %shard_map.131 = bf16[8,16,4096]{2,1,0:T(8,128)(2,1)S(1)} custom-call(bf16[64,4096]{1,0:T(8,128)(2,1)} %copy-done.2, bf16[64,4096]{1,0:T(8,128)(2,1)} %copy-done.3, bf16[2,64,16]{2,1,0:T(8,128)(2,1)} %get-tuple-element.20.columns_h, f32[3,16,128]{2,1,0:T(8,128)} %get-tuple-element.23.rows16_h, bf16[1,4096]{1,0:T(2,128)(2,1)} %gain_h.5), custom_call_target="tpu_custom_call" | custom-call | flops 5000000000 | tf_op jit(solution)/shard_map/pallas_call | solution.py:89
  37.9 6.3 %all-to-all-done.1 = bf16[8,8,4096]{2,1,0:T(8,128)(2,1)} async-done(((bf16[8,8,4096]{2,1,0:T(8,128)(2,1)}), bf16[8,8,4096]{2,1,0:T(8,128)(2,1)}, u32[]{:S(2)}, u32[]{:S(2)}) %all-to-all-start.1) | async-done | bytes 524320 | tf_op jit(solution)/shard_map/all_to_all | solution.py:338
  44.2 29.0 %all_to_all.15.mixed_h = bf16[8,16,4096]{2,1,0:T(8,128)(2,1)S(1)} all-to-all(bf16[8,16,4096]{2,1,0:T(8,128)(2,1)S(1)} %shard_map.131), channel_id=1, replica_groups=mesh['section'=16,'y'=8,'xl'=2,'core'=2] {'y'}, dimensions={0} | all-to-all | bytes 2097152 | tf_op jit(solution)/shard_map/all_to_all | solution.py:338
  73.2 0.0 collective-permute-done.3.slab1
  73.2 0.0 copy-done
  73.2 7.5 %shard_map.132 = (f32[2,64,4096]{2,1,0:T(8,128)S(1)}, f32[2,128]{1,0:T(2,128)}, bf16[128,4096]{1,0:T(8,128)(2,1)S(1)}, bf16[64,4096]{1,0:T(8,128)(2,1)S(1)}) custom-call(bf16[8,16,4096]{2,1,0:T(8,128)(2,1)S(1)} %all_to_all.15.mixed_h, bf16[64,4096]{1,0:T(8,128)(2,1)} %bitcast.14.saved_h, bf16[288,4096]{1,0:T(8,128)(2,1)} %get-tuple-element.25.slab0, ...), custom_call_target="tpu_custom_call" | custom-call | flops 2000000000 | tf_op jit(solution)/shard_map/pallas_call | solution.py:89
  80.7 5.8 %collective-permute-done.4.slab = bf16[288,4096]{1,0:T(8,128)(2,1)S(1)} collective-permute-done((bf16[288,4096]{1,0:T(8,128)(2,1)}, bf16[288,4096]{1,0:T(8,128)(2,1)S(1)}, u32[]{:S(2)}, u32[]{:S(2)}) %collective-permute-start.4) | collective-permute-done | bytes 2359328 | tf_op jit(solution)/shard_map/ppermute | solution.py:334
  86.5 3.2 %collective-permute-start.5 = (bf16[288,4096]{1,0:T(8,128)(2,1)S(1)}, bf16[288,4096]{1,0:T(8,128)(2,1)S(1)}, u32[]{:S(2)}, u32[]{:S(2)}) collective-permute-start(bf16[288,4096]{1,0:T(8,128)(2,1)S(1)} %collective-permute-done.4.slab), channel_id=1, source_target_pairs={{1,0},{0,1},{3,2},{2,3},{5,4},{4,5},{7,6},{6,7},{9,8},{8,9},{11,10... | collective-permute-start | bytes 7077896 | tf_op jit(solution)/shard_map/ppermute | solution.py:334
  89.8 2.2 %collective-permute-start.6 = (f32[2,128]{1,0:T(2,128)}, f32[2,128]{1,0:T(2,128)S(1)}, u32[]{:S(2)}, u32[]{:S(2)}) collective-permute-start(f32[2,128]{1,0:T(2,128)} %get-tuple-element.32.usage0), channel_id=1, source_target_pairs={{2,0},{0,2},{3,1},{1,3},{6,4},{4,6},{7,5},{5,7},{10,8},{8,10},{11,... | collective-permute-start | bytes 3080 | tf_op jit(solution)/shard_map/ppermute | solution.py:334
  92.0 0.0 copy-start.1
  92.0 1.8 %shard_map.133.second = f32[2,64,4096]{2,1,0:T(8,128)S(1)} custom-call(bf16[128,4096]{1,0:T(8,128)(2,1)S(1)} %get-tuple-element.27.both, bf16[64,4096]{1,0:T(8,128)(2,1)S(1)} %get-tuple-element.28.grads, bf16[288,4096]{1,0:T(8,128)(2,1)S(1)} %collective-permute-done.4.slab, f32[2,64,4096]{2,1,0:T(8,128)S(1)} %get-tuple-element.31.first), custom_call_target="tpu_custom_call" | custom-call | flops 2000000000 | tf_op jit(solution)/shard_map/pallas_call | solution.py:89
  93.8 0.5 collective-permute-done.6.usage1
  94.3 0.0 collective-permute-done.5.slab
  94.3 0.0 copy-done.1
  94.3 1.8 %shard_map.134 = bf16[8,16,4224]{2,1,0:T(8,128)(2,1)S(1)} custom-call(bf16[128,4096]{1,0:T(8,128)(2,1)S(1)} %get-tuple-element.27.both, bf16[64,4096]{1,0:T(8,128)(2,1)S(1)} %get-tuple-element.28.grads, bf16[288,4096]{1,0:T(8,128)(2,1)S(1)} %collective-permute-done.5.slab, f32[2,64,4096]{2,1,0:T(8,128)S(1)} %shard_map.133.second, f32[2,128]{1,0:T(2,128)S(1)} %copy-done.1, ...), custom_call_target="tpu_custom_call" | custom-call | flops 2000000000 | tf_op jit(solution)/shard_map/pallas_call | solution.py:89
  96.1 34.1 %all_to_all.16.parts = bf16[8,16,4224]{2,1,0:T(8,128)(2,1)S(1)} all-to-all(bf16[8,16,4224]{2,1,0:T(8,128)(2,1)S(1)} %shard_map.134), channel_id=1, replica_groups=mesh['section'=16,'y'=8,'xl'=2,'core'=2] {'y'}, dimensions={0} | all-to-all | bytes 2162688 | tf_op jit(solution)/shard_map/all_to_all | solution.py:338
  130.1 2.8 %shard_map.135 = (bf16[64,4096]{1,0:T(8,128)(2,1)}, bf16[64,4096]{1,0:T(8,128)(2,1)}, f32[1,128]{1,0:T(1,128)}) custom-call(bf16[8,16,4224]{2,1,0:T(8,128)(2,1)S(1)} %all_to_all.16.parts, bf16[2,64,16]{2,1,0:T(8,128)(2,1)} %get-tuple-element.20.columns_h, f32[3,16,128]{2,1,0:T(8,128)} %get-tuple-element.23.rows16_h, ...), custom_call_target="tpu_custom_call" | custom-call | flops 2000000000 | tf_op jit(solution)/shard_map/pallas_call | solution.py:89
Async XLA Ops:
  0.6 33.9 %collective-permute-start = (bf16[64,4096]{1,0:T(8,128)(2,1)}, bf16[64,4096]{1,0:T(8,128)(2,1)S(1)}, u32[]{:S(2)}, u32[]{:S(2)}) collective-permute-start(bf16[64,4096]{1,0:T(8,128)(2,1)} %bitcast.25), channel_id=1, source_target_pairs={{480,0},{0,32},{32,64},{64,96},{96,128},{128,160},{160,192},{192,2... | collective-permute-start | bytes 1572872 | tf_op jit(solution)/shard_map/ppermute | solution.py:334
  6.1 28.4 %collective-permute-start.1 = (bf16[64,4096]{1,0:T(8,128)(2,1)}, bf16[64,4096]{1,0:T(8,128)(2,1)S(1)}, u32[]{:S(2)}, u32[]{:S(2)}) collective-permute-start(bf16[64,4096]{1,0:T(8,128)(2,1)} %bitcast.26), channel_id=1, source_target_pairs={{32,0},{64,32},{96,64},{128,96},{160,128},{192,160},{224,192},{256... | collective-permute-start | bytes 1572872 | tf_op jit(solution)/shard_map/ppermute | solution.py:334
  20.2 24.0 %all-to-all-start.1 = ((bf16[8,8,4096]{2,1,0:T(8,128)(2,1)}), bf16[8,8,4096]{2,1,0:T(8,128)(2,1)}, u32[]{:S(2)}, u32[]{:S(2)}) async-start(bf16[8,8,4096]{2,1,0:T(8,128)(2,1)} %get-tuple-element.24), calls=%async_computation.1 | async-start | bytes 1048576 | tf_op jit(solution)/shard_map/all_to_all | solution.py:338
  27.0 46.2 %collective-permute-start.3 = (bf16[288,4096]{1,0:T(8,128)(2,1)}, bf16[288,4096]{1,0:T(8,128)(2,1)}, u32[]{:S(2)}, u32[]{:S(2)}) collective-permute-start(bf16[288,4096]{1,0:T(8,128)(2,1)} %get-tuple-element.25.slab0), channel_id=1, source_target_pairs={{1,0},{0,1},{3,2},{2,3},{5,4},{4,5},{7,6},{6,7},{9,8},{8,9},{11,10... | collective-permute-start | bytes 7077896 | tf_op jit(solution)/shard_map/ppermute | solution.py:334
  30.2 4.4 %collective-permute-start.2 = (f32[2,128]{1,0:T(2,128)}, f32[2,128]{1,0:T(2,128)S(1)}, u32[]{:S(2)}, u32[]{:S(2)}) collective-permute-start(f32[2,128]{1,0:T(2,128)} %get-tuple-element.22.usage0), channel_id=1, source_target_pairs={{1,0},{0,1},{3,2},{2,3},{5,4},{4,5},{7,6},{6,7},{9,8},{8,9},{11,10... | collective-permute-start | bytes 3080 | tf_op jit(solution)/shard_map/ppermute | solution.py:334
  32.1 54.4 %collective-permute-start.4 = (bf16[288,4096]{1,0:T(8,128)(2,1)}, bf16[288,4096]{1,0:T(8,128)(2,1)S(1)}, u32[]{:S(2)}, u32[]{:S(2)}) collective-permute-start(bf16[288,4096]{1,0:T(8,128)(2,1)} %get-tuple-element.25.slab0), channel_id=1, source_target_pairs={{2,0},{0,2},{3,1},{1,3},{6,4},{4,6},{7,5},{5,7},{10,8},{8,10},{11,... | collective-permute-start | bytes 7077896 | tf_op jit(solution)/shard_map/ppermute | solution.py:334
  34.5 0.8 copy-start.2
  35.3 0.8 copy-start.3
  36.2 37.1 %copy-start = (f32[2,128]{1,0:T(2,128)S(1)}, f32[2,128]{1,0:T(2,128)}, u32[]{:S(2)}) copy-start(f32[2,128]{1,0:T(2,128)} %get-tuple-element.22.usage0) | copy-start | bytes 3076
  86.5 7.8 %collective-permute-start.5 = (bf16[288,4096]{1,0:T(8,128)(2,1)S(1)}, bf16[288,4096]{1,0:T(8,128)(2,1)S(1)}, u32[]{:S(2)}, u32[]{:S(2)}) collective-permute-start(bf16[288,4096]{1,0:T(8,128)(2,1)S(1)} %collective-permute-done.4.slab), channel_id=1, source_target_pairs={{1,0},{0,1},{3,2},{2,3},{5,4},{4,5},{7,6},{6,7},{9,8},{8,9},{11,10... | collective-permute-start | bytes 7077896 | tf_op jit(solution)/shard_map/ppermute | solution.py:334
  89.8 4.5 %collective-permute-start.6 = (f32[2,128]{1,0:T(2,128)}, f32[2,128]{1,0:T(2,128)S(1)}, u32[]{:S(2)}, u32[]{:S(2)}) collective-permute-start(f32[2,128]{1,0:T(2,128)} %get-tuple-element.32.usage0), channel_id=1, source_target_pairs={{2,0},{0,2},{3,1},{1,3},{6,4},{4,6},{7,5},{5,7},{10,8},{8,10},{11,... | collective-permute-start | bytes 3080 | tf_op jit(solution)/shard_map/ppermute | solution.py:334
  92.0 2.3 %copy-start.1 = (f32[2,128]{1,0:T(2,128)S(1)}, f32[2,128]{1,0:T(2,128)}, u32[]{:S(2)}) copy-start(f32[2,128]{1,0:T(2,128)} %get-tuple-element.32.usage0) | copy-start | bytes 3076
